TPU v7x, 256 devices: a whole 4x4x8 slice. The times are simulated.
256 devices in a mesh: wide: 32 (over z_lo, x, core), narrow: 8 (over z_hi, y).
Axes of the slice: x: 4, y: 4, z: 8 (z_hi: 2, z_lo: 4; z = z_hi * 4 + z_lo), core: 2. Of those that a mesh axis runs over, the one named last changes fastest.
Arguments:
- krylov: float32 [2, 134217728], P(None, ('wide', 'narrow')), may hold values from -6 to 6
- fitness_class: int32 [4194304], P(('wide', 'narrow')), may hold values from 0 to 7
- rate_index: int32 [2], replicated, may hold values from 4 to 15
Outputs:
- images: float32 [2, 134217728], P(None, ('wide', 'narrow'))
All inputs are finite; a program needn't handle non-finite values.
Results may differ from a plain program's by a relative error of at most 0.00014.
Values sent between devices are 32-bit elements; how exact they have to be, the bound alone decides.
No kernel may reach another device: no remote copies, remote signals or barrier semaphores. Data moves between devices by JAX's collectives and lax.ppermute only.
A program may use at most 128 MiB of HBM per device.

v0:
```python
import jax
import jax.numpy as jnp
import numpy as np
from jax import lax
from jax.experimental import pallas as pl
from jax.experimental.pallas import tpu as pltpu
from jax.sharding import PartitionSpec as P


AXES = ("wide", "narrow")
SITES = 27
RING = 8
PLANE = 32
REST = 16
PROFILE = [float(1.0 + 0.5 * np.cos(2.0 * site)) for site in range(SITES)]
RING_HERE = [16, 17, 18]
PLANE_HERE = [11, 12, 13, 14, 15]
RING_AWAY = [25, 26, 21]
PLANE_AWAY = [19, 20, 22, 23, 24]
F32 = jnp.float32
BF16 = jnp.bfloat16


def device_at(ring, plane):
    x, core, y = plane // 8, plane // 4 % 2, plane % 4
    return ((ring % 4 * 4 + x) * 2 + core) * 8 + ring // 4 * 4 + y


def ring_pairs(shift):
    return [
        (device_at(ring, plane), device_at((ring + shift) % RING, plane))
        for ring in range(RING)
        for plane in range(PLANE)
    ]


PLANE_GROUPS = [[device_at(ring, plane) for plane in range(PLANE)] for ring in range(RING)]


def chances(rate_ref, vector):
    level = 0.004 * (rate_ref[vector].astype(F32) + 1.0)
    return [level * PROFILE[site] for site in range(SITES)]


def pick(chance, sites):
    return [chance[site] for site in sites]


def mix_bits(tiles, chance_of_bit):
    tiles = list(tiles)
    for bit, chance in enumerate(chance_of_bit):
        step = 1 << bit
        for low in range(len(tiles)):
            if low & step:
                continue
            flow = chance * (tiles[low | step] - tiles[low])
            tiles[low] = tiles[low] + flow
            tiles[low | step] = tiles[low | step] - flow
    return tiles


def lane_matrix(chance):
    row = lax.broadcasted_iota(jnp.int32, (128, 128), 0)
    column = lax.broadcasted_iota(jnp.int32, (128, 128), 1)
    differ = row ^ column
    product = jnp.ones((128, 128), F32)
    for site in range(7):
        product = product * jnp.where((differ >> site) & 1 == 0, 1.0 - chance[site], chance[site])
    high = product.astype(BF16)
    low = (product - high.astype(F32)).astype(BF16)
    top = jnp.concatenate([high, low], axis=1)
    bottom = jnp.concatenate([high, jnp.zeros_like(low)], axis=1)
    return jnp.concatenate([top, bottom], axis=0)


def mix_lanes(tiles, matrix):
    rows = jnp.concatenate(tiles, axis=0)
    high = rows.astype(BF16)
    low = (rows - high.astype(F32)).astype(BF16)
    both = jnp.dot(jnp.concatenate([high, low], axis=1), matrix, preferred_element_type=F32)
    mixed = both[:, :128] + both[:, 128:]
    return [mixed[8 * at : 8 * at + 8] for at in range(len(tiles))]


def mix_sublanes(tiles, chance):
    sub = lax.broadcasted_iota(jnp.int32, (8, 128), 0)
    mixed = []
    for tile in tiles:
        for bit in range(3):
            step = 1 << bit
            if step == 4:
                partner = pltpu.roll(tile, 4, 0)
            else:
                partner = jnp.where(
                    sub & step == 0, pltpu.roll(tile, 8 - step, 0), pltpu.roll(tile, step, 0)
                )
            tile = tile + chance[bit] * (partner - tile)
        mixed.append(tile)
    return mixed


def mix_rest(tiles, chance, matrix):
    tiles = mix_sublanes(mix_lanes(tiles, matrix), chance[7:10])
    paired = []
    for at in range(0, len(tiles), 2):
        paired += mix_bits(tiles[at : at + 2], chance[10:11])
    return paired


def spread(row, pattern):
    sub = lax.broadcasted_iota(jnp.int32, (8, 128), 0)
    lane = lax.broadcasted_iota(jnp.int32, (8, 128), 1)
    index = 4 * (8 * pattern + sub) + (lane >> 5)
    return jnp.take_along_axis(
        jnp.broadcast_to(row, (8, 128)), index, axis=1, mode="promise_in_bounds"
    )


def half_rows(half):
    return pl.ds(pl.multiple_of(8 * half, 8), 8)


def mix_ring(held, chance):
    @pl.loop(0, 2 * PLANE, unroll=4)
    def _(at):
        plane, rows = at // 2, half_rows(at % 2)
        mixed = mix_bits([held[ring, plane, rows, :] for ring in range(RING)], chance)
        for ring in range(RING):
            held[ring, plane, rows, :] = mixed[ring]


def mix_plane(held, ring, chance):
    for half in range(2):
        rows = pl.ds(8 * half, 8)
        mixed = mix_bits([held[ring, plane, rows, :] for plane in range(PLANE)], chance)
        for plane in range(PLANE):
            held[ring, plane, rows, :] = mixed[plane]


def my_ring():
    return lax.axis_index("narrow") // 4 * 4 + lax.axis_index("wide") // 8


def ring_slot(shift):
    return lax.rem(my_ring() + shift + RING, RING)


def from_ring(refs, held, sems):
    def copies():
        return [
            pltpu.make_async_copy(ref, held.at[ring_slot(-shift)], sems.at[shift])
            for shift, ref in enumerate(refs)
        ]

    return copies


def to_ring(held, refs, sems):
    def copies():
        return [
            pltpu.make_async_copy(held.at[ring_slot(shift)], ref, sems.at[shift])
            for shift, ref in enumerate(refs)
        ]

    return copies


def plane_copy(ref, held, ring, sems, outward=False):
    rows = pl.ds(pl.multiple_of(REST * ring, REST), REST)
    here, there = held.at[ring], ref.at[:, rows, :]
    if outward:
        return pltpu.make_async_copy(here, there, sems.at[ring])
    return pltpu.make_async_copy(there, here, sems.at[ring])


def start_all(copies):
    for copy in copies:
        copy.start()


def wait_all(copies):
    for copy in copies:
        copy.wait()


def begin_ring(rate_ref, class_ref, x_ref, *refs):
    outs, (x_held, class_held, held, in_sems, out_sems, class_sem) = refs[:RING], refs[RING:]
    chance = chances(rate_ref, 0)

    def load(part):
        rows = pl.ds(pl.multiple_of(128 * part, 128), 128)
        return pltpu.make_async_copy(
            x_ref.at[:, rows, :], x_held.at[:, rows, :], in_sems.at[part]
        )

    classes = pltpu.make_async_copy(class_ref, class_held, class_sem)
    classes.start()
    for part in range(RING):
        load(part).start()
    classes.wait()
    for ring in range(RING):
        held[ring, PLANE] = 0.5 + 0.25 * class_held[REST * ring : REST * ring + REST].astype(F32)

    @pl.loop(0, RING)
    def _(part):
        load(part).wait()
        for at in range(8):
            plane, rows = 4 * part + at // 2, pl.ds(8 * (at % 2), 8)
            tiles = []
            for ring in range(RING):
                scale = spread(held[ring, PLANE, pl.ds(2 * part + at // 4, 1), :], at % 4)
                start = pl.multiple_of(128 * part + 16 * at, 16)
                tiles.append(x_held[ring, pl.ds(start, 8, stride=2), :] * scale)
            for ring, tile in enumerate(mix_bits(tiles, pick(chance, RING_HERE))):
                held[ring, plane, rows, :] = tile

    copies = to_ring(held, outs, out_sems)()
    start_all(copies)
    wait_all(copies)


def begin_plane(rate_ref, class_ref, x_ref, out_ref, x_held, class_held, held, in_sems, out_sems, class_sem):
    chance = chances(rate_ref, 1)

    def load(ring):
        return pltpu.make_async_copy(x_ref.at[ring], x_held.at[ring], in_sems.at[ring])

    classes = pltpu.make_async_copy(class_ref, class_held, class_sem)
    classes.start()
    for ring in range(RING):
        load(ring).start()
    classes.wait()

    @pl.loop(0, RING)
    def _(ring):
        load(ring).wait()
        first_row = pl.multiple_of(REST * ring, REST)
        fitness = 0.5 + 0.25 * class_held[pl.ds(first_row, REST), :].astype(F32)
        for half in range(2):
            tiles = []
            for plane in range(PLANE):
                scale = spread(fitness[plane // 2 : plane // 2 + 1], plane % 2 * 2 + half)
                tiles.append(x_held[ring, pl.ds(32 * plane + 16 * half + 1, 8, stride=2), :] * scale)
            for plane, tile in enumerate(mix_bits(tiles, pick(chance, PLANE_HERE))):
                held[ring, plane, pl.ds(8 * half, 8), :] = tile
        plane_copy(out_ref, held, ring, out_sems, outward=True).start()

    wait_all([plane_copy(out_ref, held, ring, out_sems, outward=True) for ring in range(RING)])


def ring_to_plane_first(rate_ref, *refs):
    parts, out_ref, (held, rows_held, in_sems, out_sems, row_sem) = refs[:RING], refs[RING], refs[RING + 1 :]
    chance = chances(rate_ref, 0)
    copies = from_ring(parts, held, in_sems)()
    start_all(copies)
    wait_all(copies)
    for ring in range(RING):
        straight = held[ring, PLANE]
        turned = pltpu.roll(straight, 64, 1)
        for pair in range(REST):
            rows_held[2 * pair, ring : ring + 1, :] = straight[pair : pair + 1]
            rows_held[2 * pair + 1, ring : ring + 1, :] = turned[pair : pair + 1]
    rows_copy = pltpu.make_async_copy(rows_held, out_ref.at[:, pl.ds(RING * REST, RING), :], row_sem)
    rows_copy.start()
    mix_ring(held, pick(chance, RING_AWAY))

    def send(ring):
        return plane_copy(out_ref, held.at[:, pl.ds(0, PLANE)], ring, out_sems, outward=True)

    @pl.loop(0, RING)
    def _(ring):
        mix_plane(held, ring, pick(chance, PLANE_HERE))
        send(ring).start()

    wait_all([send(ring) for ring in range(RING)])
    rows_copy.wait()


def apply_middle(held, rows_held, ring, chance, matrix):
    @pl.loop(0, 4)
    def _(eighth):
        places = [(8 * eighth + at // 2, pl.ds(8 * (at % 2), 8)) for at in range(16)]
        tiles = [held[ring, plane, rows, :] for plane, rows in places]
        tiles = mix_rest(tiles, chance, matrix)
        for at, (plane, _) in enumerate(places):
            tiles[at] = tiles[at] * spread(rows_held[plane, pl.ds(ring, 1), :], at % 2)
        tiles = mix_rest(tiles, chance, matrix)
        for (plane, rows), tile in zip(places, tiles):
            held[ring, plane, rows, :] = tile


def middle_ring(rate_ref, x_ref, *refs):
    outs, (held, rows_held, in_sems, out_sems, row_sem) = refs[:RING], refs[RING:]
    chance = chances(rate_ref, 0)
    rows_copy = pltpu.make_async_copy(x_ref.at[:, pl.ds(RING * REST, RING), :], rows_held, row_sem)
    rows_copy.start()
    start_all([plane_copy(x_ref, held, ring, in_sems) for ring in range(RING)])
    matrix = lane_matrix(chance)
    rows_copy.wait()

    @pl.loop(0, RING)
    def _(ring):
        plane_copy(x_ref, held, ring, in_sems).wait()
        mix_plane(held, ring, pick(chance, PLANE_AWAY))
        apply_middle(held, rows_held, ring, chance, matrix)
        mix_plane(held, ring, pick(chance, PLANE_AWAY))

    mix_ring(held, pick(chance, RING_AWAY))
    copies = to_ring(held, outs, out_sems)()
    start_all(copies)
    wait_all(copies)


def ring_to_plane(rate_ref, *refs):
    parts, out_ref, (held, in_sems, out_sems) = refs[:RING], refs[RING], refs[RING + 1 :]
    chance = chances(rate_ref, 0)
    copies = from_ring(parts, held, in_sems)()
    start_all(copies)
    wait_all(copies)
    mix_ring(held, pick(chance, RING_HERE))
    copies = [plane_copy(out_ref, held, ring, out_sems, outward=True) for ring in range(RING)]
    start_all(copies)
    wait_all(copies)


def end_plane(rate_ref, x_ref, out_ref, held, in_sems, out_sems):
    chance = chances(rate_ref, 0)
    start_all([plane_copy(x_ref, held, ring, in_sems) for ring in range(RING)])

    def send(ring):
        return pltpu.make_async_copy(held.at[ring], out_ref.at[ring], out_sems.at[ring])

    @pl.loop(0, RING)
    def _(ring):
        plane_copy(x_ref, held, ring, in_sems).wait()
        mix_plane(held, ring, pick(chance, PLANE_HERE))
        send(ring).start()

    wait_all([send(ring) for ring in range(RING)])


def plane_to_ring(plane_sites, ring_sites):
    def kernel(rate_ref, x_ref, *refs):
        outs, (held, in_sems, out_sems) = refs[:RING], refs[RING:]
        chance = chances(rate_ref, 1)
        start_all([plane_copy(x_ref, held, ring, in_sems) for ring in range(RING)])

        @pl.loop(0, RING)
        def _(ring):
            plane_copy(x_ref, held, ring, in_sems).wait()
            mix_plane(held, ring, pick(chance, plane_sites))

        if ring_sites:
            mix_ring(held, pick(chance, ring_sites))
        copies = to_ring(held, outs, out_sems)()
        start_all(copies)
        wait_all(copies)

    return kernel


def middle_plane(rate_ref, fitness_ref, *refs):
    parts, out_ref, (held, rows_held, in_sems, out_sems, row_sem) = refs[:RING], refs[RING], refs[RING + 1 :]
    chance = chances(rate_ref, 1)
    rows_copy = pltpu.make_async_copy(fitness_ref.at[:, pl.ds(RING * REST, RING), :], rows_held, row_sem)
    rows_copy.start()
    copies = from_ring(parts, held, in_sems)()
    start_all(copies)
    matrix = lane_matrix(chance)
    rows_copy.wait()
    wait_all(copies)
    mix_ring(held, pick(chance, RING_AWAY))

    @pl.loop(0, RING)
    def _(ring):
        apply_middle(held, rows_held, ring, chance, matrix)
        mix_plane(held, ring, pick(chance, PLANE_AWAY))

    mix_ring(held, pick(chance, RING_AWAY))
    copies = [plane_copy(out_ref, held, ring, out_sems, outward=True) for ring in range(RING)]
    start_all(copies)
    wait_all(copies)


def end_ring(rate_ref, other_ref, *refs):
    parts, out_ref, (held, other_held, out_held, in_sems, other_sems, out_sems) = refs[:RING], refs[RING], refs[RING + 1 :]
    chance = chances(rate_ref, 1)
    other_copies = [
        pltpu.make_async_copy(other_ref.at[ring], other_held.at[ring], other_sems.at[ring])
        for ring in range(RING)
    ]
    copies = from_ring(parts, held, in_sems)()
    start_all(copies + other_copies)
    wait_all(copies + other_copies)

    def send(part):
        rows = pl.ds(pl.multiple_of(128 * part, 128), 128)
        return pltpu.make_async_copy(
            out_held.at[:, rows, :], out_ref.at[:, rows, :], out_sems.at[part]
        )

    @pl.loop(0, RING)
    def _(part):
        for at in range(8):
            plane, rows = 4 * part + at // 2, pl.ds(8 * (at % 2), 8)
            start = pl.multiple_of(128 * part + 16 * at, 16)
            tiles = [held[ring, plane, rows, :] for ring in range(RING)]
            for ring, tile in enumerate(mix_bits(tiles, pick(chance, RING_HERE))):
                out_held[ring, pl.ds(start, 8, stride=2), :] = other_held[ring, plane, rows, :]
                out_held[ring, pl.ds(start + 1, 8, stride=2), :] = tile
        send(part).start()

    wait_all([send(part) for part in range(RING)])


SMEM = pl.BlockSpec(memory_space=pltpu.SMEM)
ANY = pl.BlockSpec(memory_space=pl.ANY)
HELD = pltpu.VMEM((RING, PLANE, REST, 128), F32)
HELD_MORE = pltpu.VMEM((RING, PLANE + 1, REST, 128), F32)
WHOLE = pltpu.VMEM((RING, 1024, 128), F32)
CLASSES = pltpu.VMEM((128, 128), jnp.int32)
ROWS = pltpu.VMEM((PLANE, RING, 128), F32)
EIGHT = pltpu.SemaphoreType.DMA((RING,))
ONE = pltpu.SemaphoreType.DMA
SENT_RING = [jax.ShapeDtypeStruct((PLANE, REST, 128), F32)] * RING
SENT_RING_MORE = [jax.ShapeDtypeStruct((PLANE + 1, REST, 128), F32)] * RING
SENT_PLANE = jax.ShapeDtypeStruct((PLANE, RING * REST, 128), F32)
SENT_PLANE_MORE = jax.ShapeDtypeStruct((PLANE, RING * REST + RING, 128), F32)


def call(kernel, name, outs, scratch, rate_index, *operands):
    many = isinstance(outs, list)
    return pl.pallas_call(
        kernel,
        out_shape=outs,
        in_specs=[SMEM] + [ANY] * len(operands),
        out_specs=[ANY] * len(outs) if many else ANY,
        scratch_shapes=scratch,
        cost_estimate=pl.CostEstimate(
            flops=1 << 28, bytes_accessed=8 << 20, transcendentals=0
        ),
        compiler_params=pltpu.CompilerParams(vmem_limit_bytes=(56 if name in ("a1", "b1") else 16) << 20),
    )(rate_index, *operands)


def round_ring(parts):
    return [parts[0]] + [
        lax.ppermute(part, AXES, ring_pairs(shift))
        for shift, part in enumerate(parts)
        if shift
    ]


def in_plane(piece):
    return lax.all_to_all(
        piece, AXES, split_axis=0, concat_axis=0, tiled=True, axis_index_groups=PLANE_GROUPS
    )


def per_device(krylov, fitness_class, rate_index):
    rows = krylov.reshape(2, 4096, 128).transpose(1, 0, 2).reshape(RING, 1024, 128)
    classes = fitness_class.reshape(128, 128)
    rate = rate_index
    begin = [WHOLE, CLASSES]
    ends = [EIGHT, EIGHT]

    a = call(begin_ring, "a1", SENT_RING_MORE, begin + [HELD_MORE] + ends + [ONE], rate, classes, rows)
    a = round_ring(a)
    b = call(begin_plane, "b1", SENT_PLANE, begin + [HELD] + ends + [ONE], rate, classes, rows)
    b = in_plane(b)
    b = call(plane_to_ring(PLANE_AWAY, RING_HERE), "b2", SENT_RING, [HELD] + ends, rate, b)
    b = round_ring(b)
    a = call(ring_to_plane_first, "a2", SENT_PLANE_MORE, [HELD_MORE, ROWS] + ends + [ONE], rate, *a)
    a = in_plane(a)
    fitness = a
    a = call(middle_ring, "a3", SENT_RING, [HELD, ROWS] + ends + [ONE], rate, a)
    a = round_ring(a)
    b = call(middle_plane, "b3", SENT_PLANE, [HELD, ROWS] + ends + [ONE], rate, fitness, *b)
    b = in_plane(b)
    b = call(plane_to_ring(PLANE_HERE, []), "b4", SENT_RING, [HELD] + ends, rate, b)
    b = round_ring(b)
    a = call(ring_to_plane, "a4", SENT_PLANE, [HELD] + ends, rate, *a)
    a = in_plane(a)
    done = jax.ShapeDtypeStruct((RING, PLANE, REST, 128), F32)
    a = call(end_plane, "a5", done, [HELD] + ends, rate, a)
    whole = jax.ShapeDtypeStruct((RING, 1024, 128), F32)
    result = call(end_ring, "b5", whole, [HELD, HELD, WHOLE, EIGHT] + ends, rate, a, *b)
    return result.reshape(4096, 2, 128).transpose(1, 0, 2).reshape(2, 4096 * 128)


def solution(mesh):
    in_specs = (P(None, AXES), P(AXES), P())
    out_specs = P(None, AXES)
    return jax.shard_map(per_device, mesh=mesh, in_specs=in_specs, out_specs=out_specs, check_vma=False)
```

profile of v0, /device:TPU:1, one launch (start us, length us, event | category | flops | bytes accessed | tf_op | source)
XLA Modules:
  0.0 328.2 jit_solution(15754765868588894168)
XLA Ops:
  0.0 5.1 %shard_map.42 = f32[32,128,128]{2,1,0:T(8,128)} custom-call(s32[2]{0:T(128)} %rate_ref.19, s32[128,128]{1,0:T(8,128)} %bitcast.13, f32[8,1024,128]{2,1,0:T(8,128)} %bitcast.11), custom_call_target="tpu_custom_call" | custom-call | flops 268435456 | bytes 8388608 | tf_op jit(solution)/shard_map/pallas_call | solution.py:433
  5.2 8.6 %all-to-all-start.2 = ((f32[32,128,128]{2,1,0:T(8,128)}), f32[32,128,128]{2,1,0:T(8,128)S(1)}, u32[]{:S(2)}, u32[]{:S(2)}) async-start(f32[32,128,128]{2,1,0:T(8,128)} %shard_map.42), calls=%async_computation.2 | async-start | bytes 4194304 | tf_op jit(solution)/shard_map/all_to_all | solution.py:455
  13.8 9.9 %shard_map.37 = (f32[33,16,128]{2,1,0:T(8,128)}, f32[33,16,128]{2,1,0:T(8,128)}, f32[33,16,128]{2,1,0:T(8,128)}, f32[33,16,128]{2,1,0:T(8,128)}, f32[33,16,128]{...) custom-call(s32[2]{0:T(128)} %rate_ref.19, s32[128,128]{1,0:T(8,128)} %bitcast.14, ...), custom_call_target="tpu_custom_call" | custom-call | flops 268435456 | bytes 8388608 | tf_op jit(solution)/shard_map/pallas_call | solution.py:433
  25.4 3.0 collective-permute-start.1
  28.4 3.8 %collective-permute-start.2 = (f32[33,16,128]{2,1,0:T(8,128)}, f32[33,16,128]{2,1,0:T(8,128)S(1)}, u32[]{:S(2)}, u32[]{:S(2)}) collective-permute-start(f32[33,16,128]{2,1,0:T(8,128)} %get-tuple-element.40), channel_id=1, source_target_pairs={{0,192},{1,193},{2,194},{3,195},{8,200},{9,201},{10,202},{11,203},... | collective-permute-start | bytes 811016 | tf_op jit(solution)/shard_map/ppermute | solution.py:448
  32.6 4.5 %collective-permute-start.4 = (f32[33,16,128]{2,1,0:T(8,128)}, f32[33,16,128]{2,1,0:T(8,128)S(1)}, u32[]{:S(2)}, u32[]{:S(2)}) collective-permute-start(f32[33,16,128]{2,1,0:T(8,128)} %get-tuple-element.42), channel_id=1, source_target_pairs={{0,68},{1,69},{2,70},{3,71},{8,76},{9,77},{10,78},{11,79},{16,84},... | collective-permute-start | bytes 811016 | tf_op jit(solution)/shard_map/ppermute | solution.py:448
  37.1 2.4 collective-permute-start.5
  39.5 4.0 %collective-permute-done.1.refs_2_ = f32[33,16,128]{2,1,0:T(8,128)S(1)} collective-permute-done((f32[33,16,128]{2,1,0:T(8,128)}, f32[33,16,128]{2,1,0:T(8,128)S(1)}, u32[]{:S(2)}, u32[]{:S(2)}) %collective-permute-start.1) | collective-permute-done | bytes 270368 | tf_op jit(solution)/shard_map/ppermute | solution.py:448
  43.5 6.9 %collective-permute-start.6 = (f32[33,16,128]{2,1,0:T(8,128)}, f32[33,16,128]{2,1,0:T(8,128)S(1)}, u32[]{:S(2)}, u32[]{:S(2)}) collective-permute-start(f32[33,16,128]{2,1,0:T(8,128)} %get-tuple-element.44), channel_id=1, source_target_pairs={{0,196},{1,197},{2,198},{3,199},{8,204},{9,205},{10,206},{11,207},... | collective-permute-start | bytes 811016 | tf_op jit(solution)/shard_map/ppermute | solution.py:448
  50.4 15.1 %collective-permute-done.2.refs_3_ = f32[33,16,128]{2,1,0:T(8,128)S(1)} collective-permute-done((f32[33,16,128]{2,1,0:T(8,128)}, f32[33,16,128]{2,1,0:T(8,128)S(1)}, u32[]{:S(2)}, u32[]{:S(2)}) %collective-permute-start.2) | collective-permute-done | bytes 270368 | tf_op jit(solution)/shard_map/ppermute | solution.py:448
  65.5 5.1 %collective-permute-done.3.refs_4_ = f32[33,16,128]{2,1,0:T(8,128)S(1)} collective-permute-done((f32[33,16,128]{2,1,0:T(8,128)}, f32[33,16,128]{2,1,0:T(8,128)S(1)}, u32[]{:S(2)}, u32[]{:S(2)}) %collective-permute-start.3) | collective-permute-done | bytes 270368 | tf_op jit(solution)/shard_map/ppermute | solution.py:448
  70.7 7.8 %collective-permute-done.5.refs_6_ = f32[33,16,128]{2,1,0:T(8,128)S(1)} collective-permute-done((f32[33,16,128]{2,1,0:T(8,128)}, f32[33,16,128]{2,1,0:T(8,128)S(1)}, u32[]{:S(2)}, u32[]{:S(2)}) %collective-permute-start.5) | collective-permute-done | bytes 270368 | tf_op jit(solution)/shard_map/ppermute | solution.py:448
  78.5 2.4 collective-permute-done.6.refs_7_
  81.8 3.0 shard_map.38
  87.6 8.5 %all-to-all-start = ((f32[32,136,128]{2,1,0:T(8,128)}), f32[32,136,128]{2,1,0:T(8,128)S(1)}, u32[]{:S(2)}, u32[]{:S(2)}) async-start(f32[32,136,128]{2,1,0:T(8,128)} %copy-done), calls=%async_computation | async-start | bytes 4456448 | tf_op jit(solution)/shard_map/all_to_all | solution.py:455
  97.6 2.9 shard_map.43
  100.5 3.4 %collective-permute-start.14 = (f32[32,16,128]{2,1,0:T(8,128)S(1)}, f32[32,16,128]{2,1,0:T(8,128)S(1)}, u32[]{:S(2)}, u32[]{:S(2)}) collective-permute-start(f32[32,16,128]{2,1,0:T(8,128)S(1)} %get-tuple-element.54), channel_id=1, source_target_pairs={{0,64},{1,65},{2,66},{3,67},{8,72},{9,73},{10,74},{11,75},{16,80},... | collective-permute-start | bytes 786440 | tf_op jit(solution)/shard_map/ppermute | solution.py:448
  105.1 4.5 %collective-permute-start.17 = (f32[32,16,128]{2,1,0:T(8,128)S(1)}, f32[32,16,128]{2,1,0:T(8,128)S(1)}, u32[]{:S(2)}, u32[]{:S(2)}) collective-permute-start(f32[32,16,128]{2,1,0:T(8,128)S(1)} %get-tuple-element.57), channel_id=1, source_target_pairs={{0,4},{1,5},{2,6},{3,7},{8,12},{9,13},{10,14},{11,15},{16,20},{17,... | collective-permute-start | bytes 786440 | tf_op jit(solution)/shard_map/ppermute | solution.py:448
  110.7 2.1 collective-permute-start.19
  112.8 9.5 %collective-permute-done.15.refs_2_ = f32[32,16,128]{2,1,0:T(8,128)S(1)} collective-permute-done((f32[32,16,128]{2,1,0:T(8,128)S(1)}, f32[32,16,128]{2,1,0:T(8,128)S(1)}, u32[]{:S(2)}, u32[]{:S(2)}) %collective-permute-start.15) | collective-permute-done | bytes 262176 | tf_op jit(solution)/shard_map/ppermute | solution.py:448
  122.3 9.8 %collective-permute-done.16.refs_3_ = f32[32,16,128]{2,1,0:T(8,128)S(1)} collective-permute-done((f32[32,16,128]{2,1,0:T(8,128)S(1)}, f32[32,16,128]{2,1,0:T(8,128)S(1)}, u32[]{:S(2)}, u32[]{:S(2)}) %collective-permute-start.16) | collective-permute-done | bytes 262176 | tf_op jit(solution)/shard_map/ppermute | solution.py:448
  132.1 14.0 %collective-permute-done.17.refs_4_ = f32[32,16,128]{2,1,0:T(8,128)S(1)} collective-permute-done((f32[32,16,128]{2,1,0:T(8,128)S(1)}, f32[32,16,128]{2,1,0:T(8,128)S(1)}, u32[]{:S(2)}, u32[]{:S(2)}) %collective-permute-start.17) | collective-permute-done | bytes 262176 | tf_op jit(solution)/shard_map/ppermute | solution.py:448
  146.9 4.0 %collective-permute-done.19.refs_6_ = f32[32,16,128]{2,1,0:T(8,128)S(1)} collective-permute-done((f32[32,16,128]{2,1,0:T(8,128)S(1)}, f32[32,16,128]{2,1,0:T(8,128)S(1)}, u32[]{:S(2)}, u32[]{:S(2)}) %collective-permute-start.19) | collective-permute-done | bytes 262176 | tf_op jit(solution)/shard_map/ppermute | solution.py:448
  151.5 4.8 %collective-permute-done.20.refs_7_ = f32[32,16,128]{2,1,0:T(8,128)S(1)} collective-permute-done((f32[32,16,128]{2,1,0:T(8,128)S(1)}, f32[32,16,128]{2,1,0:T(8,128)S(1)}, u32[]{:S(2)}, u32[]{:S(2)}) %collective-permute-start.20) | collective-permute-done | bytes 262176 | tf_op jit(solution)/shard_map/ppermute | solution.py:448
  160.0 15.6 %shard_map.44 = f32[32,128,128]{2,1,0:T(8,128)S(1)} custom-call(s32[2]{0:T(128)S(1)} %copy-done.11, f32[32,136,128]{2,1,0:T(8,128)S(1)} %all-to-all-done.x_ref.fitness_ref, f32[32,16,128]{2,1,0:T(8,128)S(1)} %get-tuple-element.53.refs_0_, f32[32,16,128]{2,1,0:T(8,128)S(1)} %collective-permute-done.14.refs_1_, ...), custom_call_target="tpu_custom_call" | custom-call | flops 268435456 | bytes 8388608 | tf_op jit(solution)/shard_map/pallas_call | solution.py:433
  176.9 7.7 %all-to-all-start.3 = ((f32[32,128,128]{2,1,0:T(8,128)}), f32[32,128,128]{2,1,0:T(8,128)}, u32[]{:S(2)}, u32[]{:S(2)}) async-start(f32[32,128,128]{2,1,0:T(8,128)} %copy-done.1), calls=%async_computation.3 | async-start | bytes 4194304 | tf_op jit(solution)/shard_map/all_to_all | solution.py:455
  184.6 15.2 %shard_map.39 = (f32[32,16,128]{2,1,0:T(8,128)S(1)}, f32[32,16,128]{2,1,0:T(8,128)S(1)}, f32[32,16,128]{2,1,0:T(8,128)S(1)}, f32[32,16,128]{2,1,0:T(8,128)S(1)},...) custom-call(s32[2]{0:T(128)S(1)} %copy-done.11, ...), custom_call_target="tpu_custom_call" | custom-call | flops 268435456 | bytes 8388608 | tf_op jit(solution)/shard_map/pallas_call | solution.py:433
  201.7 3.3 %collective-permute-start.9 = (f32[32,16,128]{2,1,0:T(8,128)S(1)}, f32[32,16,128]{2,1,0:T(8,128)S(1)}, u32[]{:S(2)}, u32[]{:S(2)}) collective-permute-start(f32[32,16,128]{2,1,0:T(8,128)S(1)} %get-tuple-element.48), channel_id=1, source_target_pairs={{0,192},{1,193},{2,194},{3,195},{8,200},{9,201},{10,202},{11,203},... | collective-permute-start | bytes 786440 | tf_op jit(solution)/shard_map/ppermute | solution.py:448
  205.9 4.1 %collective-permute-start.11 = (f32[32,16,128]{2,1,0:T(8,128)S(1)}, f32[32,16,128]{2,1,0:T(8,128)S(1)}, u32[]{:S(2)}, u32[]{:S(2)}) collective-permute-start(f32[32,16,128]{2,1,0:T(8,128)S(1)} %get-tuple-element.50), channel_id=1, source_target_pairs={{0,68},{1,69},{2,70},{3,71},{8,76},{9,77},{10,78},{11,79},{16,84},... | collective-permute-start | bytes 786440 | tf_op jit(solution)/shard_map/ppermute | solution.py:448
  210.0 2.7 collective-permute-start.12
  212.7 8.8 %collective-permute-done.8.refs_2_ = f32[32,16,128]{2,1,0:T(8,128)S(1)} collective-permute-done((f32[32,16,128]{2,1,0:T(8,128)S(1)}, f32[32,16,128]{2,1,0:T(8,128)S(1)}, u32[]{:S(2)}, u32[]{:S(2)}) %collective-permute-start.8) | collective-permute-done | bytes 262176 | tf_op jit(solution)/shard_map/ppermute | solution.py:448
  221.4 15.0 %collective-permute-done.9.refs_3_ = f32[32,16,128]{2,1,0:T(8,128)S(1)} collective-permute-done((f32[32,16,128]{2,1,0:T(8,128)S(1)}, f32[32,16,128]{2,1,0:T(8,128)S(1)}, u32[]{:S(2)}, u32[]{:S(2)}) %collective-permute-start.9) | collective-permute-done | bytes 262176 | tf_op jit(solution)/shard_map/ppermute | solution.py:448
  236.4 10.1 %collective-permute-done.10.refs_4_ = f32[32,16,128]{2,1,0:T(8,128)S(1)} collective-permute-done((f32[32,16,128]{2,1,0:T(8,128)S(1)}, f32[32,16,128]{2,1,0:T(8,128)S(1)}, u32[]{:S(2)}, u32[]{:S(2)}) %collective-permute-start.10) | collective-permute-done | bytes 262176 | tf_op jit(solution)/shard_map/ppermute | solution.py:448
  246.5 3.7 %collective-permute-done.12.refs_6_ = f32[32,16,128]{2,1,0:T(8,128)S(1)} collective-permute-done((f32[32,16,128]{2,1,0:T(8,128)S(1)}, f32[32,16,128]{2,1,0:T(8,128)S(1)}, u32[]{:S(2)}, u32[]{:S(2)}) %collective-permute-start.12) | collective-permute-done | bytes 262176 | tf_op jit(solution)/shard_map/ppermute | solution.py:448
  250.2 2.2 collective-permute-done.13.refs_7_
  252.5 3.3 shard_map.40
  255.8 8.6 %all-to-all-start.1 = ((f32[32,128,128]{2,1,0:T(8,128)}), f32[32,128,128]{2,1,0:T(8,128)S(1)}, u32[]{:S(2)}, u32[]{:S(2)}) async-start(f32[32,128,128]{2,1,0:T(8,128)} %shard_map.40), calls=%async_computation.1 | async-start | bytes 4194304 | tf_op jit(solution)/shard_map/all_to_all | solution.py:455
  264.3 3.5 %shard_map.45 = (f32[32,16,128]{2,1,0:T(8,128)S(1)}, f32[32,16,128]{2,1,0:T(8,128)S(1)}, f32[32,16,128]{2,1,0:T(8,128)S(1)}, f32[32,16,128]{2,1,0:T(8,128)}, f32...) custom-call(s32[2]{0:T(128)S(1)} %copy-done.11, ...), custom_call_target="tpu_custom_call" | custom-call | flops 268435456 | bytes 8388608 | tf_op jit(solution)/shard_map/pallas_call | solution.py:433
  267.9 3.2 collective-permute-start.21
  272.4 4.4 %collective-permute-start.24 = (f32[32,16,128]{2,1,0:T(8,128)}, f32[32,16,128]{2,1,0:T(8,128)S(1)}, u32[]{:S(2)}, u32[]{:S(2)}) collective-permute-start(f32[32,16,128]{2,1,0:T(8,128)} %get-tuple-element.65), channel_id=1, source_target_pairs={{0,4},{1,5},{2,6},{3,7},{8,12},{9,13},{10,14},{11,15},{16,20},{17,... | collective-permute-start | bytes 786440 | tf_op jit(solution)/shard_map/ppermute | solution.py:448
  278.0 2.1 collective-permute-start.26
  280.1 9.5 %collective-permute-done.22.refs_2_ = f32[32,16,128]{2,1,0:T(8,128)S(1)} collective-permute-done((f32[32,16,128]{2,1,0:T(8,128)S(1)}, f32[32,16,128]{2,1,0:T(8,128)S(1)}, u32[]{:S(2)}, u32[]{:S(2)}) %collective-permute-start.22) | collective-permute-done | bytes 262176 | tf_op jit(solution)/shard_map/ppermute | solution.py:448
  291.4 1.8 shard_map.41.other_ref
  293.2 6.4 %collective-permute-done.23.refs_3_ = f32[32,16,128]{2,1,0:T(8,128)S(1)} collective-permute-done((f32[32,16,128]{2,1,0:T(8,128)}, f32[32,16,128]{2,1,0:T(8,128)S(1)}, u32[]{:S(2)}, u32[]{:S(2)}) %collective-permute-start.23) | collective-permute-done | bytes 262176 | tf_op jit(solution)/shard_map/ppermute | solution.py:448
  299.6 13.8 %collective-permute-done.24.refs_4_ = f32[32,16,128]{2,1,0:T(8,128)S(1)} collective-permute-done((f32[32,16,128]{2,1,0:T(8,128)}, f32[32,16,128]{2,1,0:T(8,128)S(1)}, u32[]{:S(2)}, u32[]{:S(2)}) %collective-permute-start.24) | collective-permute-done | bytes 262176 | tf_op jit(solution)/shard_map/ppermute | solution.py:448
  313.4 5.1 %collective-permute-done.26.refs_6_ = f32[32,16,128]{2,1,0:T(8,128)} collective-permute-done((f32[32,16,128]{2,1,0:T(8,128)}, f32[32,16,128]{2,1,0:T(8,128)}, u32[]{:S(2)}, u32[]{:S(2)}) %collective-permute-start.26) | collective-permute-done | bytes 262176 | tf_op jit(solution)/shard_map/ppermute | solution.py:448
  318.5 5.5 %collective-permute-done.27.refs_7_ = f32[32,16,128]{2,1,0:T(8,128)} collective-permute-done((f32[32,16,128]{2,1,0:T(8,128)}, f32[32,16,128]{2,1,0:T(8,128)}, u32[]{:S(2)}, u32[]{:S(2)}) %collective-permute-start.27) | collective-permute-done | bytes 262176 | tf_op jit(solution)/shard_map/ppermute | solution.py:448
  324.0 4.1 %shard_map.46 = f32[8,1024,128]{2,1,0:T(8,128)} custom-call(s32[2]{0:T(128)S(1)} %copy-done.11, f32[8,32,16,128]{3,2,1,0:T(8,128)S(1)} %shard_map.41.other_ref, f32[32,16,128]{2,1,0:T(8,128)S(1)} %get-tuple-element.61.refs_0_, f32[32,16,128]{2,1,0:T(8,128)S(1)} %collective-permute-done.21.refs_1_, f32[32,16,128]{2,1,0:T(8,128)S(1)} %collective-permute-done.22.refs_2_, ...), custom_call_target="tpu_custom_call" | custom-call | flops 268435456 | bytes 8388608 | tf_op jit(solution)/shard_map/pallas_call | solution.py:433
  (50 shorter events, 23.0 us)
Async XLA Ops:
  5.2 81.1 %all-to-all-start.2 = ((f32[32,128,128]{2,1,0:T(8,128)}), f32[32,128,128]{2,1,0:T(8,128)S(1)}, u32[]{:S(2)}, u32[]{:S(2)}) async-start(f32[32,128,128]{2,1,0:T(8,128)} %shard_map.42), calls=%async_computation.2 | async-start | bytes 4194304 | tf_op jit(solution)/shard_map/all_to_all | solution.py:455
  13.8 67.1 %copy-start.11 = (s32[2]{0:T(128)S(1)}, s32[2]{0:T(128)}, u32[]{:S(2)}) copy-start(s32[2]{0:T(128)} %rate_ref.19) | copy-start | bytes 28
  23.7 13.4 %collective-permute-start = (f32[33,16,128]{2,1,0:T(8,128)}, f32[33,16,128]{2,1,0:T(8,128)S(1)}, u32[]{:S(2)}, u32[]{:S(2)}) collective-permute-start(f32[33,16,128]{2,1,0:T(8,128)} %get-tuple-element.38), channel_id=1, source_target_pairs={{0,64},{1,65},{2,66},{3,67},{8,72},{9,73},{10,74},{11,75},{16,80},... | collective-permute-start | bytes 811016 | tf_op jit(solution)/shard_map/ppermute | solution.py:448
  25.4 18.1 %collective-permute-start.1 = (f32[33,16,128]{2,1,0:T(8,128)}, f32[33,16,128]{2,1,0:T(8,128)S(1)}, u32[]{:S(2)}, u32[]{:S(2)}) collective-permute-start(f32[33,16,128]{2,1,0:T(8,128)} %get-tuple-element.39), channel_id=1, source_target_pairs={{0,128},{1,129},{2,130},{3,131},{8,136},{9,137},{10,138},{11,139},... | collective-permute-start | bytes 811016 | tf_op jit(solution)/shard_map/ppermute | solution.py:448
  28.4 37.1 %collective-permute-start.2 = (f32[33,16,128]{2,1,0:T(8,128)}, f32[33,16,128]{2,1,0:T(8,128)S(1)}, u32[]{:S(2)}, u32[]{:S(2)}) collective-permute-start(f32[33,16,128]{2,1,0:T(8,128)} %get-tuple-element.40), channel_id=1, source_target_pairs={{0,192},{1,193},{2,194},{3,195},{8,200},{9,201},{10,202},{11,203},... | collective-permute-start | bytes 811016 | tf_op jit(solution)/shard_map/ppermute | solution.py:448
  32.2 38.5 %collective-permute-start.3 = (f32[33,16,128]{2,1,0:T(8,128)}, f32[33,16,128]{2,1,0:T(8,128)S(1)}, u32[]{:S(2)}, u32[]{:S(2)}) collective-permute-start(f32[33,16,128]{2,1,0:T(8,128)} %get-tuple-element.41), channel_id=1, source_target_pairs={{0,4},{1,5},{2,6},{3,7},{8,12},{9,13},{10,14},{11,15},{16,20},{17,... | collective-permute-start | bytes 811016 | tf_op jit(solution)/shard_map/ppermute | solution.py:448
  32.6 38.0 %collective-permute-start.4 = (f32[33,16,128]{2,1,0:T(8,128)}, f32[33,16,128]{2,1,0:T(8,128)S(1)}, u32[]{:S(2)}, u32[]{:S(2)}) collective-permute-start(f32[33,16,128]{2,1,0:T(8,128)} %get-tuple-element.42), channel_id=1, source_target_pairs={{0,68},{1,69},{2,70},{3,71},{8,76},{9,77},{10,78},{11,79},{16,84},... | collective-permute-start | bytes 811016 | tf_op jit(solution)/shard_map/ppermute | solution.py:448
  37.1 41.4 %collective-permute-start.5 = (f32[33,16,128]{2,1,0:T(8,128)}, f32[33,16,128]{2,1,0:T(8,128)S(1)}, u32[]{:S(2)}, u32[]{:S(2)}) collective-permute-start(f32[33,16,128]{2,1,0:T(8,128)} %get-tuple-element.43), channel_id=1, source_target_pairs={{0,132},{1,133},{2,134},{3,135},{8,140},{9,141},{10,142},{11,143},... | collective-permute-start | bytes 811016 | tf_op jit(solution)/shard_map/ppermute | solution.py:448
  43.5 37.4 %collective-permute-start.6 = (f32[33,16,128]{2,1,0:T(8,128)}, f32[33,16,128]{2,1,0:T(8,128)S(1)}, u32[]{:S(2)}, u32[]{:S(2)}) collective-permute-start(f32[33,16,128]{2,1,0:T(8,128)} %get-tuple-element.44), channel_id=1, source_target_pairs={{0,196},{1,197},{2,198},{3,199},{8,204},{9,205},{10,206},{11,207},... | collective-permute-start | bytes 811016 | tf_op jit(solution)/shard_map/ppermute | solution.py:448
  80.9 1.0 copy-start.4
  84.9 1.4 copy-start
  86.2 1.3 copy-start.2
  87.6 69.5 %all-to-all-start = ((f32[32,136,128]{2,1,0:T(8,128)}), f32[32,136,128]{2,1,0:T(8,128)S(1)}, u32[]{:S(2)}, u32[]{:S(2)}) async-start(f32[32,136,128]{2,1,0:T(8,128)} %copy-done), calls=%async_computation | async-start | bytes 4456448 | tf_op jit(solution)/shard_map/all_to_all | solution.py:455
  96.0 1.6 copy-start.3
  100.5 10.2 %collective-permute-start.14 = (f32[32,16,128]{2,1,0:T(8,128)S(1)}, f32[32,16,128]{2,1,0:T(8,128)S(1)}, u32[]{:S(2)}, u32[]{:S(2)}) collective-permute-start(f32[32,16,128]{2,1,0:T(8,128)S(1)} %get-tuple-element.54), channel_id=1, source_target_pairs={{0,64},{1,65},{2,66},{3,67},{8,72},{9,73},{10,74},{11,75},{16,80},... | collective-permute-start | bytes 786440 | tf_op jit(solution)/shard_map/ppermute | solution.py:448
  103.9 18.4 %collective-permute-start.15 = (f32[32,16,128]{2,1,0:T(8,128)S(1)}, f32[32,16,128]{2,1,0:T(8,128)S(1)}, u32[]{:S(2)}, u32[]{:S(2)}) collective-permute-start(f32[32,16,128]{2,1,0:T(8,128)S(1)} %get-tuple-element.55), channel_id=1, source_target_pairs={{0,128},{1,129},{2,130},{3,131},{8,136},{9,137},{10,138},{11,139},... | collective-permute-start | bytes 786440 | tf_op jit(solution)/shard_map/ppermute | solution.py:448
  104.7 27.4 %collective-permute-start.16 = (f32[32,16,128]{2,1,0:T(8,128)S(1)}, f32[32,16,128]{2,1,0:T(8,128)S(1)}, u32[]{:S(2)}, u32[]{:S(2)}) collective-permute-start(f32[32,16,128]{2,1,0:T(8,128)S(1)} %get-tuple-element.56), channel_id=1, source_target_pairs={{0,192},{1,193},{2,194},{3,195},{8,200},{9,201},{10,202},{11,203},... | collective-permute-start | bytes 786440 | tf_op jit(solution)/shard_map/ppermute | solution.py:448
  105.1 41.1 %collective-permute-start.17 = (f32[32,16,128]{2,1,0:T(8,128)S(1)}, f32[32,16,128]{2,1,0:T(8,128)S(1)}, u32[]{:S(2)}, u32[]{:S(2)}) collective-permute-start(f32[32,16,128]{2,1,0:T(8,128)S(1)} %get-tuple-element.57), channel_id=1, source_target_pairs={{0,4},{1,5},{2,6},{3,7},{8,12},{9,13},{10,14},{11,15},{16,20},{17,... | collective-permute-start | bytes 786440 | tf_op jit(solution)/shard_map/ppermute | solution.py:448
  109.6 36.6 %collective-permute-start.18 = (f32[32,16,128]{2,1,0:T(8,128)S(1)}, f32[32,16,128]{2,1,0:T(8,128)S(1)}, u32[]{:S(2)}, u32[]{:S(2)}) collective-permute-start(f32[32,16,128]{2,1,0:T(8,128)S(1)} %get-tuple-element.58), channel_id=1, source_target_pairs={{0,68},{1,69},{2,70},{3,71},{8,76},{9,77},{10,78},{11,79},{16,84},... | collective-permute-start | bytes 786440 | tf_op jit(solution)/shard_map/ppermute | solution.py:448
  110.7 40.1 %collective-permute-start.19 = (f32[32,16,128]{2,1,0:T(8,128)S(1)}, f32[32,16,128]{2,1,0:T(8,128)S(1)}, u32[]{:S(2)}, u32[]{:S(2)}) collective-permute-start(f32[32,16,128]{2,1,0:T(8,128)S(1)} %get-tuple-element.59), channel_id=1, source_target_pairs={{0,132},{1,133},{2,134},{3,135},{8,140},{9,141},{10,142},{11,143},... | collective-permute-start | bytes 786440 | tf_op jit(solution)/shard_map/ppermute | solution.py:448
  122.3 34.1 %collective-permute-start.20 = (f32[32,16,128]{2,1,0:T(8,128)S(1)}, f32[32,16,128]{2,1,0:T(8,128)S(1)}, u32[]{:S(2)}, u32[]{:S(2)}) collective-permute-start(f32[32,16,128]{2,1,0:T(8,128)S(1)} %get-tuple-element.60), channel_id=1, source_target_pairs={{0,196},{1,197},{2,198},{3,199},{8,204},{9,205},{10,206},{11,207},... | collective-permute-start | bytes 786440 | tf_op jit(solution)/shard_map/ppermute | solution.py:448
  146.2 0.7 copy-start.5
  150.8 0.7 copy-start.7
  156.4 0.7 copy-start.9
  157.1 1.0 copy-start.6
  158.1 0.9 copy-start.8
  159.0 0.9 copy-start.10
  175.5 1.3 copy-start.1
  176.9 78.9 %all-to-all-start.3 = ((f32[32,128,128]{2,1,0:T(8,128)}), f32[32,128,128]{2,1,0:T(8,128)}, u32[]{:S(2)}, u32[]{:S(2)}) async-start(f32[32,128,128]{2,1,0:T(8,128)} %copy-done.1), calls=%async_computation.3 | async-start | bytes 4194304 | tf_op jit(solution)/shard_map/all_to_all | solution.py:455
  199.8 10.2 %collective-permute-start.7 = (f32[32,16,128]{2,1,0:T(8,128)S(1)}, f32[32,16,128]{2,1,0:T(8,128)S(1)}, u32[]{:S(2)}, u32[]{:S(2)}) collective-permute-start(f32[32,16,128]{2,1,0:T(8,128)S(1)} %get-tuple-element.46), channel_id=1, source_target_pairs={{0,64},{1,65},{2,66},{3,67},{8,72},{9,73},{10,74},{11,75},{16,80},... | collective-permute-start | bytes 786440 | tf_op jit(solution)/shard_map/ppermute | solution.py:448
  200.2 21.2 %collective-permute-start.8 = (f32[32,16,128]{2,1,0:T(8,128)S(1)}, f32[32,16,128]{2,1,0:T(8,128)S(1)}, u32[]{:S(2)}, u32[]{:S(2)}) collective-permute-start(f32[32,16,128]{2,1,0:T(8,128)S(1)} %get-tuple-element.47), channel_id=1, source_target_pairs={{0,128},{1,129},{2,130},{3,131},{8,136},{9,137},{10,138},{11,139},... | collective-permute-start | bytes 786440 | tf_op jit(solution)/shard_map/ppermute | solution.py:448
  201.7 34.8 %collective-permute-start.9 = (f32[32,16,128]{2,1,0:T(8,128)S(1)}, f32[32,16,128]{2,1,0:T(8,128)S(1)}, u32[]{:S(2)}, u32[]{:S(2)}) collective-permute-start(f32[32,16,128]{2,1,0:T(8,128)S(1)} %get-tuple-element.48), channel_id=1, source_target_pairs={{0,192},{1,193},{2,194},{3,195},{8,200},{9,201},{10,202},{11,203},... | collective-permute-start | bytes 786440 | tf_op jit(solution)/shard_map/ppermute | solution.py:448
  205.0 41.5 %collective-permute-start.10 = (f32[32,16,128]{2,1,0:T(8,128)S(1)}, f32[32,16,128]{2,1,0:T(8,128)S(1)}, u32[]{:S(2)}, u32[]{:S(2)}) collective-permute-start(f32[32,16,128]{2,1,0:T(8,128)S(1)} %get-tuple-element.49), channel_id=1, source_target_pairs={{0,4},{1,5},{2,6},{3,7},{8,12},{9,13},{10,14},{11,15},{16,20},{17,... | collective-permute-start | bytes 786440 | tf_op jit(solution)/shard_map/ppermute | solution.py:448
  205.9 40.7 %collective-permute-start.11 = (f32[32,16,128]{2,1,0:T(8,128)S(1)}, f32[32,16,128]{2,1,0:T(8,128)S(1)}, u32[]{:S(2)}, u32[]{:S(2)}) collective-permute-start(f32[32,16,128]{2,1,0:T(8,128)S(1)} %get-tuple-element.50), channel_id=1, source_target_pairs={{0,68},{1,69},{2,70},{3,71},{8,76},{9,77},{10,78},{11,79},{16,84},... | collective-permute-start | bytes 786440 | tf_op jit(solution)/shard_map/ppermute | solution.py:448
  210.0 40.2 %collective-permute-start.12 = (f32[32,16,128]{2,1,0:T(8,128)S(1)}, f32[32,16,128]{2,1,0:T(8,128)S(1)}, u32[]{:S(2)}, u32[]{:S(2)}) collective-permute-start(f32[32,16,128]{2,1,0:T(8,128)S(1)} %get-tuple-element.51), channel_id=1, source_target_pairs={{0,132},{1,133},{2,134},{3,135},{8,140},{9,141},{10,142},{11,143},... | collective-permute-start | bytes 786440 | tf_op jit(solution)/shard_map/ppermute | solution.py:448
  221.4 31.0 %collective-permute-start.13 = (f32[32,16,128]{2,1,0:T(8,128)S(1)}, f32[32,16,128]{2,1,0:T(8,128)S(1)}, u32[]{:S(2)}, u32[]{:S(2)}) collective-permute-start(f32[32,16,128]{2,1,0:T(8,128)S(1)} %get-tuple-element.52), channel_id=1, source_target_pairs={{0,196},{1,197},{2,198},{3,199},{8,204},{9,205},{10,206},{11,207},... | collective-permute-start | bytes 786440 | tf_op jit(solution)/shard_map/ppermute | solution.py:448
  255.8 35.6 %all-to-all-start.1 = ((f32[32,128,128]{2,1,0:T(8,128)}), f32[32,128,128]{2,1,0:T(8,128)S(1)}, u32[]{:S(2)}, u32[]{:S(2)}) async-start(f32[32,128,128]{2,1,0:T(8,128)} %shard_map.40), calls=%async_computation.1 | async-start | bytes 4194304 | tf_op jit(solution)/shard_map/all_to_all | solution.py:455
  267.9 10.2 %collective-permute-start.21 = (f32[32,16,128]{2,1,0:T(8,128)S(1)}, f32[32,16,128]{2,1,0:T(8,128)S(1)}, u32[]{:S(2)}, u32[]{:S(2)}) collective-permute-start(f32[32,16,128]{2,1,0:T(8,128)S(1)} %get-tuple-element.62), channel_id=1, source_target_pairs={{0,64},{1,65},{2,66},{3,67},{8,72},{9,73},{10,74},{11,75},{16,80},... | collective-permute-start | bytes 786440 | tf_op jit(solution)/shard_map/ppermute | solution.py:448
  271.1 18.6 %collective-permute-start.22 = (f32[32,16,128]{2,1,0:T(8,128)S(1)}, f32[32,16,128]{2,1,0:T(8,128)S(1)}, u32[]{:S(2)}, u32[]{:S(2)}) collective-permute-start(f32[32,16,128]{2,1,0:T(8,128)S(1)} %get-tuple-element.63), channel_id=1, source_target_pairs={{0,128},{1,129},{2,130},{3,131},{8,136},{9,137},{10,138},{11,139},... | collective-permute-start | bytes 786440 | tf_op jit(solution)/shard_map/ppermute | solution.py:448
  272.0 27.6 %collective-permute-start.23 = (f32[32,16,128]{2,1,0:T(8,128)}, f32[32,16,128]{2,1,0:T(8,128)S(1)}, u32[]{:S(2)}, u32[]{:S(2)}) collective-permute-start(f32[32,16,128]{2,1,0:T(8,128)} %get-tuple-element.64), channel_id=1, source_target_pairs={{0,192},{1,193},{2,194},{3,195},{8,200},{9,201},{10,202},{11,203},... | collective-permute-start | bytes 786440 | tf_op jit(solution)/shard_map/ppermute | solution.py:448
  272.4 41.0 %collective-permute-start.24 = (f32[32,16,128]{2,1,0:T(8,128)}, f32[32,16,128]{2,1,0:T(8,128)S(1)}, u32[]{:S(2)}, u32[]{:S(2)}) collective-permute-start(f32[32,16,128]{2,1,0:T(8,128)} %get-tuple-element.65), channel_id=1, source_target_pairs={{0,4},{1,5},{2,6},{3,7},{8,12},{9,13},{10,14},{11,15},{16,20},{17,... | collective-permute-start | bytes 786440 | tf_op jit(solution)/shard_map/ppermute | solution.py:448
  276.8 36.6 %collective-permute-start.25 = (f32[32,16,128]{2,1,0:T(8,128)}, f32[32,16,128]{2,1,0:T(8,128)}, u32[]{:S(2)}, u32[]{:S(2)}) collective-permute-start(f32[32,16,128]{2,1,0:T(8,128)} %get-tuple-element.66), channel_id=1, source_target_pairs={{0,68},{1,69},{2,70},{3,71},{8,76},{9,77},{10,78},{11,79},{16,84},... | collective-permute-start | bytes 786440 | tf_op jit(solution)/shard_map/ppermute | solution.py:448
  278.0 40.5 %collective-permute-start.26 = (f32[32,16,128]{2,1,0:T(8,128)}, f32[32,16,128]{2,1,0:T(8,128)}, u32[]{:S(2)}, u32[]{:S(2)}) collective-permute-start(f32[32,16,128]{2,1,0:T(8,128)} %get-tuple-element.67), channel_id=1, source_target_pairs={{0,132},{1,133},{2,134},{3,135},{8,140},{9,141},{10,142},{11,143},... | collective-permute-start | bytes 786440 | tf_op jit(solution)/shard_map/ppermute | solution.py:448
  289.7 34.3 %collective-permute-start.27 = (f32[32,16,128]{2,1,0:T(8,128)}, f32[32,16,128]{2,1,0:T(8,128)}, u32[]{:S(2)}, u32[]{:S(2)}) collective-permute-start(f32[32,16,128]{2,1,0:T(8,128)} %get-tuple-element.68), channel_id=1, source_target_pairs={{0,196},{1,197},{2,198},{3,199},{8,204},{9,205},{10,206},{11,207},... | collective-permute-start | bytes 786440 | tf_op jit(solution)/shard_map/ppermute | solution.py:448
where the time goes:
time: 329 us; the launch traced here: 328 us
  waiting for transfers between devices  159 us (48%)
  starting transfers between devices  93.3 us (28%)
  Pallas kernels  64.5 us (20%)
  local copies, waits for them, and re-layouts  11.5 us (3%)
    ppermute x28, waiting for transfers between devices, round_ring(): lax.ppermute(part, AXES, ring_pairs(shift))  157 us
    pallas_call x10, Pallas kernels, call(): pl.pallas_call(kernel, out_shape=outs, in_specs=[SMEM] + [ANY] * len(oper...  64.5 us
    ppermute x28, starting transfers between devices, round_ring(): lax.ppermute(part, AXES, ring_pairs(shift))  60 us
    all_to_all x4, starting transfers between devices, in_plane(): lax.all_to_all(piece, AXES, split_axis=0, concat_axis=0, tiled=True, axis...  33.3 us
    unnamed x24, local copies, waits for them, and re-layouts  11.5 us
  transfers between devices with their start and end apart: 32, of which 21 were waited for; matrix products, arithmetic and copies ran while one was open for 0% of the time, Pallas kernels for 12%

commit v1 on v0

--- a/solution.py
+++ b/solution.py
@@ -59,52 +59,46 @@
     return tiles
 
 
-def lane_matrix(chance):
-    row = lax.broadcasted_iota(jnp.int32, (128, 128), 0)
-    column = lax.broadcasted_iota(jnp.int32, (128, 128), 1)
+def crossing(size, chance_of_bit):
+    row = lax.broadcasted_iota(jnp.int32, (size, size), 0)
+    column = lax.broadcasted_iota(jnp.int32, (size, size), 1)
     differ = row ^ column
-    product = jnp.ones((128, 128), F32)
-    for site in range(7):
-        product = product * jnp.where((differ >> site) & 1 == 0, 1.0 - chance[site], chance[site])
-    high = product.astype(BF16)
-    low = (product - high.astype(F32)).astype(BF16)
+    product = jnp.ones((size, size), F32)
+    for bit, chance in enumerate(chance_of_bit):
+        product = product * jnp.where((differ >> bit) & 1 == 0, 1.0 - chance, chance)
+    return halves(product)
+
+
+def halves(values):
+    high = values.astype(BF16)
+    return high, (values - high.astype(F32)).astype(BF16)
+
+
+def right_matrix(chance):
+    high, low = crossing(128, chance[:7])
     top = jnp.concatenate([high, low], axis=1)
     bottom = jnp.concatenate([high, jnp.zeros_like(low)], axis=1)
     return jnp.concatenate([top, bottom], axis=0)
 
 
-def mix_lanes(tiles, matrix):
-    rows = jnp.concatenate(tiles, axis=0)
-    high = rows.astype(BF16)
-    low = (rows - high.astype(F32)).astype(BF16)
-    both = jnp.dot(jnp.concatenate([high, low], axis=1), matrix, preferred_element_type=F32)
-    mixed = both[:, :128] + both[:, 128:]
-    return [mixed[8 * at : 8 * at + 8] for at in range(len(tiles))]
-
-
-def mix_sublanes(tiles, chance):
-    sub = lax.broadcasted_iota(jnp.int32, (8, 128), 0)
-    mixed = []
-    for tile in tiles:
-        for bit in range(3):
-            step = 1 << bit
-            if step == 4:
-                partner = pltpu.roll(tile, 4, 0)
-            else:
-                partner = jnp.where(
-                    sub & step == 0, pltpu.roll(tile, 8 - step, 0), pltpu.roll(tile, step, 0)
-                )
-            tile = tile + chance[bit] * (partner - tile)
-        mixed.append(tile)
-    return mixed
-
-
-def mix_rest(tiles, chance, matrix):
-    tiles = mix_sublanes(mix_lanes(tiles, matrix), chance[7:10])
-    paired = []
-    for at in range(0, len(tiles), 2):
-        paired += mix_bits(tiles[at : at + 2], chance[10:11])
-    return paired
+def left_matrix(chance):
+    high, low = crossing(256, pick(chance, [7, 8, 9, 10] + PLANE_AWAY[:4]))
+    return jnp.concatenate([high, high, low], axis=1)
+
+
+def mix_blocks(blocks, left, right, chance):
+    stacks = []
+    for block in blocks:
+        high, low = halves(jnp.concatenate([block[:256], block[256:]], axis=1))
+        stacks.append(jnp.concatenate([high, low, high], axis=0))
+    mixed = [jnp.dot(left, stack, preferred_element_type=F32) for stack in stacks]
+    pairs = []
+    for both in mixed:
+        flow = chance * (both[:, 128:] - both[:, :128])
+        tall = jnp.concatenate([both[:, :128] + flow, both[:, 128:] - flow], axis=0)
+        pairs.append(jnp.concatenate(halves(tall), axis=1))
+    mixed = [jnp.dot(pair, right, preferred_element_type=F32) for pair in pairs]
+    return [both[:, :128] + both[:, 128:] for both in mixed]
 
 
 def spread(row, pattern):
@@ -116,17 +110,14 @@
     )
 
 
-def half_rows(half):
-    return pl.ds(pl.multiple_of(8 * half, 8), 8)
-
-
 def mix_ring(held, chance):
-    @pl.loop(0, 2 * PLANE, unroll=4)
-    def _(at):
-        plane, rows = at // 2, half_rows(at % 2)
-        mixed = mix_bits([held[ring, plane, rows, :] for ring in range(RING)], chance)
-        for ring in range(RING):
-            held[ring, plane, rows, :] = mixed[ring]
+    @pl.loop(0, PLANE, unroll=2)
+    def _(plane):
+        for half in range(2):
+            rows = pl.ds(8 * half, 8)
+            mixed = mix_bits([held[ring, plane, rows, :] for ring in range(RING)], chance)
+            for ring in range(RING):
+                held[ring, plane, rows, :] = mixed[ring]
 
 
 def mix_plane(held, ring, chance):
@@ -184,13 +175,24 @@
 
 
 def begin_ring(rate_ref, class_ref, x_ref, *refs):
-    outs, (x_held, class_held, held, in_sems, out_sems, class_sem) = refs[:RING], refs[RING:]
+    outs, (x_held, class_held, held, rows_held, in_sems, out_sems, class_sem, rows_sems) = refs[:RING], refs[RING:]
     chance = chances(rate_ref, 0)
 
     def load(part):
         rows = pl.ds(pl.multiple_of(128 * part, 128), 128)
         return pltpu.make_async_copy(
             x_ref.at[:, rows, :], x_held.at[:, rows, :], in_sems.at[part]
+        )
+
+    def send(shift, part):
+        planes = pl.ds(4 * part, 4)
+        return pltpu.make_async_copy(
+            held.at[ring_slot(shift), planes], outs[shift].at[planes], out_sems.at[shift, part]
+        )
+
+    def send_rows(shift):
+        return pltpu.make_async_copy(
+            held.at[ring_slot(shift), PLANE], outs[shift].at[PLANE], rows_sems.at[shift]
         )
 
     classes = pltpu.make_async_copy(class_ref, class_held, class_sem)
@@ -199,7 +201,11 @@
         load(part).start()
     classes.wait()
     for ring in range(RING):
-        held[ring, PLANE] = 0.5 + 0.25 * class_held[REST * ring : REST * ring + REST].astype(F32)
+        fitness = 0.5 + 0.25 * class_held[REST * ring : REST * ring + REST].astype(F32)
+        held[ring, PLANE] = fitness
+        for part in range(RING):
+            rows_held[part, ring, 0:2, :] = fitness[2 * part : 2 * part + 2]
+    start_all([send_rows(shift) for shift in range(RING)])
 
     @pl.loop(0, RING)
     def _(part):
@@ -208,15 +214,19 @@
             plane, rows = 4 * part + at // 2, pl.ds(8 * (at % 2), 8)
             tiles = []
             for ring in range(RING):
-                scale = spread(held[ring, PLANE, pl.ds(2 * part + at // 4, 1), :], at % 4)
-                start = pl.multiple_of(128 * part + 16 * at, 16)
+                row = at // 4
+                scale = spread(rows_held[part, ring, row : row + 1, :], at % 4)
+                start = pl.multiple_of(128 * part, 128) + 16 * at
                 tiles.append(x_held[ring, pl.ds(start, 8, stride=2), :] * scale)
             for ring, tile in enumerate(mix_bits(tiles, pick(chance, RING_HERE))):
                 held[ring, plane, rows, :] = tile
-
-    copies = to_ring(held, outs, out_sems)()
-    start_all(copies)
-    wait_all(copies)
+        start_all([send(shift, part) for shift in range(RING)])
+
+    @pl.loop(0, RING)
+    def _(part):
+        wait_all([send(shift, part) for shift in range(RING)])
+
+    wait_all([send_rows(shift) for shift in range(RING)])
 
 
 def begin_plane(rate_ref, class_ref, x_ref, out_ref, x_held, class_held, held, in_sems, out_sems, class_sem):
@@ -276,34 +286,41 @@
     rows_copy.wait()
 
 
-def apply_middle(held, rows_held, ring, chance, matrix):
-    @pl.loop(0, 4)
-    def _(eighth):
-        places = [(8 * eighth + at // 2, pl.ds(8 * (at % 2), 8)) for at in range(16)]
-        tiles = [held[ring, plane, rows, :] for plane, rows in places]
-        tiles = mix_rest(tiles, chance, matrix)
-        for at, (plane, _) in enumerate(places):
-            tiles[at] = tiles[at] * spread(rows_held[plane, pl.ds(ring, 1), :], at % 2)
-        tiles = mix_rest(tiles, chance, matrix)
-        for (plane, rows), tile in zip(places, tiles):
-            held[ring, plane, rows, :] = tile
+TOGETHER = 2
+
+
+def apply_middle(held, rows_held, first_ring, chance, left_ref, right_ref):
+    left, right, across = left_ref[...], right_ref[...], chance[PLANE_AWAY[4]]
+    rings = [first_ring + at for at in range(TOGETHER)]
+    blocks = [held[ring].reshape(PLANE * REST, 128) for ring in rings]
+    blocks = mix_blocks(blocks, left, right, across)
+    scaled = []
+    for ring, block in zip(rings, blocks):
+        tiles = []
+        for at in range(2 * PLANE):
+            scale = spread(rows_held[at // 2, pl.ds(ring, 1), :], at % 2)
+            tiles.append(block[8 * at : 8 * at + 8] * scale)
+        scaled.append(jnp.concatenate(tiles, axis=0))
+    blocks = mix_blocks(scaled, left, right, across)
+    for ring, block in zip(rings, blocks):
+        held[ring] = block.reshape(PLANE, REST, 128)
 
 
 def middle_ring(rate_ref, x_ref, *refs):
-    outs, (held, rows_held, in_sems, out_sems, row_sem) = refs[:RING], refs[RING:]
+    outs, (held, rows_held, left, right, in_sems, out_sems, row_sem) = refs[:RING], refs[RING:]
     chance = chances(rate_ref, 0)
     rows_copy = pltpu.make_async_copy(x_ref.at[:, pl.ds(RING * REST, RING), :], rows_held, row_sem)
     rows_copy.start()
     start_all([plane_copy(x_ref, held, ring, in_sems) for ring in range(RING)])
-    matrix = lane_matrix(chance)
+    left[...] = left_matrix(chance)
+    right[...] = right_matrix(chance)
     rows_copy.wait()
 
-    @pl.loop(0, RING)
+    @pl.loop(0, RING, step=TOGETHER)
     def _(ring):
-        plane_copy(x_ref, held, ring, in_sems).wait()
-        mix_plane(held, ring, pick(chance, PLANE_AWAY))
-        apply_middle(held, rows_held, ring, chance, matrix)
-        mix_plane(held, ring, pick(chance, PLANE_AWAY))
+        for at in range(TOGETHER):
+            plane_copy(x_ref, held, ring + at, in_sems).wait()
+        apply_middle(held, rows_held, ring, chance, left, right)
 
     mix_ring(held, pick(chance, RING_AWAY))
     copies = to_ring(held, outs, out_sems)()
@@ -345,11 +362,15 @@
         chance = chances(rate_ref, 1)
         start_all([plane_copy(x_ref, held, ring, in_sems) for ring in range(RING)])
 
-        @pl.loop(0, RING)
-        def _(ring):
-            plane_copy(x_ref, held, ring, in_sems).wait()
-            mix_plane(held, ring, pick(chance, plane_sites))
-
+        if plane_sites:
+
+            @pl.loop(0, RING)
+            def _(ring):
+                plane_copy(x_ref, held, ring, in_sems).wait()
+                mix_plane(held, ring, pick(chance, plane_sites))
+
+        else:
+            wait_all([plane_copy(x_ref, held, ring, in_sems) for ring in range(RING)])
         if ring_sites:
             mix_ring(held, pick(chance, ring_sites))
         copies = to_ring(held, outs, out_sems)()
@@ -360,21 +381,21 @@
 
 
 def middle_plane(rate_ref, fitness_ref, *refs):
-    parts, out_ref, (held, rows_held, in_sems, out_sems, row_sem) = refs[:RING], refs[RING], refs[RING + 1 :]
+    parts, out_ref, (held, rows_held, left, right, in_sems, out_sems, row_sem) = refs[:RING], refs[RING], refs[RING + 1 :]
     chance = chances(rate_ref, 1)
     rows_copy = pltpu.make_async_copy(fitness_ref.at[:, pl.ds(RING * REST, RING), :], rows_held, row_sem)
     rows_copy.start()
     copies = from_ring(parts, held, in_sems)()
     start_all(copies)
-    matrix = lane_matrix(chance)
+    left[...] = left_matrix(chance)
+    right[...] = right_matrix(chance)
     rows_copy.wait()
     wait_all(copies)
     mix_ring(held, pick(chance, RING_AWAY))
 
-    @pl.loop(0, RING)
+    @pl.loop(0, RING, step=TOGETHER)
     def _(ring):
-        apply_middle(held, rows_held, ring, chance, matrix)
-        mix_plane(held, ring, pick(chance, PLANE_AWAY))
+        apply_middle(held, rows_held, ring, chance, left, right)
 
     mix_ring(held, pick(chance, RING_AWAY))
     copies = [plane_copy(out_ref, held, ring, out_sems, outward=True) for ring in range(RING)]
@@ -420,6 +441,10 @@
 WHOLE = pltpu.VMEM((RING, 1024, 128), F32)
 CLASSES = pltpu.VMEM((128, 128), jnp.int32)
 ROWS = pltpu.VMEM((PLANE, RING, 128), F32)
+CLASS_ROWS = pltpu.VMEM((RING, RING, 8, 128), F32)
+MANY = pltpu.SemaphoreType.DMA((RING, RING))
+LEFT = pltpu.VMEM((256, 768), BF16)
+RIGHT = pltpu.VMEM((256, 256), BF16)
 EIGHT = pltpu.SemaphoreType.DMA((RING,))
 ONE = pltpu.SemaphoreType.DMA
 SENT_RING = [jax.ShapeDtypeStruct((PLANE, REST, 128), F32)] * RING
@@ -464,18 +489,18 @@
     begin = [WHOLE, CLASSES]
     ends = [EIGHT, EIGHT]
 
-    a = call(begin_ring, "a1", SENT_RING_MORE, begin + [HELD_MORE] + ends + [ONE], rate, classes, rows)
+    a = call(begin_ring, "a1", SENT_RING_MORE, begin + [HELD_MORE, CLASS_ROWS, EIGHT, MANY, ONE, EIGHT], rate, classes, rows)
     a = round_ring(a)
     b = call(begin_plane, "b1", SENT_PLANE, begin + [HELD] + ends + [ONE], rate, classes, rows)
     b = in_plane(b)
-    b = call(plane_to_ring(PLANE_AWAY, RING_HERE), "b2", SENT_RING, [HELD] + ends, rate, b)
+    b = call(plane_to_ring([], RING_HERE), "b2", SENT_RING, [HELD] + ends, rate, b)
     b = round_ring(b)
     a = call(ring_to_plane_first, "a2", SENT_PLANE_MORE, [HELD_MORE, ROWS] + ends + [ONE], rate, *a)
     a = in_plane(a)
     fitness = a
-    a = call(middle_ring, "a3", SENT_RING, [HELD, ROWS] + ends + [ONE], rate, a)
+    a = call(middle_ring, "a3", SENT_RING, [HELD, ROWS, LEFT, RIGHT] + ends + [ONE], rate, a)
     a = round_ring(a)
-    b = call(middle_plane, "b3", SENT_PLANE, [HELD, ROWS] + ends + [ONE], rate, fitness, *b)
+    b = call(middle_plane, "b3", SENT_PLANE, [HELD, ROWS, LEFT, RIGHT] + ends + [ONE], rate, fitness, *b)
     b = in_plane(b)
     b = call(plane_to_ring(PLANE_HERE, []), "b4", SENT_RING, [HELD] + ends, rate, b)
     b = round_ring(b)

time: 329 us -> 306 us (0.930)
  Pallas kernels: 64.5 us -> 41.1 us
    pallas_call x10, Pallas kernels: 64.5 us -> 41.1 us  [call(): pl.pallas_call(kernel, out_shape=outs, in_specs=[SMEM] + [ANY] * len(oper...]
  transfers between devices with their start and end apart: 32 -> 32, of which waited for: 21 -> 21; matrix products, arithmetic and copies ran while one was open for 0% -> 0% of each run, Pallas kernels for 12% -> 8%
where the time goes in v1:
time: 306 us; the launch traced here: 305 us
  waiting for transfers between devices  159 us (52%)
  starting transfers between devices  93.3 us (30%)
  Pallas kernels  41.1 us (13%)
  local copies, waits for them, and re-layouts  11.5 us (4%)
    ppermute x28, waiting for transfers between devices, round_ring(): lax.ppermute(part, AXES, ring_pairs(shift))  157 us
    ppermute x28, starting transfers between devices, round_ring(): lax.ppermute(part, AXES, ring_pairs(shift))  60 us
    pallas_call x10, Pallas kernels, call(): pl.pallas_call(kernel, out_shape=outs, in_specs=[SMEM] + [ANY] * len(oper...  41.1 us
    all_to_all x4, starting transfers between devices, in_plane(): lax.all_to_all(piece, AXES, split_axis=0, concat_axis=0, tiled=True, axis...  33.3 us
    unnamed x24, local copies, waits for them, and re-layouts  11.5 us
  transfers between devices with their start and end apart: 32, of which 21 were waited for; matrix products, arithmetic and copies ran while one was open for 0% of the time, Pallas kernels for 8%

profile of v1, /device:TPU:1, one launch (start us, length us, event | category | flops | bytes accessed | tf_op | source)
XLA Modules:
  0.0 304.9 jit_solution(9288376931021898560)
XLA Ops:
  0.0 5.1 %shard_map.42 = f32[32,128,128]{2,1,0:T(8,128)} custom-call(s32[2]{0:T(128)} %rate_ref.19, s32[128,128]{1,0:T(8,128)} %bitcast.13, f32[8,1024,128]{2,1,0:T(8,128)} %bitcast.11), custom_call_target="tpu_custom_call" | custom-call | flops 268435456 | bytes 8388608 | tf_op jit(solution)/shard_map/pallas_call | solution.py:458
  5.2 8.6 %all-to-all-start.2 = ((f32[32,128,128]{2,1,0:T(8,128)}), f32[32,128,128]{2,1,0:T(8,128)S(1)}, u32[]{:S(2)}, u32[]{:S(2)}) async-start(f32[32,128,128]{2,1,0:T(8,128)} %shard_map.42), calls=%async_computation.2 | async-start | bytes 4194304 | tf_op jit(solution)/shard_map/all_to_all | solution.py:480
  13.8 5.6 %shard_map.37 = (f32[33,16,128]{2,1,0:T(8,128)}, f32[33,16,128]{2,1,0:T(8,128)}, f32[33,16,128]{2,1,0:T(8,128)}, f32[33,16,128]{2,1,0:T(8,128)}, f32[33,16,128]{...) custom-call(s32[2]{0:T(128)} %rate_ref.19, s32[128,128]{1,0:T(8,128)} %bitcast.14, ...), custom_call_target="tpu_custom_call" | custom-call | flops 268435456 | bytes 8388608 | tf_op jit(solution)/shard_map/pallas_call | solution.py:458
  19.4 1.7 collective-permute-start
  21.1 3.0 collective-permute-start.1
  24.1 3.8 %collective-permute-start.2 = (f32[33,16,128]{2,1,0:T(8,128)}, f32[33,16,128]{2,1,0:T(8,128)S(1)}, u32[]{:S(2)}, u32[]{:S(2)}) collective-permute-start(f32[33,16,128]{2,1,0:T(8,128)} %get-tuple-element.40), channel_id=1, source_target_pairs={{0,192},{1,193},{2,194},{3,195},{8,200},{9,201},{10,202},{11,203},... | collective-permute-start | bytes 811016 | tf_op jit(solution)/shard_map/ppermute | solution.py:473
  28.3 4.5 %collective-permute-start.4 = (f32[33,16,128]{2,1,0:T(8,128)}, f32[33,16,128]{2,1,0:T(8,128)S(1)}, u32[]{:S(2)}, u32[]{:S(2)}) collective-permute-start(f32[33,16,128]{2,1,0:T(8,128)} %get-tuple-element.42), channel_id=1, source_target_pairs={{0,68},{1,69},{2,70},{3,71},{8,76},{9,77},{10,78},{11,79},{16,84},... | collective-permute-start | bytes 811016 | tf_op jit(solution)/shard_map/ppermute | solution.py:473
  32.8 2.4 collective-permute-start.5
  35.1 4.0 %collective-permute-done.1.refs_2_ = f32[33,16,128]{2,1,0:T(8,128)S(1)} collective-permute-done((f32[33,16,128]{2,1,0:T(8,128)}, f32[33,16,128]{2,1,0:T(8,128)S(1)}, u32[]{:S(2)}, u32[]{:S(2)}) %collective-permute-start.1) | collective-permute-done | bytes 270368 | tf_op jit(solution)/shard_map/ppermute | solution.py:473
  39.2 6.9 %collective-permute-start.6 = (f32[33,16,128]{2,1,0:T(8,128)}, f32[33,16,128]{2,1,0:T(8,128)S(1)}, u32[]{:S(2)}, u32[]{:S(2)}) collective-permute-start(f32[33,16,128]{2,1,0:T(8,128)} %get-tuple-element.44), channel_id=1, source_target_pairs={{0,196},{1,197},{2,198},{3,199},{8,204},{9,205},{10,206},{11,207},... | collective-permute-start | bytes 811016 | tf_op jit(solution)/shard_map/ppermute | solution.py:473
  46.1 15.1 %collective-permute-done.2.refs_3_ = f32[33,16,128]{2,1,0:T(8,128)S(1)} collective-permute-done((f32[33,16,128]{2,1,0:T(8,128)}, f32[33,16,128]{2,1,0:T(8,128)S(1)}, u32[]{:S(2)}, u32[]{:S(2)}) %collective-permute-start.2) | collective-permute-done | bytes 270368 | tf_op jit(solution)/shard_map/ppermute | solution.py:473
  61.2 5.1 %collective-permute-done.3.refs_4_ = f32[33,16,128]{2,1,0:T(8,128)S(1)} collective-permute-done((f32[33,16,128]{2,1,0:T(8,128)}, f32[33,16,128]{2,1,0:T(8,128)S(1)}, u32[]{:S(2)}, u32[]{:S(2)}) %collective-permute-start.3) | collective-permute-done | bytes 270368 | tf_op jit(solution)/shard_map/ppermute | solution.py:473
  66.3 7.8 %collective-permute-done.5.refs_6_ = f32[33,16,128]{2,1,0:T(8,128)S(1)} collective-permute-done((f32[33,16,128]{2,1,0:T(8,128)}, f32[33,16,128]{2,1,0:T(8,128)S(1)}, u32[]{:S(2)}, u32[]{:S(2)}) %collective-permute-start.5) | collective-permute-done | bytes 270368 | tf_op jit(solution)/shard_map/ppermute | solution.py:473
  74.1 2.4 collective-permute-done.6.refs_7_
  77.5 2.6 shard_map.38
  82.8 8.5 %all-to-all-start = ((f32[32,136,128]{2,1,0:T(8,128)}), f32[32,136,128]{2,1,0:T(8,128)S(1)}, u32[]{:S(2)}, u32[]{:S(2)}) async-start(f32[32,136,128]{2,1,0:T(8,128)} %copy-done), calls=%async_computation | async-start | bytes 4456448 | tf_op jit(solution)/shard_map/all_to_all | solution.py:480
  94.5 3.4 %collective-permute-start.14 = (f32[32,16,128]{2,1,0:T(8,128)S(1)}, f32[32,16,128]{2,1,0:T(8,128)S(1)}, u32[]{:S(2)}, u32[]{:S(2)}) collective-permute-start(f32[32,16,128]{2,1,0:T(8,128)S(1)} %get-tuple-element.54), channel_id=1, source_target_pairs={{0,64},{1,65},{2,66},{3,67},{8,72},{9,73},{10,74},{11,75},{16,80},... | collective-permute-start | bytes 786440 | tf_op jit(solution)/shard_map/ppermute | solution.py:473
  99.0 4.5 %collective-permute-start.17 = (f32[32,16,128]{2,1,0:T(8,128)S(1)}, f32[32,16,128]{2,1,0:T(8,128)S(1)}, u32[]{:S(2)}, u32[]{:S(2)}) collective-permute-start(f32[32,16,128]{2,1,0:T(8,128)S(1)} %get-tuple-element.57), channel_id=1, source_target_pairs={{0,4},{1,5},{2,6},{3,7},{8,12},{9,13},{10,14},{11,15},{16,20},{17,... | collective-permute-start | bytes 786440 | tf_op jit(solution)/shard_map/ppermute | solution.py:473
  104.7 2.1 collective-permute-start.19
  106.8 9.5 %collective-permute-done.15.refs_2_ = f32[32,16,128]{2,1,0:T(8,128)S(1)} collective-permute-done((f32[32,16,128]{2,1,0:T(8,128)S(1)}, f32[32,16,128]{2,1,0:T(8,128)S(1)}, u32[]{:S(2)}, u32[]{:S(2)}) %collective-permute-start.15) | collective-permute-done | bytes 262176 | tf_op jit(solution)/shard_map/ppermute | solution.py:473
  116.3 9.8 %collective-permute-done.16.refs_3_ = f32[32,16,128]{2,1,0:T(8,128)S(1)} collective-permute-done((f32[32,16,128]{2,1,0:T(8,128)S(1)}, f32[32,16,128]{2,1,0:T(8,128)S(1)}, u32[]{:S(2)}, u32[]{:S(2)}) %collective-permute-start.16) | collective-permute-done | bytes 262176 | tf_op jit(solution)/shard_map/ppermute | solution.py:473
  126.1 14.0 %collective-permute-done.17.refs_4_ = f32[32,16,128]{2,1,0:T(8,128)S(1)} collective-permute-done((f32[32,16,128]{2,1,0:T(8,128)S(1)}, f32[32,16,128]{2,1,0:T(8,128)S(1)}, u32[]{:S(2)}, u32[]{:S(2)}) %collective-permute-start.17) | collective-permute-done | bytes 262176 | tf_op jit(solution)/shard_map/ppermute | solution.py:473
  140.8 4.0 %collective-permute-done.19.refs_6_ = f32[32,16,128]{2,1,0:T(8,128)S(1)} collective-permute-done((f32[32,16,128]{2,1,0:T(8,128)S(1)}, f32[32,16,128]{2,1,0:T(8,128)S(1)}, u32[]{:S(2)}, u32[]{:S(2)}) %collective-permute-start.19) | collective-permute-done | bytes 262176 | tf_op jit(solution)/shard_map/ppermute | solution.py:473
  145.5 4.8 %collective-permute-done.20.refs_7_ = f32[32,16,128]{2,1,0:T(8,128)S(1)} collective-permute-done((f32[32,16,128]{2,1,0:T(8,128)S(1)}, f32[32,16,128]{2,1,0:T(8,128)S(1)}, u32[]{:S(2)}, u32[]{:S(2)}) %collective-permute-start.20) | collective-permute-done | bytes 262176 | tf_op jit(solution)/shard_map/ppermute | solution.py:473
  153.9 7.3 %shard_map.44 = f32[32,128,128]{2,1,0:T(8,128)S(1)} custom-call(s32[2]{0:T(128)S(1)} %copy-done.11, f32[32,136,128]{2,1,0:T(8,128)S(1)} %all-to-all-done.x_ref.fitness_ref, f32[32,16,128]{2,1,0:T(8,128)S(1)} %get-tuple-element.53.refs_0_, f32[32,16,128]{2,1,0:T(8,128)S(1)} %collective-permute-done.14.refs_1_, ...), custom_call_target="tpu_custom_call" | custom-call | flops 268435456 | bytes 8388608 | tf_op jit(solution)/shard_map/pallas_call | solution.py:458
  162.6 7.7 %all-to-all-start.3 = ((f32[32,128,128]{2,1,0:T(8,128)}), f32[32,128,128]{2,1,0:T(8,128)}, u32[]{:S(2)}, u32[]{:S(2)}) async-start(f32[32,128,128]{2,1,0:T(8,128)} %copy-done.1), calls=%async_computation.3 | async-start | bytes 4194304 | tf_op jit(solution)/shard_map/all_to_all | solution.py:480
  170.3 6.7 %shard_map.39 = (f32[32,16,128]{2,1,0:T(8,128)S(1)}, f32[32,16,128]{2,1,0:T(8,128)S(1)}, f32[32,16,128]{2,1,0:T(8,128)S(1)}, f32[32,16,128]{2,1,0:T(8,128)S(1)},...) custom-call(s32[2]{0:T(128)S(1)} %copy-done.11, ...), custom_call_target="tpu_custom_call" | custom-call | flops 268435456 | bytes 8388608 | tf_op jit(solution)/shard_map/pallas_call | solution.py:458
  178.9 3.3 %collective-permute-start.9 = (f32[32,16,128]{2,1,0:T(8,128)S(1)}, f32[32,16,128]{2,1,0:T(8,128)S(1)}, u32[]{:S(2)}, u32[]{:S(2)}) collective-permute-start(f32[32,16,128]{2,1,0:T(8,128)S(1)} %get-tuple-element.48), channel_id=1, source_target_pairs={{0,192},{1,193},{2,194},{3,195},{8,200},{9,201},{10,202},{11,203},... | collective-permute-start | bytes 786440 | tf_op jit(solution)/shard_map/ppermute | solution.py:473
  183.1 4.1 %collective-permute-start.11 = (f32[32,16,128]{2,1,0:T(8,128)S(1)}, f32[32,16,128]{2,1,0:T(8,128)S(1)}, u32[]{:S(2)}, u32[]{:S(2)}) collective-permute-start(f32[32,16,128]{2,1,0:T(8,128)S(1)} %get-tuple-element.50), channel_id=1, source_target_pairs={{0,68},{1,69},{2,70},{3,71},{8,76},{9,77},{10,78},{11,79},{16,84},... | collective-permute-start | bytes 786440 | tf_op jit(solution)/shard_map/ppermute | solution.py:473
  187.2 2.7 collective-permute-start.12
  189.9 8.8 %collective-permute-done.8.refs_2_ = f32[32,16,128]{2,1,0:T(8,128)S(1)} collective-permute-done((f32[32,16,128]{2,1,0:T(8,128)S(1)}, f32[32,16,128]{2,1,0:T(8,128)S(1)}, u32[]{:S(2)}, u32[]{:S(2)}) %collective-permute-start.8) | collective-permute-done | bytes 262176 | tf_op jit(solution)/shard_map/ppermute | solution.py:473
  198.7 15.0 %collective-permute-done.9.refs_3_ = f32[32,16,128]{2,1,0:T(8,128)S(1)} collective-permute-done((f32[32,16,128]{2,1,0:T(8,128)S(1)}, f32[32,16,128]{2,1,0:T(8,128)S(1)}, u32[]{:S(2)}, u32[]{:S(2)}) %collective-permute-start.9) | collective-permute-done | bytes 262176 | tf_op jit(solution)/shard_map/ppermute | solution.py:473
  213.6 10.1 %collective-permute-done.10.refs_4_ = f32[32,16,128]{2,1,0:T(8,128)S(1)} collective-permute-done((f32[32,16,128]{2,1,0:T(8,128)S(1)}, f32[32,16,128]{2,1,0:T(8,128)S(1)}, u32[]{:S(2)}, u32[]{:S(2)}) %collective-permute-start.10) | collective-permute-done | bytes 262176 | tf_op jit(solution)/shard_map/ppermute | solution.py:473
  223.7 3.7 %collective-permute-done.12.refs_6_ = f32[32,16,128]{2,1,0:T(8,128)S(1)} collective-permute-done((f32[32,16,128]{2,1,0:T(8,128)S(1)}, f32[32,16,128]{2,1,0:T(8,128)S(1)}, u32[]{:S(2)}, u32[]{:S(2)}) %collective-permute-start.12) | collective-permute-done | bytes 262176 | tf_op jit(solution)/shard_map/ppermute | solution.py:473
  227.4 2.2 collective-permute-done.13.refs_7_
  229.6 2.7 shard_map.40
  232.4 8.6 %all-to-all-start.1 = ((f32[32,128,128]{2,1,0:T(8,128)}), f32[32,128,128]{2,1,0:T(8,128)S(1)}, u32[]{:S(2)}, u32[]{:S(2)}) async-start(f32[32,128,128]{2,1,0:T(8,128)} %shard_map.40), calls=%async_computation.1 | async-start | bytes 4194304 | tf_op jit(solution)/shard_map/all_to_all | solution.py:480
  241.0 3.5 %shard_map.45 = (f32[32,16,128]{2,1,0:T(8,128)S(1)}, f32[32,16,128]{2,1,0:T(8,128)S(1)}, f32[32,16,128]{2,1,0:T(8,128)S(1)}, f32[32,16,128]{2,1,0:T(8,128)}, f32...) custom-call(s32[2]{0:T(128)S(1)} %copy-done.11, ...), custom_call_target="tpu_custom_call" | custom-call | flops 268435456 | bytes 8388608 | tf_op jit(solution)/shard_map/pallas_call | solution.py:458
  244.5 3.2 %collective-permute-start.21 = (f32[32,16,128]{2,1,0:T(8,128)S(1)}, f32[32,16,128]{2,1,0:T(8,128)S(1)}, u32[]{:S(2)}, u32[]{:S(2)}) collective-permute-start(f32[32,16,128]{2,1,0:T(8,128)S(1)} %get-tuple-element.62), channel_id=1, source_target_pairs={{0,64},{1,65},{2,66},{3,67},{8,72},{9,73},{10,74},{11,75},{16,80},... | collective-permute-start | bytes 786440 | tf_op jit(solution)/shard_map/ppermute | solution.py:473
  249.0 4.4 %collective-permute-start.24 = (f32[32,16,128]{2,1,0:T(8,128)}, f32[32,16,128]{2,1,0:T(8,128)S(1)}, u32[]{:S(2)}, u32[]{:S(2)}) collective-permute-start(f32[32,16,128]{2,1,0:T(8,128)} %get-tuple-element.65), channel_id=1, source_target_pairs={{0,4},{1,5},{2,6},{3,7},{8,12},{9,13},{10,14},{11,15},{16,20},{17,... | collective-permute-start | bytes 786440 | tf_op jit(solution)/shard_map/ppermute | solution.py:473
  254.7 2.1 collective-permute-start.26
  256.8 9.6 %collective-permute-done.22.refs_2_ = f32[32,16,128]{2,1,0:T(8,128)S(1)} collective-permute-done((f32[32,16,128]{2,1,0:T(8,128)S(1)}, f32[32,16,128]{2,1,0:T(8,128)S(1)}, u32[]{:S(2)}, u32[]{:S(2)}) %collective-permute-start.22) | collective-permute-done | bytes 262176 | tf_op jit(solution)/shard_map/ppermute | solution.py:473
  268.0 1.8 shard_map.41.other_ref
  269.9 6.3 %collective-permute-done.23.refs_3_ = f32[32,16,128]{2,1,0:T(8,128)S(1)} collective-permute-done((f32[32,16,128]{2,1,0:T(8,128)}, f32[32,16,128]{2,1,0:T(8,128)S(1)}, u32[]{:S(2)}, u32[]{:S(2)}) %collective-permute-start.23) | collective-permute-done | bytes 262176 | tf_op jit(solution)/shard_map/ppermute | solution.py:473
  276.2 13.8 %collective-permute-done.24.refs_4_ = f32[32,16,128]{2,1,0:T(8,128)S(1)} collective-permute-done((f32[32,16,128]{2,1,0:T(8,128)}, f32[32,16,128]{2,1,0:T(8,128)S(1)}, u32[]{:S(2)}, u32[]{:S(2)}) %collective-permute-start.24) | collective-permute-done | bytes 262176 | tf_op jit(solution)/shard_map/ppermute | solution.py:473
  290.0 5.1 %collective-permute-done.26.refs_6_ = f32[32,16,128]{2,1,0:T(8,128)} collective-permute-done((f32[32,16,128]{2,1,0:T(8,128)}, f32[32,16,128]{2,1,0:T(8,128)}, u32[]{:S(2)}, u32[]{:S(2)}) %collective-permute-start.26) | collective-permute-done | bytes 262176 | tf_op jit(solution)/shard_map/ppermute | solution.py:473
  295.2 5.4 %collective-permute-done.27.refs_7_ = f32[32,16,128]{2,1,0:T(8,128)} collective-permute-done((f32[32,16,128]{2,1,0:T(8,128)}, f32[32,16,128]{2,1,0:T(8,128)}, u32[]{:S(2)}, u32[]{:S(2)}) %collective-permute-start.27) | collective-permute-done | bytes 262176 | tf_op jit(solution)/shard_map/ppermute | solution.py:473
  300.6 4.1 %shard_map.46 = f32[8,1024,128]{2,1,0:T(8,128)} custom-call(s32[2]{0:T(128)S(1)} %copy-done.11, f32[8,32,16,128]{3,2,1,0:T(8,128)S(1)} %shard_map.41.other_ref, f32[32,16,128]{2,1,0:T(8,128)S(1)} %get-tuple-element.61.refs_0_, f32[32,16,128]{2,1,0:T(8,128)S(1)} %collective-permute-done.21.refs_1_, f32[32,16,128]{2,1,0:T(8,128)S(1)} %collective-permute-done.22.refs_2_, ...), custom_call_target="tpu_custom_call" | custom-call | flops 268435456 | bytes 8388608 | tf_op jit(solution)/shard_map/pallas_call | solution.py:458
  (50 shorter events, 22.9 us)
Async XLA Ops:
  5.2 76.3 %all-to-all-start.2 = ((f32[32,128,128]{2,1,0:T(8,128)}), f32[32,128,128]{2,1,0:T(8,128)S(1)}, u32[]{:S(2)}, u32[]{:S(2)}) async-start(f32[32,128,128]{2,1,0:T(8,128)} %shard_map.42), calls=%async_computation.2 | async-start | bytes 4194304 | tf_op jit(solution)/shard_map/all_to_all | solution.py:480
  13.8 62.8 %copy-start.11 = (s32[2]{0:T(128)S(1)}, s32[2]{0:T(128)}, u32[]{:S(2)}) copy-start(s32[2]{0:T(128)} %rate_ref.19) | copy-start | bytes 28
  19.4 13.4 %collective-permute-start = (f32[33,16,128]{2,1,0:T(8,128)}, f32[33,16,128]{2,1,0:T(8,128)S(1)}, u32[]{:S(2)}, u32[]{:S(2)}) collective-permute-start(f32[33,16,128]{2,1,0:T(8,128)} %get-tuple-element.38), channel_id=1, source_target_pairs={{0,64},{1,65},{2,66},{3,67},{8,72},{9,73},{10,74},{11,75},{16,80},... | collective-permute-start | bytes 811016 | tf_op jit(solution)/shard_map/ppermute | solution.py:473
  21.1 18.1 %collective-permute-start.1 = (f32[33,16,128]{2,1,0:T(8,128)}, f32[33,16,128]{2,1,0:T(8,128)S(1)}, u32[]{:S(2)}, u32[]{:S(2)}) collective-permute-start(f32[33,16,128]{2,1,0:T(8,128)} %get-tuple-element.39), channel_id=1, source_target_pairs={{0,128},{1,129},{2,130},{3,131},{8,136},{9,137},{10,138},{11,139},... | collective-permute-start | bytes 811016 | tf_op jit(solution)/shard_map/ppermute | solution.py:473
  24.1 37.1 %collective-permute-start.2 = (f32[33,16,128]{2,1,0:T(8,128)}, f32[33,16,128]{2,1,0:T(8,128)S(1)}, u32[]{:S(2)}, u32[]{:S(2)}) collective-permute-start(f32[33,16,128]{2,1,0:T(8,128)} %get-tuple-element.40), channel_id=1, source_target_pairs={{0,192},{1,193},{2,194},{3,195},{8,200},{9,201},{10,202},{11,203},... | collective-permute-start | bytes 811016 | tf_op jit(solution)/shard_map/ppermute | solution.py:473
  27.8 38.5 %collective-permute-start.3 = (f32[33,16,128]{2,1,0:T(8,128)}, f32[33,16,128]{2,1,0:T(8,128)S(1)}, u32[]{:S(2)}, u32[]{:S(2)}) collective-permute-start(f32[33,16,128]{2,1,0:T(8,128)} %get-tuple-element.41), channel_id=1, source_target_pairs={{0,4},{1,5},{2,6},{3,7},{8,12},{9,13},{10,14},{11,15},{16,20},{17,... | collective-permute-start | bytes 811016 | tf_op jit(solution)/shard_map/ppermute | solution.py:473
  28.3 38.0 %collective-permute-start.4 = (f32[33,16,128]{2,1,0:T(8,128)}, f32[33,16,128]{2,1,0:T(8,128)S(1)}, u32[]{:S(2)}, u32[]{:S(2)}) collective-permute-start(f32[33,16,128]{2,1,0:T(8,128)} %get-tuple-element.42), channel_id=1, source_target_pairs={{0,68},{1,69},{2,70},{3,71},{8,76},{9,77},{10,78},{11,79},{16,84},... | collective-permute-start | bytes 811016 | tf_op jit(solution)/shard_map/ppermute | solution.py:473
  32.8 41.4 %collective-permute-start.5 = (f32[33,16,128]{2,1,0:T(8,128)}, f32[33,16,128]{2,1,0:T(8,128)S(1)}, u32[]{:S(2)}, u32[]{:S(2)}) collective-permute-start(f32[33,16,128]{2,1,0:T(8,128)} %get-tuple-element.43), channel_id=1, source_target_pairs={{0,132},{1,133},{2,134},{3,135},{8,140},{9,141},{10,142},{11,143},... | collective-permute-start | bytes 811016 | tf_op jit(solution)/shard_map/ppermute | solution.py:473
  39.2 37.4 %collective-permute-start.6 = (f32[33,16,128]{2,1,0:T(8,128)}, f32[33,16,128]{2,1,0:T(8,128)S(1)}, u32[]{:S(2)}, u32[]{:S(2)}) collective-permute-start(f32[33,16,128]{2,1,0:T(8,128)} %get-tuple-element.44), channel_id=1, source_target_pairs={{0,196},{1,197},{2,198},{3,199},{8,204},{9,205},{10,206},{11,207},... | collective-permute-start | bytes 811016 | tf_op jit(solution)/shard_map/ppermute | solution.py:473
  76.6 1.0 copy-start.4
  80.1 1.4 copy-start
  81.5 1.3 copy-start.2
  82.8 68.2 %all-to-all-start = ((f32[32,136,128]{2,1,0:T(8,128)}), f32[32,136,128]{2,1,0:T(8,128)S(1)}, u32[]{:S(2)}, u32[]{:S(2)}) async-start(f32[32,136,128]{2,1,0:T(8,128)} %copy-done), calls=%async_computation | async-start | bytes 4456448 | tf_op jit(solution)/shard_map/all_to_all | solution.py:480
  91.3 1.6 copy-start.3
  94.5 10.2 %collective-permute-start.14 = (f32[32,16,128]{2,1,0:T(8,128)S(1)}, f32[32,16,128]{2,1,0:T(8,128)S(1)}, u32[]{:S(2)}, u32[]{:S(2)}) collective-permute-start(f32[32,16,128]{2,1,0:T(8,128)S(1)} %get-tuple-element.54), channel_id=1, source_target_pairs={{0,64},{1,65},{2,66},{3,67},{8,72},{9,73},{10,74},{11,75},{16,80},... | collective-permute-start | bytes 786440 | tf_op jit(solution)/shard_map/ppermute | solution.py:473
  97.9 18.4 %collective-permute-start.15 = (f32[32,16,128]{2,1,0:T(8,128)S(1)}, f32[32,16,128]{2,1,0:T(8,128)S(1)}, u32[]{:S(2)}, u32[]{:S(2)}) collective-permute-start(f32[32,16,128]{2,1,0:T(8,128)S(1)} %get-tuple-element.55), channel_id=1, source_target_pairs={{0,128},{1,129},{2,130},{3,131},{8,136},{9,137},{10,138},{11,139},... | collective-permute-start | bytes 786440 | tf_op jit(solution)/shard_map/ppermute | solution.py:473
  98.7 27.4 %collective-permute-start.16 = (f32[32,16,128]{2,1,0:T(8,128)S(1)}, f32[32,16,128]{2,1,0:T(8,128)S(1)}, u32[]{:S(2)}, u32[]{:S(2)}) collective-permute-start(f32[32,16,128]{2,1,0:T(8,128)S(1)} %get-tuple-element.56), channel_id=1, source_target_pairs={{0,192},{1,193},{2,194},{3,195},{8,200},{9,201},{10,202},{11,203},... | collective-permute-start | bytes 786440 | tf_op jit(solution)/shard_map/ppermute | solution.py:473
  99.0 41.1 %collective-permute-start.17 = (f32[32,16,128]{2,1,0:T(8,128)S(1)}, f32[32,16,128]{2,1,0:T(8,128)S(1)}, u32[]{:S(2)}, u32[]{:S(2)}) collective-permute-start(f32[32,16,128]{2,1,0:T(8,128)S(1)} %get-tuple-element.57), channel_id=1, source_target_pairs={{0,4},{1,5},{2,6},{3,7},{8,12},{9,13},{10,14},{11,15},{16,20},{17,... | collective-permute-start | bytes 786440 | tf_op jit(solution)/shard_map/ppermute | solution.py:473
  103.5 36.6 %collective-permute-start.18 = (f32[32,16,128]{2,1,0:T(8,128)S(1)}, f32[32,16,128]{2,1,0:T(8,128)S(1)}, u32[]{:S(2)}, u32[]{:S(2)}) collective-permute-start(f32[32,16,128]{2,1,0:T(8,128)S(1)} %get-tuple-element.58), channel_id=1, source_target_pairs={{0,68},{1,69},{2,70},{3,71},{8,76},{9,77},{10,78},{11,79},{16,84},... | collective-permute-start | bytes 786440 | tf_op jit(solution)/shard_map/ppermute | solution.py:473
  104.7 40.1 %collective-permute-start.19 = (f32[32,16,128]{2,1,0:T(8,128)S(1)}, f32[32,16,128]{2,1,0:T(8,128)S(1)}, u32[]{:S(2)}, u32[]{:S(2)}) collective-permute-start(f32[32,16,128]{2,1,0:T(8,128)S(1)} %get-tuple-element.59), channel_id=1, source_target_pairs={{0,132},{1,133},{2,134},{3,135},{8,140},{9,141},{10,142},{11,143},... | collective-permute-start | bytes 786440 | tf_op jit(solution)/shard_map/ppermute | solution.py:473
  116.3 34.1 %collective-permute-start.20 = (f32[32,16,128]{2,1,0:T(8,128)S(1)}, f32[32,16,128]{2,1,0:T(8,128)S(1)}, u32[]{:S(2)}, u32[]{:S(2)}) collective-permute-start(f32[32,16,128]{2,1,0:T(8,128)S(1)} %get-tuple-element.60), channel_id=1, source_target_pairs={{0,196},{1,197},{2,198},{3,199},{8,204},{9,205},{10,206},{11,207},... | collective-permute-start | bytes 786440 | tf_op jit(solution)/shard_map/ppermute | solution.py:473
  140.1 0.7 copy-start.5
  144.8 0.7 copy-start.7
  150.4 0.7 copy-start.9
  151.1 1.0 copy-start.6
  152.0 0.9 copy-start.8
  153.0 0.9 copy-start.10
  161.2 1.3 copy-start.1
  162.6 69.8 %all-to-all-start.3 = ((f32[32,128,128]{2,1,0:T(8,128)}), f32[32,128,128]{2,1,0:T(8,128)}, u32[]{:S(2)}, u32[]{:S(2)}) async-start(f32[32,128,128]{2,1,0:T(8,128)} %copy-done.1), calls=%async_computation.3 | async-start | bytes 4194304 | tf_op jit(solution)/shard_map/all_to_all | solution.py:480
  177.0 10.2 %collective-permute-start.7 = (f32[32,16,128]{2,1,0:T(8,128)S(1)}, f32[32,16,128]{2,1,0:T(8,128)S(1)}, u32[]{:S(2)}, u32[]{:S(2)}) collective-permute-start(f32[32,16,128]{2,1,0:T(8,128)S(1)} %get-tuple-element.46), channel_id=1, source_target_pairs={{0,64},{1,65},{2,66},{3,67},{8,72},{9,73},{10,74},{11,75},{16,80},... | collective-permute-start | bytes 786440 | tf_op jit(solution)/shard_map/ppermute | solution.py:473
  177.4 21.3 %collective-permute-start.8 = (f32[32,16,128]{2,1,0:T(8,128)S(1)}, f32[32,16,128]{2,1,0:T(8,128)S(1)}, u32[]{:S(2)}, u32[]{:S(2)}) collective-permute-start(f32[32,16,128]{2,1,0:T(8,128)S(1)} %get-tuple-element.47), channel_id=1, source_target_pairs={{0,128},{1,129},{2,130},{3,131},{8,136},{9,137},{10,138},{11,139},... | collective-permute-start | bytes 786440 | tf_op jit(solution)/shard_map/ppermute | solution.py:473
  178.9 34.8 %collective-permute-start.9 = (f32[32,16,128]{2,1,0:T(8,128)S(1)}, f32[32,16,128]{2,1,0:T(8,128)S(1)}, u32[]{:S(2)}, u32[]{:S(2)}) collective-permute-start(f32[32,16,128]{2,1,0:T(8,128)S(1)} %get-tuple-element.48), channel_id=1, source_target_pairs={{0,192},{1,193},{2,194},{3,195},{8,200},{9,201},{10,202},{11,203},... | collective-permute-start | bytes 786440 | tf_op jit(solution)/shard_map/ppermute | solution.py:473
  182.2 41.5 %collective-permute-start.10 = (f32[32,16,128]{2,1,0:T(8,128)S(1)}, f32[32,16,128]{2,1,0:T(8,128)S(1)}, u32[]{:S(2)}, u32[]{:S(2)}) collective-permute-start(f32[32,16,128]{2,1,0:T(8,128)S(1)} %get-tuple-element.49), channel_id=1, source_target_pairs={{0,4},{1,5},{2,6},{3,7},{8,12},{9,13},{10,14},{11,15},{16,20},{17,... | collective-permute-start | bytes 786440 | tf_op jit(solution)/shard_map/ppermute | solution.py:473
  183.1 40.7 %collective-permute-start.11 = (f32[32,16,128]{2,1,0:T(8,128)S(1)}, f32[32,16,128]{2,1,0:T(8,128)S(1)}, u32[]{:S(2)}, u32[]{:S(2)}) collective-permute-start(f32[32,16,128]{2,1,0:T(8,128)S(1)} %get-tuple-element.50), channel_id=1, source_target_pairs={{0,68},{1,69},{2,70},{3,71},{8,76},{9,77},{10,78},{11,79},{16,84},... | collective-permute-start | bytes 786440 | tf_op jit(solution)/shard_map/ppermute | solution.py:473
  187.2 40.2 %collective-permute-start.12 = (f32[32,16,128]{2,1,0:T(8,128)S(1)}, f32[32,16,128]{2,1,0:T(8,128)S(1)}, u32[]{:S(2)}, u32[]{:S(2)}) collective-permute-start(f32[32,16,128]{2,1,0:T(8,128)S(1)} %get-tuple-element.51), channel_id=1, source_target_pairs={{0,132},{1,133},{2,134},{3,135},{8,140},{9,141},{10,142},{11,143},... | collective-permute-start | bytes 786440 | tf_op jit(solution)/shard_map/ppermute | solution.py:473
  198.6 31.0 %collective-permute-start.13 = (f32[32,16,128]{2,1,0:T(8,128)S(1)}, f32[32,16,128]{2,1,0:T(8,128)S(1)}, u32[]{:S(2)}, u32[]{:S(2)}) collective-permute-start(f32[32,16,128]{2,1,0:T(8,128)S(1)} %get-tuple-element.52), channel_id=1, source_target_pairs={{0,196},{1,197},{2,198},{3,199},{8,204},{9,205},{10,206},{11,207},... | collective-permute-start | bytes 786440 | tf_op jit(solution)/shard_map/ppermute | solution.py:473
  232.4 35.6 %all-to-all-start.1 = ((f32[32,128,128]{2,1,0:T(8,128)}), f32[32,128,128]{2,1,0:T(8,128)S(1)}, u32[]{:S(2)}, u32[]{:S(2)}) async-start(f32[32,128,128]{2,1,0:T(8,128)} %shard_map.40), calls=%async_computation.1 | async-start | bytes 4194304 | tf_op jit(solution)/shard_map/all_to_all | solution.py:480
  244.5 10.2 %collective-permute-start.21 = (f32[32,16,128]{2,1,0:T(8,128)S(1)}, f32[32,16,128]{2,1,0:T(8,128)S(1)}, u32[]{:S(2)}, u32[]{:S(2)}) collective-permute-start(f32[32,16,128]{2,1,0:T(8,128)S(1)} %get-tuple-element.62), channel_id=1, source_target_pairs={{0,64},{1,65},{2,66},{3,67},{8,72},{9,73},{10,74},{11,75},{16,80},... | collective-permute-start | bytes 786440 | tf_op jit(solution)/shard_map/ppermute | solution.py:473
  247.7 18.6 %collective-permute-start.22 = (f32[32,16,128]{2,1,0:T(8,128)S(1)}, f32[32,16,128]{2,1,0:T(8,128)S(1)}, u32[]{:S(2)}, u32[]{:S(2)}) collective-permute-start(f32[32,16,128]{2,1,0:T(8,128)S(1)} %get-tuple-element.63), channel_id=1, source_target_pairs={{0,128},{1,129},{2,130},{3,131},{8,136},{9,137},{10,138},{11,139},... | collective-permute-start | bytes 786440 | tf_op jit(solution)/shard_map/ppermute | solution.py:473
  248.6 27.6 %collective-permute-start.23 = (f32[32,16,128]{2,1,0:T(8,128)}, f32[32,16,128]{2,1,0:T(8,128)S(1)}, u32[]{:S(2)}, u32[]{:S(2)}) collective-permute-start(f32[32,16,128]{2,1,0:T(8,128)} %get-tuple-element.64), channel_id=1, source_target_pairs={{0,192},{1,193},{2,194},{3,195},{8,200},{9,201},{10,202},{11,203},... | collective-permute-start | bytes 786440 | tf_op jit(solution)/shard_map/ppermute | solution.py:473
  249.0 41.0 %collective-permute-start.24 = (f32[32,16,128]{2,1,0:T(8,128)}, f32[32,16,128]{2,1,0:T(8,128)S(1)}, u32[]{:S(2)}, u32[]{:S(2)}) collective-permute-start(f32[32,16,128]{2,1,0:T(8,128)} %get-tuple-element.65), channel_id=1, source_target_pairs={{0,4},{1,5},{2,6},{3,7},{8,12},{9,13},{10,14},{11,15},{16,20},{17,... | collective-permute-start | bytes 786440 | tf_op jit(solution)/shard_map/ppermute | solution.py:473
  253.4 36.6 %collective-permute-start.25 = (f32[32,16,128]{2,1,0:T(8,128)}, f32[32,16,128]{2,1,0:T(8,128)}, u32[]{:S(2)}, u32[]{:S(2)}) collective-permute-start(f32[32,16,128]{2,1,0:T(8,128)} %get-tuple-element.66), channel_id=1, source_target_pairs={{0,68},{1,69},{2,70},{3,71},{8,76},{9,77},{10,78},{11,79},{16,84},... | collective-permute-start | bytes 786440 | tf_op jit(solution)/shard_map/ppermute | solution.py:473
  254.7 40.5 %collective-permute-start.26 = (f32[32,16,128]{2,1,0:T(8,128)}, f32[32,16,128]{2,1,0:T(8,128)}, u32[]{:S(2)}, u32[]{:S(2)}) collective-permute-start(f32[32,16,128]{2,1,0:T(8,128)} %get-tuple-element.67), channel_id=1, source_target_pairs={{0,132},{1,133},{2,134},{3,135},{8,140},{9,141},{10,142},{11,143},... | collective-permute-start | bytes 786440 | tf_op jit(solution)/shard_map/ppermute | solution.py:473
  266.3 34.3 %collective-permute-start.27 = (f32[32,16,128]{2,1,0:T(8,128)}, f32[32,16,128]{2,1,0:T(8,128)}, u32[]{:S(2)}, u32[]{:S(2)}) collective-permute-start(f32[32,16,128]{2,1,0:T(8,128)} %get-tuple-element.68), channel_id=1, source_target_pairs={{0,196},{1,197},{2,198},{3,199},{8,204},{9,205},{10,206},{11,207},... | collective-permute-start | bytes 786440 | tf_op jit(solution)/shard_map/ppermute | solution.py:473

commit v2 on v1

--- a/solution.py
+++ b/solution.py
@@ -468,12 +468,15 @@
     )(rate_index, *operands)
 
 
+SOONER = (3, 5)
+
+
 def round_ring(parts):
-    return [parts[0]] + [
-        lax.ppermute(part, AXES, ring_pairs(shift))
-        for shift, part in enumerate(parts)
-        if shift
-    ]
+    moved = list(parts)
+    for shifts in (SOONER, [shift for shift in range(1, RING) if shift not in SOONER]):
+        for shift in shifts:
+            moved[shift] = lax.ppermute(parts[shift], AXES, ring_pairs(shift))
+    return moved
 
 
 def in_plane(piece):

time: 306 us -> 306 us (level)
  no operation moved by 1% of the time
where the time goes in v2:
time: 306 us; the launch traced here: 305 us
  waiting for transfers between devices  159 us (52%)
  starting transfers between devices  93.3 us (30%)
  Pallas kernels  41.1 us (13%)
  local copies, waits for them, and re-layouts  11.5 us (4%)
    ppermute x28, waiting for transfers between devices, round_ring(): moved[shift] = lax.ppermute(parts[shift], AXES, ring_pairs(shift))  157 us
    ppermute x28, starting transfers between devices, round_ring(): moved[shift] = lax.ppermute(parts[shift], AXES, ring_pairs(shift))  60 us
    pallas_call x10, Pallas kernels, call(): pl.pallas_call(kernel, out_shape=outs, in_specs=[SMEM] + [ANY] * len(oper...  41.1 us
    all_to_all x4, starting transfers between devices, in_plane(): lax.all_to_all(piece, AXES, split_axis=0, concat_axis=0, tiled=True, axis...  33.3 us
    unnamed x24, local copies, waits for them, and re-layouts  11.5 us
  transfers between devices with their start and end apart: 32, of which 21 were waited for; matrix products, arithmetic and copies ran while one was open for 0% of the time, Pallas kernels for 8%

profile of v2, /device:TPU:1, one launch (start us, length us, event | category | flops | bytes accessed | tf_op | source)
XLA Modules:
  0.0 304.9 jit_solution(9288376931021898560)
XLA Ops:
  0.0 5.1 %shard_map.42 = f32[32,128,128]{2,1,0:T(8,128)} custom-call(s32[2]{0:T(128)} %rate_ref.19, s32[128,128]{1,0:T(8,128)} %bitcast.13, f32[8,1024,128]{2,1,0:T(8,128)} %bitcast.11), custom_call_target="tpu_custom_call" | custom-call | flops 268435456 | bytes 8388608 | tf_op jit(solution)/shard_map/pallas_call | solution.py:458
  5.2 8.6 %all-to-all-start.2 = ((f32[32,128,128]{2,1,0:T(8,128)}), f32[32,128,128]{2,1,0:T(8,128)S(1)}, u32[]{:S(2)}, u32[]{:S(2)}) async-start(f32[32,128,128]{2,1,0:T(8,128)} %shard_map.42), calls=%async_computation.2 | async-start | bytes 4194304 | tf_op jit(solution)/shard_map/all_to_all | solution.py:483
  13.8 5.6 %shard_map.37 = (f32[33,16,128]{2,1,0:T(8,128)}, f32[33,16,128]{2,1,0:T(8,128)}, f32[33,16,128]{2,1,0:T(8,128)}, f32[33,16,128]{2,1,0:T(8,128)}, f32[33,16,128]{...) custom-call(s32[2]{0:T(128)} %rate_ref.19, s32[128,128]{1,0:T(8,128)} %bitcast.14, ...), custom_call_target="tpu_custom_call" | custom-call | flops 268435456 | bytes 8388608 | tf_op jit(solution)/shard_map/pallas_call | solution.py:458
  19.4 1.7 collective-permute-start
  21.1 3.0 collective-permute-start.1
  24.1 3.8 %collective-permute-start.2 = (f32[33,16,128]{2,1,0:T(8,128)}, f32[33,16,128]{2,1,0:T(8,128)S(1)}, u32[]{:S(2)}, u32[]{:S(2)}) collective-permute-start(f32[33,16,128]{2,1,0:T(8,128)} %get-tuple-element.40), channel_id=1, source_target_pairs={{0,192},{1,193},{2,194},{3,195},{8,200},{9,201},{10,202},{11,203},... | collective-permute-start | bytes 811016 | tf_op jit(solution)/shard_map/ppermute | solution.py:478
  28.3 4.5 %collective-permute-start.4 = (f32[33,16,128]{2,1,0:T(8,128)}, f32[33,16,128]{2,1,0:T(8,128)S(1)}, u32[]{:S(2)}, u32[]{:S(2)}) collective-permute-start(f32[33,16,128]{2,1,0:T(8,128)} %get-tuple-element.42), channel_id=1, source_target_pairs={{0,68},{1,69},{2,70},{3,71},{8,76},{9,77},{10,78},{11,79},{16,84},... | collective-permute-start | bytes 811016 | tf_op jit(solution)/shard_map/ppermute | solution.py:478
  32.8 2.4 collective-permute-start.5
  35.1 4.0 %collective-permute-done.1.refs_2_ = f32[33,16,128]{2,1,0:T(8,128)S(1)} collective-permute-done((f32[33,16,128]{2,1,0:T(8,128)}, f32[33,16,128]{2,1,0:T(8,128)S(1)}, u32[]{:S(2)}, u32[]{:S(2)}) %collective-permute-start.1) | collective-permute-done | bytes 270368 | tf_op jit(solution)/shard_map/ppermute | solution.py:478
  39.2 6.9 %collective-permute-start.6 = (f32[33,16,128]{2,1,0:T(8,128)}, f32[33,16,128]{2,1,0:T(8,128)S(1)}, u32[]{:S(2)}, u32[]{:S(2)}) collective-permute-start(f32[33,16,128]{2,1,0:T(8,128)} %get-tuple-element.44), channel_id=1, source_target_pairs={{0,196},{1,197},{2,198},{3,199},{8,204},{9,205},{10,206},{11,207},... | collective-permute-start | bytes 811016 | tf_op jit(solution)/shard_map/ppermute | solution.py:478
  46.1 15.1 %collective-permute-done.2.refs_3_ = f32[33,16,128]{2,1,0:T(8,128)S(1)} collective-permute-done((f32[33,16,128]{2,1,0:T(8,128)}, f32[33,16,128]{2,1,0:T(8,128)S(1)}, u32[]{:S(2)}, u32[]{:S(2)}) %collective-permute-start.2) | collective-permute-done | bytes 270368 | tf_op jit(solution)/shard_map/ppermute | solution.py:478
  61.2 5.1 %collective-permute-done.3.refs_4_ = f32[33,16,128]{2,1,0:T(8,128)S(1)} collective-permute-done((f32[33,16,128]{2,1,0:T(8,128)}, f32[33,16,128]{2,1,0:T(8,128)S(1)}, u32[]{:S(2)}, u32[]{:S(2)}) %collective-permute-start.3) | collective-permute-done | bytes 270368 | tf_op jit(solution)/shard_map/ppermute | solution.py:478
  66.3 7.8 %collective-permute-done.5.refs_6_ = f32[33,16,128]{2,1,0:T(8,128)S(1)} collective-permute-done((f32[33,16,128]{2,1,0:T(8,128)}, f32[33,16,128]{2,1,0:T(8,128)S(1)}, u32[]{:S(2)}, u32[]{:S(2)}) %collective-permute-start.5) | collective-permute-done | bytes 270368 | tf_op jit(solution)/shard_map/ppermute | solution.py:478
  74.1 2.4 collective-permute-done.6.refs_7_
  77.5 2.6 shard_map.38
  82.8 8.5 %all-to-all-start = ((f32[32,136,128]{2,1,0:T(8,128)}), f32[32,136,128]{2,1,0:T(8,128)S(1)}, u32[]{:S(2)}, u32[]{:S(2)}) async-start(f32[32,136,128]{2,1,0:T(8,128)} %copy-done), calls=%async_computation | async-start | bytes 4456448 | tf_op jit(solution)/shard_map/all_to_all | solution.py:483
  94.5 3.4 %collective-permute-start.14 = (f32[32,16,128]{2,1,0:T(8,128)S(1)}, f32[32,16,128]{2,1,0:T(8,128)S(1)}, u32[]{:S(2)}, u32[]{:S(2)}) collective-permute-start(f32[32,16,128]{2,1,0:T(8,128)S(1)} %get-tuple-element.54), channel_id=1, source_target_pairs={{0,64},{1,65},{2,66},{3,67},{8,72},{9,73},{10,74},{11,75},{16,80},... | collective-permute-start | bytes 786440 | tf_op jit(solution)/shard_map/ppermute | solution.py:478
  99.0 4.5 %collective-permute-start.17 = (f32[32,16,128]{2,1,0:T(8,128)S(1)}, f32[32,16,128]{2,1,0:T(8,128)S(1)}, u32[]{:S(2)}, u32[]{:S(2)}) collective-permute-start(f32[32,16,128]{2,1,0:T(8,128)S(1)} %get-tuple-element.57), channel_id=1, source_target_pairs={{0,4},{1,5},{2,6},{3,7},{8,12},{9,13},{10,14},{11,15},{16,20},{17,... | collective-permute-start | bytes 786440 | tf_op jit(solution)/shard_map/ppermute | solution.py:478
  104.7 2.1 collective-permute-start.19
  106.8 9.5 %collective-permute-done.15.refs_2_ = f32[32,16,128]{2,1,0:T(8,128)S(1)} collective-permute-done((f32[32,16,128]{2,1,0:T(8,128)S(1)}, f32[32,16,128]{2,1,0:T(8,128)S(1)}, u32[]{:S(2)}, u32[]{:S(2)}) %collective-permute-start.15) | collective-permute-done | bytes 262176 | tf_op jit(solution)/shard_map/ppermute | solution.py:478
  116.3 9.8 %collective-permute-done.16.refs_3_ = f32[32,16,128]{2,1,0:T(8,128)S(1)} collective-permute-done((f32[32,16,128]{2,1,0:T(8,128)S(1)}, f32[32,16,128]{2,1,0:T(8,128)S(1)}, u32[]{:S(2)}, u32[]{:S(2)}) %collective-permute-start.16) | collective-permute-done | bytes 262176 | tf_op jit(solution)/shard_map/ppermute | solution.py:478
  126.1 14.0 %collective-permute-done.17.refs_4_ = f32[32,16,128]{2,1,0:T(8,128)S(1)} collective-permute-done((f32[32,16,128]{2,1,0:T(8,128)S(1)}, f32[32,16,128]{2,1,0:T(8,128)S(1)}, u32[]{:S(2)}, u32[]{:S(2)}) %collective-permute-start.17) | collective-permute-done | bytes 262176 | tf_op jit(solution)/shard_map/ppermute | solution.py:478
  140.8 4.0 %collective-permute-done.19.refs_6_ = f32[32,16,128]{2,1,0:T(8,128)S(1)} collective-permute-done((f32[32,16,128]{2,1,0:T(8,128)S(1)}, f32[32,16,128]{2,1,0:T(8,128)S(1)}, u32[]{:S(2)}, u32[]{:S(2)}) %collective-permute-start.19) | collective-permute-done | bytes 262176 | tf_op jit(solution)/shard_map/ppermute | solution.py:478
  145.5 4.8 %collective-permute-done.20.refs_7_ = f32[32,16,128]{2,1,0:T(8,128)S(1)} collective-permute-done((f32[32,16,128]{2,1,0:T(8,128)S(1)}, f32[32,16,128]{2,1,0:T(8,128)S(1)}, u32[]{:S(2)}, u32[]{:S(2)}) %collective-permute-start.20) | collective-permute-done | bytes 262176 | tf_op jit(solution)/shard_map/ppermute | solution.py:478
  153.9 7.3 %shard_map.44 = f32[32,128,128]{2,1,0:T(8,128)S(1)} custom-call(s32[2]{0:T(128)S(1)} %copy-done.11, f32[32,136,128]{2,1,0:T(8,128)S(1)} %all-to-all-done.x_ref.fitness_ref, f32[32,16,128]{2,1,0:T(8,128)S(1)} %get-tuple-element.53.refs_0_, f32[32,16,128]{2,1,0:T(8,128)S(1)} %collective-permute-done.14.refs_1_, ...), custom_call_target="tpu_custom_call" | custom-call | flops 268435456 | bytes 8388608 | tf_op jit(solution)/shard_map/pallas_call | solution.py:458
  162.6 7.7 %all-to-all-start.3 = ((f32[32,128,128]{2,1,0:T(8,128)}), f32[32,128,128]{2,1,0:T(8,128)}, u32[]{:S(2)}, u32[]{:S(2)}) async-start(f32[32,128,128]{2,1,0:T(8,128)} %copy-done.1), calls=%async_computation.3 | async-start | bytes 4194304 | tf_op jit(solution)/shard_map/all_to_all | solution.py:483
  170.3 6.7 %shard_map.39 = (f32[32,16,128]{2,1,0:T(8,128)S(1)}, f32[32,16,128]{2,1,0:T(8,128)S(1)}, f32[32,16,128]{2,1,0:T(8,128)S(1)}, f32[32,16,128]{2,1,0:T(8,128)S(1)},...) custom-call(s32[2]{0:T(128)S(1)} %copy-done.11, ...), custom_call_target="tpu_custom_call" | custom-call | flops 268435456 | bytes 8388608 | tf_op jit(solution)/shard_map/pallas_call | solution.py:458
  178.9 3.3 %collective-permute-start.9 = (f32[32,16,128]{2,1,0:T(8,128)S(1)}, f32[32,16,128]{2,1,0:T(8,128)S(1)}, u32[]{:S(2)}, u32[]{:S(2)}) collective-permute-start(f32[32,16,128]{2,1,0:T(8,128)S(1)} %get-tuple-element.48), channel_id=1, source_target_pairs={{0,192},{1,193},{2,194},{3,195},{8,200},{9,201},{10,202},{11,203},... | collective-permute-start | bytes 786440 | tf_op jit(solution)/shard_map/ppermute | solution.py:478
  183.1 4.1 %collective-permute-start.11 = (f32[32,16,128]{2,1,0:T(8,128)S(1)}, f32[32,16,128]{2,1,0:T(8,128)S(1)}, u32[]{:S(2)}, u32[]{:S(2)}) collective-permute-start(f32[32,16,128]{2,1,0:T(8,128)S(1)} %get-tuple-element.50), channel_id=1, source_target_pairs={{0,68},{1,69},{2,70},{3,71},{8,76},{9,77},{10,78},{11,79},{16,84},... | collective-permute-start | bytes 786440 | tf_op jit(solution)/shard_map/ppermute | solution.py:478
  187.2 2.7 collective-permute-start.12
  189.9 8.8 %collective-permute-done.8.refs_2_ = f32[32,16,128]{2,1,0:T(8,128)S(1)} collective-permute-done((f32[32,16,128]{2,1,0:T(8,128)S(1)}, f32[32,16,128]{2,1,0:T(8,128)S(1)}, u32[]{:S(2)}, u32[]{:S(2)}) %collective-permute-start.8) | collective-permute-done | bytes 262176 | tf_op jit(solution)/shard_map/ppermute | solution.py:478
  198.7 15.0 %collective-permute-done.9.refs_3_ = f32[32,16,128]{2,1,0:T(8,128)S(1)} collective-permute-done((f32[32,16,128]{2,1,0:T(8,128)S(1)}, f32[32,16,128]{2,1,0:T(8,128)S(1)}, u32[]{:S(2)}, u32[]{:S(2)}) %collective-permute-start.9) | collective-permute-done | bytes 262176 | tf_op jit(solution)/shard_map/ppermute | solution.py:478
  213.6 10.1 %collective-permute-done.10.refs_4_ = f32[32,16,128]{2,1,0:T(8,128)S(1)} collective-permute-done((f32[32,16,128]{2,1,0:T(8,128)S(1)}, f32[32,16,128]{2,1,0:T(8,128)S(1)}, u32[]{:S(2)}, u32[]{:S(2)}) %collective-permute-start.10) | collective-permute-done | bytes 262176 | tf_op jit(solution)/shard_map/ppermute | solution.py:478
  223.7 3.7 %collective-permute-done.12.refs_6_ = f32[32,16,128]{2,1,0:T(8,128)S(1)} collective-permute-done((f32[32,16,128]{2,1,0:T(8,128)S(1)}, f32[32,16,128]{2,1,0:T(8,128)S(1)}, u32[]{:S(2)}, u32[]{:S(2)}) %collective-permute-start.12) | collective-permute-done | bytes 262176 | tf_op jit(solution)/shard_map/ppermute | solution.py:478
  227.4 2.2 collective-permute-done.13.refs_7_
  229.6 2.7 shard_map.40
  232.4 8.6 %all-to-all-start.1 = ((f32[32,128,128]{2,1,0:T(8,128)}), f32[32,128,128]{2,1,0:T(8,128)S(1)}, u32[]{:S(2)}, u32[]{:S(2)}) async-start(f32[32,128,128]{2,1,0:T(8,128)} %shard_map.40), calls=%async_computation.1 | async-start | bytes 4194304 | tf_op jit(solution)/shard_map/all_to_all | solution.py:483
  241.0 3.5 %shard_map.45 = (f32[32,16,128]{2,1,0:T(8,128)S(1)}, f32[32,16,128]{2,1,0:T(8,128)S(1)}, f32[32,16,128]{2,1,0:T(8,128)S(1)}, f32[32,16,128]{2,1,0:T(8,128)}, f32...) custom-call(s32[2]{0:T(128)S(1)} %copy-done.11, ...), custom_call_target="tpu_custom_call" | custom-call | flops 268435456 | bytes 8388608 | tf_op jit(solution)/shard_map/pallas_call | solution.py:458
  244.5 3.2 %collective-permute-start.21 = (f32[32,16,128]{2,1,0:T(8,128)S(1)}, f32[32,16,128]{2,1,0:T(8,128)S(1)}, u32[]{:S(2)}, u32[]{:S(2)}) collective-permute-start(f32[32,16,128]{2,1,0:T(8,128)S(1)} %get-tuple-element.62), channel_id=1, source_target_pairs={{0,64},{1,65},{2,66},{3,67},{8,72},{9,73},{10,74},{11,75},{16,80},... | collective-permute-start | bytes 786440 | tf_op jit(solution)/shard_map/ppermute | solution.py:478
  249.0 4.4 %collective-permute-start.24 = (f32[32,16,128]{2,1,0:T(8,128)}, f32[32,16,128]{2,1,0:T(8,128)S(1)}, u32[]{:S(2)}, u32[]{:S(2)}) collective-permute-start(f32[32,16,128]{2,1,0:T(8,128)} %get-tuple-element.65), channel_id=1, source_target_pairs={{0,4},{1,5},{2,6},{3,7},{8,12},{9,13},{10,14},{11,15},{16,20},{17,... | collective-permute-start | bytes 786440 | tf_op jit(solution)/shard_map/ppermute | solution.py:478
  254.7 2.1 collective-permute-start.26
  256.8 9.6 %collective-permute-done.22.refs_2_ = f32[32,16,128]{2,1,0:T(8,128)S(1)} collective-permute-done((f32[32,16,128]{2,1,0:T(8,128)S(1)}, f32[32,16,128]{2,1,0:T(8,128)S(1)}, u32[]{:S(2)}, u32[]{:S(2)}) %collective-permute-start.22) | collective-permute-done | bytes 262176 | tf_op jit(solution)/shard_map/ppermute | solution.py:478
  268.0 1.8 shard_map.41.other_ref
  269.9 6.3 %collective-permute-done.23.refs_3_ = f32[32,16,128]{2,1,0:T(8,128)S(1)} collective-permute-done((f32[32,16,128]{2,1,0:T(8,128)}, f32[32,16,128]{2,1,0:T(8,128)S(1)}, u32[]{:S(2)}, u32[]{:S(2)}) %collective-permute-start.23) | collective-permute-done | bytes 262176 | tf_op jit(solution)/shard_map/ppermute | solution.py:478
  276.2 13.8 %collective-permute-done.24.refs_4_ = f32[32,16,128]{2,1,0:T(8,128)S(1)} collective-permute-done((f32[32,16,128]{2,1,0:T(8,128)}, f32[32,16,128]{2,1,0:T(8,128)S(1)}, u32[]{:S(2)}, u32[]{:S(2)}) %collective-permute-start.24) | collective-permute-done | bytes 262176 | tf_op jit(solution)/shard_map/ppermute | solution.py:478
  290.0 5.1 %collective-permute-done.26.refs_6_ = f32[32,16,128]{2,1,0:T(8,128)} collective-permute-done((f32[32,16,128]{2,1,0:T(8,128)}, f32[32,16,128]{2,1,0:T(8,128)}, u32[]{:S(2)}, u32[]{:S(2)}) %collective-permute-start.26) | collective-permute-done | bytes 262176 | tf_op jit(solution)/shard_map/ppermute | solution.py:478
  295.2 5.4 %collective-permute-done.27.refs_7_ = f32[32,16,128]{2,1,0:T(8,128)} collective-permute-done((f32[32,16,128]{2,1,0:T(8,128)}, f32[32,16,128]{2,1,0:T(8,128)}, u32[]{:S(2)}, u32[]{:S(2)}) %collective-permute-start.27) | collective-permute-done | bytes 262176 | tf_op jit(solution)/shard_map/ppermute | solution.py:478
  300.6 4.1 %shard_map.46 = f32[8,1024,128]{2,1,0:T(8,128)} custom-call(s32[2]{0:T(128)S(1)} %copy-done.11, f32[8,32,16,128]{3,2,1,0:T(8,128)S(1)} %shard_map.41.other_ref, f32[32,16,128]{2,1,0:T(8,128)S(1)} %get-tuple-element.61.refs_0_, f32[32,16,128]{2,1,0:T(8,128)S(1)} %collective-permute-done.21.refs_1_, f32[32,16,128]{2,1,0:T(8,128)S(1)} %collective-permute-done.22.refs_2_, ...), custom_call_target="tpu_custom_call" | custom-call | flops 268435456 | bytes 8388608 | tf_op jit(solution)/shard_map/pallas_call | solution.py:458
  (50 shorter events, 22.9 us)
Async XLA Ops:
  5.2 76.3 %all-to-all-start.2 = ((f32[32,128,128]{2,1,0:T(8,128)}), f32[32,128,128]{2,1,0:T(8,128)S(1)}, u32[]{:S(2)}, u32[]{:S(2)}) async-start(f32[32,128,128]{2,1,0:T(8,128)} %shard_map.42), calls=%async_computation.2 | async-start | bytes 4194304 | tf_op jit(solution)/shard_map/all_to_all | solution.py:483
  13.8 62.8 %copy-start.11 = (s32[2]{0:T(128)S(1)}, s32[2]{0:T(128)}, u32[]{:S(2)}) copy-start(s32[2]{0:T(128)} %rate_ref.19) | copy-start | bytes 28
  19.4 13.4 %collective-permute-start = (f32[33,16,128]{2,1,0:T(8,128)}, f32[33,16,128]{2,1,0:T(8,128)S(1)}, u32[]{:S(2)}, u32[]{:S(2)}) collective-permute-start(f32[33,16,128]{2,1,0:T(8,128)} %get-tuple-element.38), channel_id=1, source_target_pairs={{0,64},{1,65},{2,66},{3,67},{8,72},{9,73},{10,74},{11,75},{16,80},... | collective-permute-start | bytes 811016 | tf_op jit(solution)/shard_map/ppermute | solution.py:478
  21.1 18.1 %collective-permute-start.1 = (f32[33,16,128]{2,1,0:T(8,128)}, f32[33,16,128]{2,1,0:T(8,128)S(1)}, u32[]{:S(2)}, u32[]{:S(2)}) collective-permute-start(f32[33,16,128]{2,1,0:T(8,128)} %get-tuple-element.39), channel_id=1, source_target_pairs={{0,128},{1,129},{2,130},{3,131},{8,136},{9,137},{10,138},{11,139},... | collective-permute-start | bytes 811016 | tf_op jit(solution)/shard_map/ppermute | solution.py:478
  24.1 37.1 %collective-permute-start.2 = (f32[33,16,128]{2,1,0:T(8,128)}, f32[33,16,128]{2,1,0:T(8,128)S(1)}, u32[]{:S(2)}, u32[]{:S(2)}) collective-permute-start(f32[33,16,128]{2,1,0:T(8,128)} %get-tuple-element.40), channel_id=1, source_target_pairs={{0,192},{1,193},{2,194},{3,195},{8,200},{9,201},{10,202},{11,203},... | collective-permute-start | bytes 811016 | tf_op jit(solution)/shard_map/ppermute | solution.py:478
  27.8 38.5 %collective-permute-start.3 = (f32[33,16,128]{2,1,0:T(8,128)}, f32[33,16,128]{2,1,0:T(8,128)S(1)}, u32[]{:S(2)}, u32[]{:S(2)}) collective-permute-start(f32[33,16,128]{2,1,0:T(8,128)} %get-tuple-element.41), channel_id=1, source_target_pairs={{0,4},{1,5},{2,6},{3,7},{8,12},{9,13},{10,14},{11,15},{16,20},{17,... | collective-permute-start | bytes 811016 | tf_op jit(solution)/shard_map/ppermute | solution.py:478
  28.3 38.0 %collective-permute-start.4 = (f32[33,16,128]{2,1,0:T(8,128)}, f32[33,16,128]{2,1,0:T(8,128)S(1)}, u32[]{:S(2)}, u32[]{:S(2)}) collective-permute-start(f32[33,16,128]{2,1,0:T(8,128)} %get-tuple-element.42), channel_id=1, source_target_pairs={{0,68},{1,69},{2,70},{3,71},{8,76},{9,77},{10,78},{11,79},{16,84},... | collective-permute-start | bytes 811016 | tf_op jit(solution)/shard_map/ppermute | solution.py:478
  32.8 41.4 %collective-permute-start.5 = (f32[33,16,128]{2,1,0:T(8,128)}, f32[33,16,128]{2,1,0:T(8,128)S(1)}, u32[]{:S(2)}, u32[]{:S(2)}) collective-permute-start(f32[33,16,128]{2,1,0:T(8,128)} %get-tuple-element.43), channel_id=1, source_target_pairs={{0,132},{1,133},{2,134},{3,135},{8,140},{9,141},{10,142},{11,143},... | collective-permute-start | bytes 811016 | tf_op jit(solution)/shard_map/ppermute | solution.py:478
  39.2 37.4 %collective-permute-start.6 = (f32[33,16,128]{2,1,0:T(8,128)}, f32[33,16,128]{2,1,0:T(8,128)S(1)}, u32[]{:S(2)}, u32[]{:S(2)}) collective-permute-start(f32[33,16,128]{2,1,0:T(8,128)} %get-tuple-element.44), channel_id=1, source_target_pairs={{0,196},{1,197},{2,198},{3,199},{8,204},{9,205},{10,206},{11,207},... | collective-permute-start | bytes 811016 | tf_op jit(solution)/shard_map/ppermute | solution.py:478
  76.6 1.0 copy-start.4
  80.1 1.4 copy-start
  81.5 1.3 copy-start.2
  82.8 68.2 %all-to-all-start = ((f32[32,136,128]{2,1,0:T(8,128)}), f32[32,136,128]{2,1,0:T(8,128)S(1)}, u32[]{:S(2)}, u32[]{:S(2)}) async-start(f32[32,136,128]{2,1,0:T(8,128)} %copy-done), calls=%async_computation | async-start | bytes 4456448 | tf_op jit(solution)/shard_map/all_to_all | solution.py:483
  91.3 1.6 copy-start.3
  94.5 10.2 %collective-permute-start.14 = (f32[32,16,128]{2,1,0:T(8,128)S(1)}, f32[32,16,128]{2,1,0:T(8,128)S(1)}, u32[]{:S(2)}, u32[]{:S(2)}) collective-permute-start(f32[32,16,128]{2,1,0:T(8,128)S(1)} %get-tuple-element.54), channel_id=1, source_target_pairs={{0,64},{1,65},{2,66},{3,67},{8,72},{9,73},{10,74},{11,75},{16,80},... | collective-permute-start | bytes 786440 | tf_op jit(solution)/shard_map/ppermute | solution.py:478
  97.9 18.4 %collective-permute-start.15 = (f32[32,16,128]{2,1,0:T(8,128)S(1)}, f32[32,16,128]{2,1,0:T(8,128)S(1)}, u32[]{:S(2)}, u32[]{:S(2)}) collective-permute-start(f32[32,16,128]{2,1,0:T(8,128)S(1)} %get-tuple-element.55), channel_id=1, source_target_pairs={{0,128},{1,129},{2,130},{3,131},{8,136},{9,137},{10,138},{11,139},... | collective-permute-start | bytes 786440 | tf_op jit(solution)/shard_map/ppermute | solution.py:478
  98.7 27.4 %collective-permute-start.16 = (f32[32,16,128]{2,1,0:T(8,128)S(1)}, f32[32,16,128]{2,1,0:T(8,128)S(1)}, u32[]{:S(2)}, u32[]{:S(2)}) collective-permute-start(f32[32,16,128]{2,1,0:T(8,128)S(1)} %get-tuple-element.56), channel_id=1, source_target_pairs={{0,192},{1,193},{2,194},{3,195},{8,200},{9,201},{10,202},{11,203},... | collective-permute-start | bytes 786440 | tf_op jit(solution)/shard_map/ppermute | solution.py:478
  99.0 41.1 %collective-permute-start.17 = (f32[32,16,128]{2,1,0:T(8,128)S(1)}, f32[32,16,128]{2,1,0:T(8,128)S(1)}, u32[]{:S(2)}, u32[]{:S(2)}) collective-permute-start(f32[32,16,128]{2,1,0:T(8,128)S(1)} %get-tuple-element.57), channel_id=1, source_target_pairs={{0,4},{1,5},{2,6},{3,7},{8,12},{9,13},{10,14},{11,15},{16,20},{17,... | collective-permute-start | bytes 786440 | tf_op jit(solution)/shard_map/ppermute | solution.py:478
  103.5 36.6 %collective-permute-start.18 = (f32[32,16,128]{2,1,0:T(8,128)S(1)}, f32[32,16,128]{2,1,0:T(8,128)S(1)}, u32[]{:S(2)}, u32[]{:S(2)}) collective-permute-start(f32[32,16,128]{2,1,0:T(8,128)S(1)} %get-tuple-element.58), channel_id=1, source_target_pairs={{0,68},{1,69},{2,70},{3,71},{8,76},{9,77},{10,78},{11,79},{16,84},... | collective-permute-start | bytes 786440 | tf_op jit(solution)/shard_map/ppermute | solution.py:478
  104.7 40.1 %collective-permute-start.19 = (f32[32,16,128]{2,1,0:T(8,128)S(1)}, f32[32,16,128]{2,1,0:T(8,128)S(1)}, u32[]{:S(2)}, u32[]{:S(2)}) collective-permute-start(f32[32,16,128]{2,1,0:T(8,128)S(1)} %get-tuple-element.59), channel_id=1, source_target_pairs={{0,132},{1,133},{2,134},{3,135},{8,140},{9,141},{10,142},{11,143},... | collective-permute-start | bytes 786440 | tf_op jit(solution)/shard_map/ppermute | solution.py:478
  116.3 34.1 %collective-permute-start.20 = (f32[32,16,128]{2,1,0:T(8,128)S(1)}, f32[32,16,128]{2,1,0:T(8,128)S(1)}, u32[]{:S(2)}, u32[]{:S(2)}) collective-permute-start(f32[32,16,128]{2,1,0:T(8,128)S(1)} %get-tuple-element.60), channel_id=1, source_target_pairs={{0,196},{1,197},{2,198},{3,199},{8,204},{9,205},{10,206},{11,207},... | collective-permute-start | bytes 786440 | tf_op jit(solution)/shard_map/ppermute | solution.py:478
  140.1 0.7 copy-start.5
  144.8 0.7 copy-start.7
  150.4 0.7 copy-start.9
  151.1 1.0 copy-start.6
  152.0 0.9 copy-start.8
  153.0 0.9 copy-start.10
  161.2 1.3 copy-start.1
  162.6 69.8 %all-to-all-start.3 = ((f32[32,128,128]{2,1,0:T(8,128)}), f32[32,128,128]{2,1,0:T(8,128)}, u32[]{:S(2)}, u32[]{:S(2)}) async-start(f32[32,128,128]{2,1,0:T(8,128)} %copy-done.1), calls=%async_computation.3 | async-start | bytes 4194304 | tf_op jit(solution)/shard_map/all_to_all | solution.py:483
  177.0 10.2 %collective-permute-start.7 = (f32[32,16,128]{2,1,0:T(8,128)S(1)}, f32[32,16,128]{2,1,0:T(8,128)S(1)}, u32[]{:S(2)}, u32[]{:S(2)}) collective-permute-start(f32[32,16,128]{2,1,0:T(8,128)S(1)} %get-tuple-element.46), channel_id=1, source_target_pairs={{0,64},{1,65},{2,66},{3,67},{8,72},{9,73},{10,74},{11,75},{16,80},... | collective-permute-start | bytes 786440 | tf_op jit(solution)/shard_map/ppermute | solution.py:478
  177.4 21.3 %collective-permute-start.8 = (f32[32,16,128]{2,1,0:T(8,128)S(1)}, f32[32,16,128]{2,1,0:T(8,128)S(1)}, u32[]{:S(2)}, u32[]{:S(2)}) collective-permute-start(f32[32,16,128]{2,1,0:T(8,128)S(1)} %get-tuple-element.47), channel_id=1, source_target_pairs={{0,128},{1,129},{2,130},{3,131},{8,136},{9,137},{10,138},{11,139},... | collective-permute-start | bytes 786440 | tf_op jit(solution)/shard_map/ppermute | solution.py:478
  178.9 34.8 %collective-permute-start.9 = (f32[32,16,128]{2,1,0:T(8,128)S(1)}, f32[32,16,128]{2,1,0:T(8,128)S(1)}, u32[]{:S(2)}, u32[]{:S(2)}) collective-permute-start(f32[32,16,128]{2,1,0:T(8,128)S(1)} %get-tuple-element.48), channel_id=1, source_target_pairs={{0,192},{1,193},{2,194},{3,195},{8,200},{9,201},{10,202},{11,203},... | collective-permute-start | bytes 786440 | tf_op jit(solution)/shard_map/ppermute | solution.py:478
  182.2 41.5 %collective-permute-start.10 = (f32[32,16,128]{2,1,0:T(8,128)S(1)}, f32[32,16,128]{2,1,0:T(8,128)S(1)}, u32[]{:S(2)}, u32[]{:S(2)}) collective-permute-start(f32[32,16,128]{2,1,0:T(8,128)S(1)} %get-tuple-element.49), channel_id=1, source_target_pairs={{0,4},{1,5},{2,6},{3,7},{8,12},{9,13},{10,14},{11,15},{16,20},{17,... | collective-permute-start | bytes 786440 | tf_op jit(solution)/shard_map/ppermute | solution.py:478
  183.1 40.7 %collective-permute-start.11 = (f32[32,16,128]{2,1,0:T(8,128)S(1)}, f32[32,16,128]{2,1,0:T(8,128)S(1)}, u32[]{:S(2)}, u32[]{:S(2)}) collective-permute-start(f32[32,16,128]{2,1,0:T(8,128)S(1)} %get-tuple-element.50), channel_id=1, source_target_pairs={{0,68},{1,69},{2,70},{3,71},{8,76},{9,77},{10,78},{11,79},{16,84},... | collective-permute-start | bytes 786440 | tf_op jit(solution)/shard_map/ppermute | solution.py:478
  187.2 40.2 %collective-permute-start.12 = (f32[32,16,128]{2,1,0:T(8,128)S(1)}, f32[32,16,128]{2,1,0:T(8,128)S(1)}, u32[]{:S(2)}, u32[]{:S(2)}) collective-permute-start(f32[32,16,128]{2,1,0:T(8,128)S(1)} %get-tuple-element.51), channel_id=1, source_target_pairs={{0,132},{1,133},{2,134},{3,135},{8,140},{9,141},{10,142},{11,143},... | collective-permute-start | bytes 786440 | tf_op jit(solution)/shard_map/ppermute | solution.py:478
  198.6 31.0 %collective-permute-start.13 = (f32[32,16,128]{2,1,0:T(8,128)S(1)}, f32[32,16,128]{2,1,0:T(8,128)S(1)}, u32[]{:S(2)}, u32[]{:S(2)}) collective-permute-start(f32[32,16,128]{2,1,0:T(8,128)S(1)} %get-tuple-element.52), channel_id=1, source_target_pairs={{0,196},{1,197},{2,198},{3,199},{8,204},{9,205},{10,206},{11,207},... | collective-permute-start | bytes 786440 | tf_op jit(solution)/shard_map/ppermute | solution.py:478
  232.4 35.6 %all-to-all-start.1 = ((f32[32,128,128]{2,1,0:T(8,128)}), f32[32,128,128]{2,1,0:T(8,128)S(1)}, u32[]{:S(2)}, u32[]{:S(2)}) async-start(f32[32,128,128]{2,1,0:T(8,128)} %shard_map.40), calls=%async_computation.1 | async-start | bytes 4194304 | tf_op jit(solution)/shard_map/all_to_all | solution.py:483
  244.5 10.2 %collective-permute-start.21 = (f32[32,16,128]{2,1,0:T(8,128)S(1)}, f32[32,16,128]{2,1,0:T(8,128)S(1)}, u32[]{:S(2)}, u32[]{:S(2)}) collective-permute-start(f32[32,16,128]{2,1,0:T(8,128)S(1)} %get-tuple-element.62), channel_id=1, source_target_pairs={{0,64},{1,65},{2,66},{3,67},{8,72},{9,73},{10,74},{11,75},{16,80},... | collective-permute-start | bytes 786440 | tf_op jit(solution)/shard_map/ppermute | solution.py:478
  247.7 18.6 %collective-permute-start.22 = (f32[32,16,128]{2,1,0:T(8,128)S(1)}, f32[32,16,128]{2,1,0:T(8,128)S(1)}, u32[]{:S(2)}, u32[]{:S(2)}) collective-permute-start(f32[32,16,128]{2,1,0:T(8,128)S(1)} %get-tuple-element.63), channel_id=1, source_target_pairs={{0,128},{1,129},{2,130},{3,131},{8,136},{9,137},{10,138},{11,139},... | collective-permute-start | bytes 786440 | tf_op jit(solution)/shard_map/ppermute | solution.py:478
  248.6 27.6 %collective-permute-start.23 = (f32[32,16,128]{2,1,0:T(8,128)}, f32[32,16,128]{2,1,0:T(8,128)S(1)}, u32[]{:S(2)}, u32[]{:S(2)}) collective-permute-start(f32[32,16,128]{2,1,0:T(8,128)} %get-tuple-element.64), channel_id=1, source_target_pairs={{0,192},{1,193},{2,194},{3,195},{8,200},{9,201},{10,202},{11,203},... | collective-permute-start | bytes 786440 | tf_op jit(solution)/shard_map/ppermute | solution.py:478
  249.0 41.0 %collective-permute-start.24 = (f32[32,16,128]{2,1,0:T(8,128)}, f32[32,16,128]{2,1,0:T(8,128)S(1)}, u32[]{:S(2)}, u32[]{:S(2)}) collective-permute-start(f32[32,16,128]{2,1,0:T(8,128)} %get-tuple-element.65), channel_id=1, source_target_pairs={{0,4},{1,5},{2,6},{3,7},{8,12},{9,13},{10,14},{11,15},{16,20},{17,... | collective-permute-start | bytes 786440 | tf_op jit(solution)/shard_map/ppermute | solution.py:478
  253.4 36.6 %collective-permute-start.25 = (f32[32,16,128]{2,1,0:T(8,128)}, f32[32,16,128]{2,1,0:T(8,128)}, u32[]{:S(2)}, u32[]{:S(2)}) collective-permute-start(f32[32,16,128]{2,1,0:T(8,128)} %get-tuple-element.66), channel_id=1, source_target_pairs={{0,68},{1,69},{2,70},{3,71},{8,76},{9,77},{10,78},{11,79},{16,84},... | collective-permute-start | bytes 786440 | tf_op jit(solution)/shard_map/ppermute | solution.py:478
  254.7 40.5 %collective-permute-start.26 = (f32[32,16,128]{2,1,0:T(8,128)}, f32[32,16,128]{2,1,0:T(8,128)}, u32[]{:S(2)}, u32[]{:S(2)}) collective-permute-start(f32[32,16,128]{2,1,0:T(8,128)} %get-tuple-element.67), channel_id=1, source_target_pairs={{0,132},{1,133},{2,134},{3,135},{8,140},{9,141},{10,142},{11,143},... | collective-permute-start | bytes 786440 | tf_op jit(solution)/shard_map/ppermute | solution.py:478
  266.3 34.3 %collective-permute-start.27 = (f32[32,16,128]{2,1,0:T(8,128)}, f32[32,16,128]{2,1,0:T(8,128)}, u32[]{:S(2)}, u32[]{:S(2)}) collective-permute-start(f32[32,16,128]{2,1,0:T(8,128)} %get-tuple-element.68), channel_id=1, source_target_pairs={{0,196},{1,197},{2,198},{3,199},{8,204},{9,205},{10,206},{11,207},... | collective-permute-start | bytes 786440 | tf_op jit(solution)/shard_map/ppermute | solution.py:478

commit v3 on v2

--- a/solution.py
+++ b/solution.py
@@ -110,14 +110,27 @@
     )
 
 
-def mix_ring(held, chance):
-    @pl.loop(0, PLANE, unroll=2)
-    def _(plane):
-        for half in range(2):
-            rows = pl.ds(8 * half, 8)
-            mixed = mix_bits([held[ring, plane, rows, :] for ring in range(RING)], chance)
-            for ring in range(RING):
-                held[ring, plane, rows, :] = mixed[ring]
+PARTS = 4
+PART = PLANE // PARTS
+
+
+def mix_ring(held, chance, sends=None):
+    @pl.loop(0, PARTS)
+    def _(part):
+        for at in range(PART):
+            for half in range(2):
+                plane, rows = PART * part + at, pl.ds(8 * half, 8)
+                mixed = mix_bits([held[ring, plane, rows, :] for ring in range(RING)], chance)
+                for ring in range(RING):
+                    held[ring, plane, rows, :] = mixed[ring]
+        if sends:
+            start_all(sends(part))
+
+    if sends:
+
+        @pl.loop(0, PARTS)
+        def _(part):
+            wait_all(sends(part))
 
 
 def mix_plane(held, ring, chance):
@@ -147,10 +160,28 @@
 
 
 def to_ring(held, refs, sems):
-    def copies():
+    def copies(part):
+        planes = pl.ds(PART * part, PART)
         return [
-            pltpu.make_async_copy(held.at[ring_slot(shift)], ref, sems.at[shift])
+            pltpu.make_async_copy(
+                held.at[ring_slot(shift), planes], ref.at[planes], sems.at[shift, part]
+            )
             for shift, ref in enumerate(refs)
+        ]
+
+    return copies
+
+
+def to_plane(held, ref, sems):
+    def copies(part):
+        planes = pl.ds(PART * part, PART)
+        return [
+            pltpu.make_async_copy(
+                held.at[ring, planes],
+                ref.at[planes, pl.ds(REST * ring, REST), :],
+                sems.at[ring, part],
+            )
+            for ring in range(RING)
         ]
 
     return copies
@@ -286,7 +317,7 @@
     rows_copy.wait()
 
 
-TOGETHER = 2
+TOGETHER = 4
 
 
 def apply_middle(held, rows_held, first_ring, chance, left_ref, right_ref):
@@ -322,10 +353,7 @@
             plane_copy(x_ref, held, ring + at, in_sems).wait()
         apply_middle(held, rows_held, ring, chance, left, right)
 
-    mix_ring(held, pick(chance, RING_AWAY))
-    copies = to_ring(held, outs, out_sems)()
-    start_all(copies)
-    wait_all(copies)
+    mix_ring(held, pick(chance, RING_AWAY), to_ring(held, outs, out_sems))
 
 
 def ring_to_plane(rate_ref, *refs):
@@ -334,10 +362,7 @@
     copies = from_ring(parts, held, in_sems)()
     start_all(copies)
     wait_all(copies)
-    mix_ring(held, pick(chance, RING_HERE))
-    copies = [plane_copy(out_ref, held, ring, out_sems, outward=True) for ring in range(RING)]
-    start_all(copies)
-    wait_all(copies)
+    mix_ring(held, pick(chance, RING_HERE), to_plane(held, out_ref, out_sems))
 
 
 def end_plane(rate_ref, x_ref, out_ref, held, in_sems, out_sems):
@@ -356,28 +381,31 @@
     wait_all([send(ring) for ring in range(RING)])
 
 
-def plane_to_ring(plane_sites, ring_sites):
-    def kernel(rate_ref, x_ref, *refs):
-        outs, (held, in_sems, out_sems) = refs[:RING], refs[RING:]
-        chance = chances(rate_ref, 1)
-        start_all([plane_copy(x_ref, held, ring, in_sems) for ring in range(RING)])
-
-        if plane_sites:
-
-            @pl.loop(0, RING)
-            def _(ring):
-                plane_copy(x_ref, held, ring, in_sems).wait()
-                mix_plane(held, ring, pick(chance, plane_sites))
-
-        else:
-            wait_all([plane_copy(x_ref, held, ring, in_sems) for ring in range(RING)])
-        if ring_sites:
-            mix_ring(held, pick(chance, ring_sites))
-        copies = to_ring(held, outs, out_sems)()
-        start_all(copies)
-        wait_all(copies)
-
-    return kernel
+def plane_to_ring_first(rate_ref, x_ref, *refs):
+    outs, (held, in_sems, out_sems) = refs[:RING], refs[RING:]
+    chance = chances(rate_ref, 1)
+    copies = [plane_copy(x_ref, held, ring, in_sems) for ring in range(RING)]
+    start_all(copies)
+    wait_all(copies)
+    mix_ring(held, pick(chance, RING_HERE), to_ring(held, outs, out_sems))
+
+
+def plane_to_ring(rate_ref, x_ref, *refs):
+    outs, (held, in_sems, out_sems) = refs[:RING], refs[RING:]
+    chance = chances(rate_ref, 1)
+    start_all([plane_copy(x_ref, held, ring, in_sems) for ring in range(RING)])
+
+    def send(shift):
+        return pltpu.make_async_copy(
+            held.at[ring_slot(shift)], outs[shift], out_sems.at[shift, 0]
+        )
+
+    for shift in (3, 5, 2, 6, 1, 4, 7, 0):
+        ring = ring_slot(shift)
+        plane_copy(x_ref, held, ring, in_sems).wait()
+        mix_plane(held, ring, pick(chance, PLANE_HERE))
+        send(shift).start()
+    wait_all([send(shift) for shift in range(RING)])
 
 
 def middle_plane(rate_ref, fitness_ref, *refs):
@@ -397,10 +425,7 @@
     def _(ring):
         apply_middle(held, rows_held, ring, chance, left, right)
 
-    mix_ring(held, pick(chance, RING_AWAY))
-    copies = [plane_copy(out_ref, held, ring, out_sems, outward=True) for ring in range(RING)]
-    start_all(copies)
-    wait_all(copies)
+    mix_ring(held, pick(chance, RING_AWAY), to_plane(held, out_ref, out_sems))
 
 
 def end_ring(rate_ref, other_ref, *refs):
@@ -453,11 +478,15 @@
 SENT_PLANE_MORE = jax.ShapeDtypeStruct((PLANE, RING * REST + RING, 128), F32)
 
 
+def far(shape):
+    return pltpu.HBM(shape.shape, shape.dtype)
+
+
 def call(kernel, name, outs, scratch, rate_index, *operands):
     many = isinstance(outs, list)
     return pl.pallas_call(
         kernel,
-        out_shape=outs,
+        out_shape=[far(out) for out in outs] if many else outs if name == "a5" else far(outs),
         in_specs=[SMEM] + [ANY] * len(operands),
         out_specs=[ANY] * len(outs) if many else ANY,
         scratch_shapes=scratch,
@@ -468,12 +497,9 @@
     )(rate_index, *operands)
 
 
-SOONER = (3, 5)
-
-
-def round_ring(parts):
+def round_ring(parts, sooner=(3, 5)):
     moved = list(parts)
-    for shifts in (SOONER, [shift for shift in range(1, RING) if shift not in SOONER]):
+    for shifts in (sooner, [shift for shift in range(1, RING) if shift not in sooner]):
         for shift in shifts:
             moved[shift] = lax.ppermute(parts[shift], AXES, ring_pairs(shift))
     return moved
@@ -491,23 +517,24 @@
     rate = rate_index
     begin = [WHOLE, CLASSES]
     ends = [EIGHT, EIGHT]
+    fine = [EIGHT, MANY]
 
     a = call(begin_ring, "a1", SENT_RING_MORE, begin + [HELD_MORE, CLASS_ROWS, EIGHT, MANY, ONE, EIGHT], rate, classes, rows)
     a = round_ring(a)
     b = call(begin_plane, "b1", SENT_PLANE, begin + [HELD] + ends + [ONE], rate, classes, rows)
     b = in_plane(b)
-    b = call(plane_to_ring([], RING_HERE), "b2", SENT_RING, [HELD] + ends, rate, b)
+    b = call(plane_to_ring_first, "b2", SENT_RING, [HELD] + fine, rate, b)
     b = round_ring(b)
     a = call(ring_to_plane_first, "a2", SENT_PLANE_MORE, [HELD_MORE, ROWS] + ends + [ONE], rate, *a)
     a = in_plane(a)
     fitness = a
-    a = call(middle_ring, "a3", SENT_RING, [HELD, ROWS, LEFT, RIGHT] + ends + [ONE], rate, a)
+    a = call(middle_ring, "a3", SENT_RING, [HELD, ROWS, LEFT, RIGHT] + fine + [ONE], rate, a)
     a = round_ring(a)
-    b = call(middle_plane, "b3", SENT_PLANE, [HELD, ROWS, LEFT, RIGHT] + ends + [ONE], rate, fitness, *b)
+    b = call(middle_plane, "b3", SENT_PLANE, [HELD, ROWS, LEFT, RIGHT] + fine + [ONE], rate, fitness, *b)
     b = in_plane(b)
-    b = call(plane_to_ring(PLANE_HERE, []), "b4", SENT_RING, [HELD] + ends, rate, b)
-    b = round_ring(b)
-    a = call(ring_to_plane, "a4", SENT_PLANE, [HELD] + ends, rate, *a)
+    b = call(plane_to_ring, "b4", SENT_RING, [HELD] + fine, rate, b)
+    b = round_ring(b, (3, 5, 2, 6))
+    a = call(ring_to_plane, "a4", SENT_PLANE, [HELD] + fine, rate, *a)
     a = in_plane(a)
     done = jax.ShapeDtypeStruct((RING, PLANE, REST, 128), F32)
     a = call(end_plane, "a5", done, [HELD] + ends, rate, a)

time: 306 us -> 306 us (level)
    unnamed x24 -> x22, local copies, waits for them, and re-layouts: 11.5 us -> 9.1 us
  transfers between devices with their start and end apart: 32 -> 32, of which waited for: 21 -> 21; matrix products, arithmetic and copies ran while one was open for 0% -> 0% of each run, Pallas kernels for 8% -> 9%
where the time goes in v3:
time: 306 us; the launch traced here: 305 us
  waiting for transfers between devices  160 us (52%)
  starting transfers between devices  93.3 us (30%)
  Pallas kernels  42.5 us (14%)
  local copies, waits for them, and re-layouts  9.1 us (3%)
    ppermute x28, waiting for transfers between devices, round_ring(): moved[shift] = lax.ppermute(parts[shift], AXES, ring_pairs(shift))  159 us
    ppermute x28, starting transfers between devices, round_ring(): moved[shift] = lax.ppermute(parts[shift], AXES, ring_pairs(shift))  60.1 us
    pallas_call x10, Pallas kernels, call(): pl.pallas_call(kernel, out_shape=[far(out) for out in outs] if many else...  42.5 us
    all_to_all x4, starting transfers between devices, in_plane(): lax.all_to_all(piece, AXES, split_axis=0, concat_axis=0, tiled=True, axis...  33.2 us
    unnamed x22, local copies, waits for them, and re-layouts  9.1 us
  transfers between devices with their start and end apart: 32, of which 21 were waited for; matrix products, arithmetic and copies ran while one was open for 0% of the time, Pallas kernels for 9%

profile of v3, /device:TPU:1, one launch (start us, length us, event | category | flops | bytes accessed | tf_op | source)
XLA Modules:
  0.0 304.9 jit_solution(4724798201010995147)
XLA Ops:
  0.0 5.2 %shard_map.42 = f32[32,128,128]{2,1,0:T(8,128)} custom-call(s32[2]{0:T(128)} %rate_ref.19, s32[128,128]{1,0:T(8,128)} %bitcast.13, f32[8,1024,128]{2,1,0:T(8,128)} %bitcast.11), custom_call_target="tpu_custom_call" | custom-call | flops 268435456 | bytes 8388608 | tf_op jit(solution)/shard_map/pallas_call | solution.py:487
  5.2 8.6 %all-to-all-start.2 = ((f32[32,128,128]{2,1,0:T(8,128)}), f32[32,128,128]{2,1,0:T(8,128)S(1)}, u32[]{:S(2)}, u32[]{:S(2)}) async-start(f32[32,128,128]{2,1,0:T(8,128)} %shard_map.42), calls=%async_computation.2 | async-start | bytes 4194304 | tf_op jit(solution)/shard_map/all_to_all | solution.py:509
  13.8 5.6 %shard_map.37 = (f32[33,16,128]{2,1,0:T(8,128)}, f32[33,16,128]{2,1,0:T(8,128)}, f32[33,16,128]{2,1,0:T(8,128)}, f32[33,16,128]{2,1,0:T(8,128)}, f32[33,16,128]{...) custom-call(s32[2]{0:T(128)} %rate_ref.19, s32[128,128]{1,0:T(8,128)} %bitcast.14, ...), custom_call_target="tpu_custom_call" | custom-call | flops 268435456 | bytes 8388608 | tf_op jit(solution)/shard_map/pallas_call | solution.py:487
  21.1 3.0 collective-permute-start.1
  24.1 3.8 %collective-permute-start.2 = (f32[33,16,128]{2,1,0:T(8,128)}, f32[33,16,128]{2,1,0:T(8,128)S(1)}, u32[]{:S(2)}, u32[]{:S(2)}) collective-permute-start(f32[33,16,128]{2,1,0:T(8,128)} %get-tuple-element.40), channel_id=1, source_target_pairs={{0,192},{1,193},{2,194},{3,195},{8,200},{9,201},{10,202},{11,203},... | collective-permute-start | bytes 811016 | tf_op jit(solution)/shard_map/ppermute | solution.py:504
  28.3 4.5 %collective-permute-start.4 = (f32[33,16,128]{2,1,0:T(8,128)}, f32[33,16,128]{2,1,0:T(8,128)S(1)}, u32[]{:S(2)}, u32[]{:S(2)}) collective-permute-start(f32[33,16,128]{2,1,0:T(8,128)} %get-tuple-element.42), channel_id=1, source_target_pairs={{0,68},{1,69},{2,70},{3,71},{8,76},{9,77},{10,78},{11,79},{16,84},... | collective-permute-start | bytes 811016 | tf_op jit(solution)/shard_map/ppermute | solution.py:504
  32.8 2.4 collective-permute-start.5
  35.2 4.0 %collective-permute-done.1.refs_2_ = f32[33,16,128]{2,1,0:T(8,128)S(1)} collective-permute-done((f32[33,16,128]{2,1,0:T(8,128)}, f32[33,16,128]{2,1,0:T(8,128)S(1)}, u32[]{:S(2)}, u32[]{:S(2)}) %collective-permute-start.1) | collective-permute-done | bytes 270368 | tf_op jit(solution)/shard_map/ppermute | solution.py:504
  39.2 6.9 %collective-permute-start.6 = (f32[33,16,128]{2,1,0:T(8,128)}, f32[33,16,128]{2,1,0:T(8,128)S(1)}, u32[]{:S(2)}, u32[]{:S(2)}) collective-permute-start(f32[33,16,128]{2,1,0:T(8,128)} %get-tuple-element.44), channel_id=1, source_target_pairs={{0,196},{1,197},{2,198},{3,199},{8,204},{9,205},{10,206},{11,207},... | collective-permute-start | bytes 811016 | tf_op jit(solution)/shard_map/ppermute | solution.py:504
  46.1 15.1 %collective-permute-done.2.refs_3_ = f32[33,16,128]{2,1,0:T(8,128)S(1)} collective-permute-done((f32[33,16,128]{2,1,0:T(8,128)}, f32[33,16,128]{2,1,0:T(8,128)S(1)}, u32[]{:S(2)}, u32[]{:S(2)}) %collective-permute-start.2) | collective-permute-done | bytes 270368 | tf_op jit(solution)/shard_map/ppermute | solution.py:504
  61.2 5.1 %collective-permute-done.3.refs_4_ = f32[33,16,128]{2,1,0:T(8,128)S(1)} collective-permute-done((f32[33,16,128]{2,1,0:T(8,128)}, f32[33,16,128]{2,1,0:T(8,128)S(1)}, u32[]{:S(2)}, u32[]{:S(2)}) %collective-permute-start.3) | collective-permute-done | bytes 270368 | tf_op jit(solution)/shard_map/ppermute | solution.py:504
  66.4 7.8 %collective-permute-done.5.refs_6_ = f32[33,16,128]{2,1,0:T(8,128)S(1)} collective-permute-done((f32[33,16,128]{2,1,0:T(8,128)}, f32[33,16,128]{2,1,0:T(8,128)S(1)}, u32[]{:S(2)}, u32[]{:S(2)}) %collective-permute-start.5) | collective-permute-done | bytes 270368 | tf_op jit(solution)/shard_map/ppermute | solution.py:504
  74.2 2.4 collective-permute-done.6.refs_7_
  77.6 3.0 shard_map.38
  81.9 8.5 %all-to-all-start = ((f32[32,136,128]{2,1,0:T(8,128)}), f32[32,136,128]{2,1,0:T(8,128)S(1)}, u32[]{:S(2)}, u32[]{:S(2)}) async-start(f32[32,136,128]{2,1,0:T(8,128)} %shard_map.38), calls=%async_computation | async-start | bytes 4456448 | tf_op jit(solution)/shard_map/all_to_all | solution.py:509
  92.0 2.8 shard_map.43
  94.8 3.4 %collective-permute-start.14 = (f32[32,16,128]{2,1,0:T(8,128)}, f32[32,16,128]{2,1,0:T(8,128)S(1)}, u32[]{:S(2)}, u32[]{:S(2)}) collective-permute-start(f32[32,16,128]{2,1,0:T(8,128)} %get-tuple-element.54), channel_id=1, source_target_pairs={{0,64},{1,65},{2,66},{3,67},{8,72},{9,73},{10,74},{11,75},{16,80},... | collective-permute-start | bytes 786440 | tf_op jit(solution)/shard_map/ppermute | solution.py:504
  99.3 4.5 %collective-permute-start.17 = (f32[32,16,128]{2,1,0:T(8,128)}, f32[32,16,128]{2,1,0:T(8,128)S(1)}, u32[]{:S(2)}, u32[]{:S(2)}) collective-permute-start(f32[32,16,128]{2,1,0:T(8,128)} %get-tuple-element.57), channel_id=1, source_target_pairs={{0,4},{1,5},{2,6},{3,7},{8,12},{9,13},{10,14},{11,15},{16,20},{17,... | collective-permute-start | bytes 786440 | tf_op jit(solution)/shard_map/ppermute | solution.py:504
  105.0 2.1 collective-permute-start.19
  107.1 9.7 %collective-permute-done.15.refs_2_ = f32[32,16,128]{2,1,0:T(8,128)S(1)} collective-permute-done((f32[32,16,128]{2,1,0:T(8,128)}, f32[32,16,128]{2,1,0:T(8,128)S(1)}, u32[]{:S(2)}, u32[]{:S(2)}) %collective-permute-start.15) | collective-permute-done | bytes 262176 | tf_op jit(solution)/shard_map/ppermute | solution.py:504
  116.8 9.9 %collective-permute-done.16.refs_3_ = f32[32,16,128]{2,1,0:T(8,128)S(1)} collective-permute-done((f32[32,16,128]{2,1,0:T(8,128)}, f32[32,16,128]{2,1,0:T(8,128)S(1)}, u32[]{:S(2)}, u32[]{:S(2)}) %collective-permute-start.16) | collective-permute-done | bytes 262176 | tf_op jit(solution)/shard_map/ppermute | solution.py:504
  126.7 13.9 %collective-permute-done.17.refs_4_ = f32[32,16,128]{2,1,0:T(8,128)S(1)} collective-permute-done((f32[32,16,128]{2,1,0:T(8,128)}, f32[32,16,128]{2,1,0:T(8,128)S(1)}, u32[]{:S(2)}, u32[]{:S(2)}) %collective-permute-start.17) | collective-permute-done | bytes 262176 | tf_op jit(solution)/shard_map/ppermute | solution.py:504
  140.7 4.7 %collective-permute-done.19.refs_6_ = f32[32,16,128]{2,1,0:T(8,128)S(1)} collective-permute-done((f32[32,16,128]{2,1,0:T(8,128)}, f32[32,16,128]{2,1,0:T(8,128)S(1)}, u32[]{:S(2)}, u32[]{:S(2)}) %collective-permute-start.19) | collective-permute-done | bytes 262176 | tf_op jit(solution)/shard_map/ppermute | solution.py:504
  146.0 4.8 %collective-permute-done.20.refs_7_ = f32[32,16,128]{2,1,0:T(8,128)S(1)} collective-permute-done((f32[32,16,128]{2,1,0:T(8,128)}, f32[32,16,128]{2,1,0:T(8,128)S(1)}, u32[]{:S(2)}, u32[]{:S(2)}) %collective-permute-start.20) | collective-permute-done | bytes 262176 | tf_op jit(solution)/shard_map/ppermute | solution.py:504
  154.4 6.9 %shard_map.44 = f32[32,128,128]{2,1,0:T(8,128)} custom-call(s32[2]{0:T(128)S(1)} %copy-done.10, f32[32,136,128]{2,1,0:T(8,128)S(1)} %all-to-all-done.x_ref.fitness_ref, f32[32,16,128]{2,1,0:T(8,128)S(1)} %copy-done.4, f32[32,16,128]{2,1,0:T(8,128)S(1)} %collective-permute-done.14.refs_1_, f32[32,16,128]{2,1,0:T(8,128)S(1)} %collective-permute-done.15.refs_2_, ...), custom_call_target="tpu_custom_call" | custom-call | flops 268435456 | bytes 8388608 | tf_op jit(solution)/shard_map/pallas_call | solution.py:487
  161.4 7.7 %all-to-all-start.3 = ((f32[32,128,128]{2,1,0:T(8,128)}), f32[32,128,128]{2,1,0:T(8,128)}, u32[]{:S(2)}, u32[]{:S(2)}) async-start(f32[32,128,128]{2,1,0:T(8,128)} %shard_map.44), calls=%async_computation.3 | async-start | bytes 4194304 | tf_op jit(solution)/shard_map/all_to_all | solution.py:509
  169.1 6.4 %shard_map.39 = (f32[32,16,128]{2,1,0:T(8,128)}, f32[32,16,128]{2,1,0:T(8,128)}, f32[32,16,128]{2,1,0:T(8,128)}, f32[32,16,128]{2,1,0:T(8,128)}, f32[32,16,128]{...) custom-call(s32[2]{0:T(128)S(1)} %copy-done.10, ...), custom_call_target="tpu_custom_call" | custom-call | flops 268435456 | bytes 8388608 | tf_op jit(solution)/shard_map/pallas_call | solution.py:487
  177.3 3.3 %collective-permute-start.9 = (f32[32,16,128]{2,1,0:T(8,128)}, f32[32,16,128]{2,1,0:T(8,128)S(1)}, u32[]{:S(2)}, u32[]{:S(2)}) collective-permute-start(f32[32,16,128]{2,1,0:T(8,128)} %get-tuple-element.48), channel_id=1, source_target_pairs={{0,192},{1,193},{2,194},{3,195},{8,200},{9,201},{10,202},{11,203},... | collective-permute-start | bytes 786440 | tf_op jit(solution)/shard_map/ppermute | solution.py:504
  181.5 4.1 %collective-permute-start.11 = (f32[32,16,128]{2,1,0:T(8,128)}, f32[32,16,128]{2,1,0:T(8,128)S(1)}, u32[]{:S(2)}, u32[]{:S(2)}) collective-permute-start(f32[32,16,128]{2,1,0:T(8,128)} %get-tuple-element.50), channel_id=1, source_target_pairs={{0,68},{1,69},{2,70},{3,71},{8,76},{9,77},{10,78},{11,79},{16,84},... | collective-permute-start | bytes 786440 | tf_op jit(solution)/shard_map/ppermute | solution.py:504
  185.6 2.7 collective-permute-start.12
  188.3 9.0 %collective-permute-done.8.refs_2_ = f32[32,16,128]{2,1,0:T(8,128)S(1)} collective-permute-done((f32[32,16,128]{2,1,0:T(8,128)}, f32[32,16,128]{2,1,0:T(8,128)S(1)}, u32[]{:S(2)}, u32[]{:S(2)}) %collective-permute-start.8) | collective-permute-done | bytes 262176 | tf_op jit(solution)/shard_map/ppermute | solution.py:504
  197.3 15.0 %collective-permute-done.9.refs_3_ = f32[32,16,128]{2,1,0:T(8,128)S(1)} collective-permute-done((f32[32,16,128]{2,1,0:T(8,128)}, f32[32,16,128]{2,1,0:T(8,128)S(1)}, u32[]{:S(2)}, u32[]{:S(2)}) %collective-permute-start.9) | collective-permute-done | bytes 262176 | tf_op jit(solution)/shard_map/ppermute | solution.py:504
  212.3 10.1 %collective-permute-done.10.refs_4_ = f32[32,16,128]{2,1,0:T(8,128)S(1)} collective-permute-done((f32[32,16,128]{2,1,0:T(8,128)}, f32[32,16,128]{2,1,0:T(8,128)S(1)}, u32[]{:S(2)}, u32[]{:S(2)}) %collective-permute-start.10) | collective-permute-done | bytes 262176 | tf_op jit(solution)/shard_map/ppermute | solution.py:504
  222.4 3.7 %collective-permute-done.12.refs_6_ = f32[32,16,128]{2,1,0:T(8,128)S(1)} collective-permute-done((f32[32,16,128]{2,1,0:T(8,128)}, f32[32,16,128]{2,1,0:T(8,128)S(1)}, u32[]{:S(2)}, u32[]{:S(2)}) %collective-permute-start.12) | collective-permute-done | bytes 262176 | tf_op jit(solution)/shard_map/ppermute | solution.py:504
  226.1 2.3 collective-permute-done.13.refs_7_
  229.4 2.8 shard_map.40
  232.2 8.5 %all-to-all-start.1 = ((f32[32,128,128]{2,1,0:T(8,128)}), f32[32,128,128]{2,1,0:T(8,128)S(1)}, u32[]{:S(2)}, u32[]{:S(2)}) async-start(f32[32,128,128]{2,1,0:T(8,128)} %shard_map.40), calls=%async_computation.1 | async-start | bytes 4194304 | tf_op jit(solution)/shard_map/all_to_all | solution.py:509
  240.6 4.0 %shard_map.45 = (f32[32,16,128]{2,1,0:T(8,128)}, f32[32,16,128]{2,1,0:T(8,128)}, f32[32,16,128]{2,1,0:T(8,128)}, f32[32,16,128]{2,1,0:T(8,128)}, f32[32,16,128]{...) custom-call(s32[2]{0:T(128)S(1)} %copy-done.10, ...), custom_call_target="tpu_custom_call" | custom-call | flops 268435456 | bytes 8388608 | tf_op jit(solution)/shard_map/pallas_call | solution.py:487
  244.6 3.3 %collective-permute-start.21 = (f32[32,16,128]{2,1,0:T(8,128)}, f32[32,16,128]{2,1,0:T(8,128)S(1)}, u32[]{:S(2)}, u32[]{:S(2)}) collective-permute-start(f32[32,16,128]{2,1,0:T(8,128)} %get-tuple-element.62), channel_id=1, source_target_pairs={{0,64},{1,65},{2,66},{3,67},{8,72},{9,73},{10,74},{11,75},{16,80},... | collective-permute-start | bytes 786440 | tf_op jit(solution)/shard_map/ppermute | solution.py:504
  249.0 4.6 %collective-permute-start.24 = (f32[32,16,128]{2,1,0:T(8,128)}, f32[32,16,128]{2,1,0:T(8,128)S(1)}, u32[]{:S(2)}, u32[]{:S(2)}) collective-permute-start(f32[32,16,128]{2,1,0:T(8,128)} %get-tuple-element.65), channel_id=1, source_target_pairs={{0,4},{1,5},{2,6},{3,7},{8,12},{9,13},{10,14},{11,15},{16,20},{17,... | collective-permute-start | bytes 786440 | tf_op jit(solution)/shard_map/ppermute | solution.py:504
  254.7 2.2 collective-permute-start.26
  256.9 9.8 %collective-permute-done.22.refs_2_ = f32[32,16,128]{2,1,0:T(8,128)S(1)} collective-permute-done((f32[32,16,128]{2,1,0:T(8,128)}, f32[32,16,128]{2,1,0:T(8,128)S(1)}, u32[]{:S(2)}, u32[]{:S(2)}) %collective-permute-start.22) | collective-permute-done | bytes 262176 | tf_op jit(solution)/shard_map/ppermute | solution.py:504
  267.7 1.8 shard_map.41.other_ref
  269.5 6.7 %collective-permute-done.23.refs_3_ = f32[32,16,128]{2,1,0:T(8,128)S(1)} collective-permute-done((f32[32,16,128]{2,1,0:T(8,128)}, f32[32,16,128]{2,1,0:T(8,128)S(1)}, u32[]{:S(2)}, u32[]{:S(2)}) %collective-permute-start.23) | collective-permute-done | bytes 262176 | tf_op jit(solution)/shard_map/ppermute | solution.py:504
  276.2 14.0 %collective-permute-done.24.refs_4_ = f32[32,16,128]{2,1,0:T(8,128)S(1)} collective-permute-done((f32[32,16,128]{2,1,0:T(8,128)}, f32[32,16,128]{2,1,0:T(8,128)S(1)}, u32[]{:S(2)}, u32[]{:S(2)}) %collective-permute-start.24) | collective-permute-done | bytes 262176 | tf_op jit(solution)/shard_map/ppermute | solution.py:504
  290.2 5.0 %collective-permute-done.26.refs_6_ = f32[32,16,128]{2,1,0:T(8,128)} collective-permute-done((f32[32,16,128]{2,1,0:T(8,128)}, f32[32,16,128]{2,1,0:T(8,128)}, u32[]{:S(2)}, u32[]{:S(2)}) %collective-permute-start.26) | collective-permute-done | bytes 262176 | tf_op jit(solution)/shard_map/ppermute | solution.py:504
  295.3 5.4 %collective-permute-done.27.refs_7_ = f32[32,16,128]{2,1,0:T(8,128)} collective-permute-done((f32[32,16,128]{2,1,0:T(8,128)}, f32[32,16,128]{2,1,0:T(8,128)}, u32[]{:S(2)}, u32[]{:S(2)}) %collective-permute-start.27) | collective-permute-done | bytes 262176 | tf_op jit(solution)/shard_map/ppermute | solution.py:504
  300.7 4.1 %shard_map.46 = f32[8,1024,128]{2,1,0:T(8,128)} custom-call(s32[2]{0:T(128)S(1)} %copy-done.10, f32[8,32,16,128]{3,2,1,0:T(8,128)S(1)} %shard_map.41.other_ref, f32[32,16,128]{2,1,0:T(8,128)S(1)} %copy-done.3, f32[32,16,128]{2,1,0:T(8,128)S(1)} %collective-permute-done.21.refs_1_, f32[32,16,128]{2,1,0:T(8,128)S(1)} %collective-permute-done.22.refs_2_, ...), custom_call_target="tpu_custom_call" | custom-call | flops 268435456 | bytes 8388608 | tf_op jit(solution)/shard_map/pallas_call | solution.py:487
  (48 shorter events, 19.5 us)
Async XLA Ops:
  5.2 75.4 %all-to-all-start.2 = ((f32[32,128,128]{2,1,0:T(8,128)}), f32[32,128,128]{2,1,0:T(8,128)S(1)}, u32[]{:S(2)}, u32[]{:S(2)}) async-start(f32[32,128,128]{2,1,0:T(8,128)} %shard_map.42), calls=%async_computation.2 | async-start | bytes 4194304 | tf_op jit(solution)/shard_map/all_to_all | solution.py:509
  13.8 62.8 %copy-start.10 = (s32[2]{0:T(128)S(1)}, s32[2]{0:T(128)}, u32[]{:S(2)}) copy-start(s32[2]{0:T(128)} %rate_ref.19) | copy-start | bytes 28
  19.4 13.4 %collective-permute-start = (f32[33,16,128]{2,1,0:T(8,128)}, f32[33,16,128]{2,1,0:T(8,128)S(1)}, u32[]{:S(2)}, u32[]{:S(2)}) collective-permute-start(f32[33,16,128]{2,1,0:T(8,128)} %get-tuple-element.38), channel_id=1, source_target_pairs={{0,64},{1,65},{2,66},{3,67},{8,72},{9,73},{10,74},{11,75},{16,80},... | collective-permute-start | bytes 811016 | tf_op jit(solution)/shard_map/ppermute | solution.py:504
  21.1 18.1 %collective-permute-start.1 = (f32[33,16,128]{2,1,0:T(8,128)}, f32[33,16,128]{2,1,0:T(8,128)S(1)}, u32[]{:S(2)}, u32[]{:S(2)}) collective-permute-start(f32[33,16,128]{2,1,0:T(8,128)} %get-tuple-element.39), channel_id=1, source_target_pairs={{0,128},{1,129},{2,130},{3,131},{8,136},{9,137},{10,138},{11,139},... | collective-permute-start | bytes 811016 | tf_op jit(solution)/shard_map/ppermute | solution.py:504
  24.1 37.1 %collective-permute-start.2 = (f32[33,16,128]{2,1,0:T(8,128)}, f32[33,16,128]{2,1,0:T(8,128)S(1)}, u32[]{:S(2)}, u32[]{:S(2)}) collective-permute-start(f32[33,16,128]{2,1,0:T(8,128)} %get-tuple-element.40), channel_id=1, source_target_pairs={{0,192},{1,193},{2,194},{3,195},{8,200},{9,201},{10,202},{11,203},... | collective-permute-start | bytes 811016 | tf_op jit(solution)/shard_map/ppermute | solution.py:504
  27.9 38.5 %collective-permute-start.3 = (f32[33,16,128]{2,1,0:T(8,128)}, f32[33,16,128]{2,1,0:T(8,128)S(1)}, u32[]{:S(2)}, u32[]{:S(2)}) collective-permute-start(f32[33,16,128]{2,1,0:T(8,128)} %get-tuple-element.41), channel_id=1, source_target_pairs={{0,4},{1,5},{2,6},{3,7},{8,12},{9,13},{10,14},{11,15},{16,20},{17,... | collective-permute-start | bytes 811016 | tf_op jit(solution)/shard_map/ppermute | solution.py:504
  28.3 38.0 %collective-permute-start.4 = (f32[33,16,128]{2,1,0:T(8,128)}, f32[33,16,128]{2,1,0:T(8,128)S(1)}, u32[]{:S(2)}, u32[]{:S(2)}) collective-permute-start(f32[33,16,128]{2,1,0:T(8,128)} %get-tuple-element.42), channel_id=1, source_target_pairs={{0,68},{1,69},{2,70},{3,71},{8,76},{9,77},{10,78},{11,79},{16,84},... | collective-permute-start | bytes 811016 | tf_op jit(solution)/shard_map/ppermute | solution.py:504
  32.8 41.4 %collective-permute-start.5 = (f32[33,16,128]{2,1,0:T(8,128)}, f32[33,16,128]{2,1,0:T(8,128)S(1)}, u32[]{:S(2)}, u32[]{:S(2)}) collective-permute-start(f32[33,16,128]{2,1,0:T(8,128)} %get-tuple-element.43), channel_id=1, source_target_pairs={{0,132},{1,133},{2,134},{3,135},{8,140},{9,141},{10,142},{11,143},... | collective-permute-start | bytes 811016 | tf_op jit(solution)/shard_map/ppermute | solution.py:504
  39.2 37.4 %collective-permute-start.6 = (f32[33,16,128]{2,1,0:T(8,128)}, f32[33,16,128]{2,1,0:T(8,128)S(1)}, u32[]{:S(2)}, u32[]{:S(2)}) collective-permute-start(f32[33,16,128]{2,1,0:T(8,128)} %get-tuple-element.44), channel_id=1, source_target_pairs={{0,196},{1,197},{2,198},{3,199},{8,204},{9,205},{10,206},{11,207},... | collective-permute-start | bytes 811016 | tf_op jit(solution)/shard_map/ppermute | solution.py:504
  76.6 1.0 copy-start.2
  80.6 1.3 copy-start
  81.9 69.7 %all-to-all-start = ((f32[32,136,128]{2,1,0:T(8,128)}), f32[32,136,128]{2,1,0:T(8,128)S(1)}, u32[]{:S(2)}, u32[]{:S(2)}) async-start(f32[32,136,128]{2,1,0:T(8,128)} %shard_map.38), calls=%async_computation | async-start | bytes 4456448 | tf_op jit(solution)/shard_map/all_to_all | solution.py:509
  90.4 1.6 copy-start.1
  94.8 10.2 %collective-permute-start.14 = (f32[32,16,128]{2,1,0:T(8,128)}, f32[32,16,128]{2,1,0:T(8,128)S(1)}, u32[]{:S(2)}, u32[]{:S(2)}) collective-permute-start(f32[32,16,128]{2,1,0:T(8,128)} %get-tuple-element.54), channel_id=1, source_target_pairs={{0,64},{1,65},{2,66},{3,67},{8,72},{9,73},{10,74},{11,75},{16,80},... | collective-permute-start | bytes 786440 | tf_op jit(solution)/shard_map/ppermute | solution.py:504
  98.2 18.6 %collective-permute-start.15 = (f32[32,16,128]{2,1,0:T(8,128)}, f32[32,16,128]{2,1,0:T(8,128)S(1)}, u32[]{:S(2)}, u32[]{:S(2)}) collective-permute-start(f32[32,16,128]{2,1,0:T(8,128)} %get-tuple-element.55), channel_id=1, source_target_pairs={{0,128},{1,129},{2,130},{3,131},{8,136},{9,137},{10,138},{11,139},... | collective-permute-start | bytes 786440 | tf_op jit(solution)/shard_map/ppermute | solution.py:504
  99.0 27.7 %collective-permute-start.16 = (f32[32,16,128]{2,1,0:T(8,128)}, f32[32,16,128]{2,1,0:T(8,128)S(1)}, u32[]{:S(2)}, u32[]{:S(2)}) collective-permute-start(f32[32,16,128]{2,1,0:T(8,128)} %get-tuple-element.56), channel_id=1, source_target_pairs={{0,192},{1,193},{2,194},{3,195},{8,200},{9,201},{10,202},{11,203},... | collective-permute-start | bytes 786440 | tf_op jit(solution)/shard_map/ppermute | solution.py:504
  99.3 41.3 %collective-permute-start.17 = (f32[32,16,128]{2,1,0:T(8,128)}, f32[32,16,128]{2,1,0:T(8,128)S(1)}, u32[]{:S(2)}, u32[]{:S(2)}) collective-permute-start(f32[32,16,128]{2,1,0:T(8,128)} %get-tuple-element.57), channel_id=1, source_target_pairs={{0,4},{1,5},{2,6},{3,7},{8,12},{9,13},{10,14},{11,15},{16,20},{17,... | collective-permute-start | bytes 786440 | tf_op jit(solution)/shard_map/ppermute | solution.py:504
  103.8 36.8 %collective-permute-start.18 = (f32[32,16,128]{2,1,0:T(8,128)}, f32[32,16,128]{2,1,0:T(8,128)S(1)}, u32[]{:S(2)}, u32[]{:S(2)}) collective-permute-start(f32[32,16,128]{2,1,0:T(8,128)} %get-tuple-element.58), channel_id=1, source_target_pairs={{0,68},{1,69},{2,70},{3,71},{8,76},{9,77},{10,78},{11,79},{16,84},... | collective-permute-start | bytes 786440 | tf_op jit(solution)/shard_map/ppermute | solution.py:504
  105.0 40.4 %collective-permute-start.19 = (f32[32,16,128]{2,1,0:T(8,128)}, f32[32,16,128]{2,1,0:T(8,128)S(1)}, u32[]{:S(2)}, u32[]{:S(2)}) collective-permute-start(f32[32,16,128]{2,1,0:T(8,128)} %get-tuple-element.59), channel_id=1, source_target_pairs={{0,132},{1,133},{2,134},{3,135},{8,140},{9,141},{10,142},{11,143},... | collective-permute-start | bytes 786440 | tf_op jit(solution)/shard_map/ppermute | solution.py:504
  116.8 34.1 %collective-permute-start.20 = (f32[32,16,128]{2,1,0:T(8,128)}, f32[32,16,128]{2,1,0:T(8,128)S(1)}, u32[]{:S(2)}, u32[]{:S(2)}) collective-permute-start(f32[32,16,128]{2,1,0:T(8,128)} %get-tuple-element.60), channel_id=1, source_target_pairs={{0,196},{1,197},{2,198},{3,199},{8,204},{9,205},{10,206},{11,207},... | collective-permute-start | bytes 786440 | tf_op jit(solution)/shard_map/ppermute | solution.py:504
  145.3 0.7 copy-start.6
  150.9 0.7 copy-start.8
  151.6 1.0 copy-start.4
  152.5 0.9 copy-start.7
  153.5 0.9 copy-start.9
  161.4 70.8 %all-to-all-start.3 = ((f32[32,128,128]{2,1,0:T(8,128)}), f32[32,128,128]{2,1,0:T(8,128)}, u32[]{:S(2)}, u32[]{:S(2)}) async-start(f32[32,128,128]{2,1,0:T(8,128)} %shard_map.44), calls=%async_computation.3 | async-start | bytes 4194304 | tf_op jit(solution)/shard_map/all_to_all | solution.py:509
  175.5 10.2 %collective-permute-start.7 = (f32[32,16,128]{2,1,0:T(8,128)}, f32[32,16,128]{2,1,0:T(8,128)S(1)}, u32[]{:S(2)}, u32[]{:S(2)}) collective-permute-start(f32[32,16,128]{2,1,0:T(8,128)} %get-tuple-element.46), channel_id=1, source_target_pairs={{0,64},{1,65},{2,66},{3,67},{8,72},{9,73},{10,74},{11,75},{16,80},... | collective-permute-start | bytes 786440 | tf_op jit(solution)/shard_map/ppermute | solution.py:504
  175.8 21.5 %collective-permute-start.8 = (f32[32,16,128]{2,1,0:T(8,128)}, f32[32,16,128]{2,1,0:T(8,128)S(1)}, u32[]{:S(2)}, u32[]{:S(2)}) collective-permute-start(f32[32,16,128]{2,1,0:T(8,128)} %get-tuple-element.47), channel_id=1, source_target_pairs={{0,128},{1,129},{2,130},{3,131},{8,136},{9,137},{10,138},{11,139},... | collective-permute-start | bytes 786440 | tf_op jit(solution)/shard_map/ppermute | solution.py:504
  177.3 35.0 %collective-permute-start.9 = (f32[32,16,128]{2,1,0:T(8,128)}, f32[32,16,128]{2,1,0:T(8,128)S(1)}, u32[]{:S(2)}, u32[]{:S(2)}) collective-permute-start(f32[32,16,128]{2,1,0:T(8,128)} %get-tuple-element.48), channel_id=1, source_target_pairs={{0,192},{1,193},{2,194},{3,195},{8,200},{9,201},{10,202},{11,203},... | collective-permute-start | bytes 786440 | tf_op jit(solution)/shard_map/ppermute | solution.py:504
  180.7 41.7 %collective-permute-start.10 = (f32[32,16,128]{2,1,0:T(8,128)}, f32[32,16,128]{2,1,0:T(8,128)S(1)}, u32[]{:S(2)}, u32[]{:S(2)}) collective-permute-start(f32[32,16,128]{2,1,0:T(8,128)} %get-tuple-element.49), channel_id=1, source_target_pairs={{0,4},{1,5},{2,6},{3,7},{8,12},{9,13},{10,14},{11,15},{16,20},{17,... | collective-permute-start | bytes 786440 | tf_op jit(solution)/shard_map/ppermute | solution.py:504
  181.5 40.8 %collective-permute-start.11 = (f32[32,16,128]{2,1,0:T(8,128)}, f32[32,16,128]{2,1,0:T(8,128)S(1)}, u32[]{:S(2)}, u32[]{:S(2)}) collective-permute-start(f32[32,16,128]{2,1,0:T(8,128)} %get-tuple-element.50), channel_id=1, source_target_pairs={{0,68},{1,69},{2,70},{3,71},{8,76},{9,77},{10,78},{11,79},{16,84},... | collective-permute-start | bytes 786440 | tf_op jit(solution)/shard_map/ppermute | solution.py:504
  185.6 40.5 %collective-permute-start.12 = (f32[32,16,128]{2,1,0:T(8,128)}, f32[32,16,128]{2,1,0:T(8,128)S(1)}, u32[]{:S(2)}, u32[]{:S(2)}) collective-permute-start(f32[32,16,128]{2,1,0:T(8,128)} %get-tuple-element.51), channel_id=1, source_target_pairs={{0,132},{1,133},{2,134},{3,135},{8,140},{9,141},{10,142},{11,143},... | collective-permute-start | bytes 786440 | tf_op jit(solution)/shard_map/ppermute | solution.py:504
  197.3 31.1 %collective-permute-start.13 = (f32[32,16,128]{2,1,0:T(8,128)}, f32[32,16,128]{2,1,0:T(8,128)S(1)}, u32[]{:S(2)}, u32[]{:S(2)}) collective-permute-start(f32[32,16,128]{2,1,0:T(8,128)} %get-tuple-element.52), channel_id=1, source_target_pairs={{0,196},{1,197},{2,198},{3,199},{8,204},{9,205},{10,206},{11,207},... | collective-permute-start | bytes 786440 | tf_op jit(solution)/shard_map/ppermute | solution.py:504
  228.4 0.9 copy-start.5
  232.2 35.5 %all-to-all-start.1 = ((f32[32,128,128]{2,1,0:T(8,128)}), f32[32,128,128]{2,1,0:T(8,128)S(1)}, u32[]{:S(2)}, u32[]{:S(2)}) async-start(f32[32,128,128]{2,1,0:T(8,128)} %shard_map.40), calls=%async_computation.1 | async-start | bytes 4194304 | tf_op jit(solution)/shard_map/all_to_all | solution.py:509
  244.6 10.1 %collective-permute-start.21 = (f32[32,16,128]{2,1,0:T(8,128)}, f32[32,16,128]{2,1,0:T(8,128)S(1)}, u32[]{:S(2)}, u32[]{:S(2)}) collective-permute-start(f32[32,16,128]{2,1,0:T(8,128)} %get-tuple-element.62), channel_id=1, source_target_pairs={{0,64},{1,65},{2,66},{3,67},{8,72},{9,73},{10,74},{11,75},{16,80},... | collective-permute-start | bytes 786440 | tf_op jit(solution)/shard_map/ppermute | solution.py:504
  247.9 18.8 %collective-permute-start.22 = (f32[32,16,128]{2,1,0:T(8,128)}, f32[32,16,128]{2,1,0:T(8,128)S(1)}, u32[]{:S(2)}, u32[]{:S(2)}) collective-permute-start(f32[32,16,128]{2,1,0:T(8,128)} %get-tuple-element.63), channel_id=1, source_target_pairs={{0,128},{1,129},{2,130},{3,131},{8,136},{9,137},{10,138},{11,139},... | collective-permute-start | bytes 786440 | tf_op jit(solution)/shard_map/ppermute | solution.py:504
  248.9 27.3 %collective-permute-start.23 = (f32[32,16,128]{2,1,0:T(8,128)}, f32[32,16,128]{2,1,0:T(8,128)S(1)}, u32[]{:S(2)}, u32[]{:S(2)}) collective-permute-start(f32[32,16,128]{2,1,0:T(8,128)} %get-tuple-element.64), channel_id=1, source_target_pairs={{0,192},{1,193},{2,194},{3,195},{8,200},{9,201},{10,202},{11,203},... | collective-permute-start | bytes 786440 | tf_op jit(solution)/shard_map/ppermute | solution.py:504
  249.0 41.2 %collective-permute-start.24 = (f32[32,16,128]{2,1,0:T(8,128)}, f32[32,16,128]{2,1,0:T(8,128)S(1)}, u32[]{:S(2)}, u32[]{:S(2)}) collective-permute-start(f32[32,16,128]{2,1,0:T(8,128)} %get-tuple-element.65), channel_id=1, source_target_pairs={{0,4},{1,5},{2,6},{3,7},{8,12},{9,13},{10,14},{11,15},{16,20},{17,... | collective-permute-start | bytes 786440 | tf_op jit(solution)/shard_map/ppermute | solution.py:504
  253.7 36.6 %collective-permute-start.25 = (f32[32,16,128]{2,1,0:T(8,128)}, f32[32,16,128]{2,1,0:T(8,128)}, u32[]{:S(2)}, u32[]{:S(2)}) collective-permute-start(f32[32,16,128]{2,1,0:T(8,128)} %get-tuple-element.66), channel_id=1, source_target_pairs={{0,68},{1,69},{2,70},{3,71},{8,76},{9,77},{10,78},{11,79},{16,84},... | collective-permute-start | bytes 786440 | tf_op jit(solution)/shard_map/ppermute | solution.py:504
  254.7 40.5 %collective-permute-start.26 = (f32[32,16,128]{2,1,0:T(8,128)}, f32[32,16,128]{2,1,0:T(8,128)}, u32[]{:S(2)}, u32[]{:S(2)}) collective-permute-start(f32[32,16,128]{2,1,0:T(8,128)} %get-tuple-element.67), channel_id=1, source_target_pairs={{0,132},{1,133},{2,134},{3,135},{8,140},{9,141},{10,142},{11,143},... | collective-permute-start | bytes 786440 | tf_op jit(solution)/shard_map/ppermute | solution.py:504
  266.7 34.0 %copy-start.3 = (f32[32,16,128]{2,1,0:T(8,128)S(1)}, f32[32,16,128]{2,1,0:T(8,128)}, u32[]{:S(2)}) copy-start(f32[32,16,128]{2,1,0:T(8,128)} %get-tuple-element.61.refs_0_) | copy-start | bytes 786436
  266.7 34.0 %collective-permute-start.27 = (f32[32,16,128]{2,1,0:T(8,128)}, f32[32,16,128]{2,1,0:T(8,128)}, u32[]{:S(2)}, u32[]{:S(2)}) collective-permute-start(f32[32,16,128]{2,1,0:T(8,128)} %get-tuple-element.68), channel_id=1, source_target_pairs={{0,196},{1,197},{2,198},{3,199},{8,204},{9,205},{10,206},{11,207},... | collective-permute-start | bytes 786440 | tf_op jit(solution)/shard_map/ppermute | solution.py:504

commit v4 on v3

--- a/solution.py
+++ b/solution.py
@@ -497,9 +497,16 @@
     )(rate_index, *operands)
 
 
-def round_ring(parts, sooner=(3, 5)):
+LATER = {"az1": (4, 6, 2, 7, 1), "bz1": (4, 6, 2, 7, 1), "az2": (4, 6, 2, 7, 1), "bz2": (6, 2, 7, 1)}
+
+
+def sooner(name):
+    return tuple(shift for shift in (3, 5, 4) if shift not in LATER[name])
+
+
+def round_ring(parts, name):
     moved = list(parts)
-    for shifts in (sooner, [shift for shift in range(1, RING) if shift not in sooner]):
+    for shifts in (sooner(name), LATER[name]):
         for shift in shifts:
             moved[shift] = lax.ppermute(parts[shift], AXES, ring_pairs(shift))
     return moved
@@ -520,20 +527,20 @@
     fine = [EIGHT, MANY]
 
     a = call(begin_ring, "a1", SENT_RING_MORE, begin + [HELD_MORE, CLASS_ROWS, EIGHT, MANY, ONE, EIGHT], rate, classes, rows)
-    a = round_ring(a)
+    a = round_ring(a, "az1")
     b = call(begin_plane, "b1", SENT_PLANE, begin + [HELD] + ends + [ONE], rate, classes, rows)
     b = in_plane(b)
     b = call(plane_to_ring_first, "b2", SENT_RING, [HELD] + fine, rate, b)
-    b = round_ring(b)
+    b = round_ring(b, "bz1")
     a = call(ring_to_plane_first, "a2", SENT_PLANE_MORE, [HELD_MORE, ROWS] + ends + [ONE], rate, *a)
     a = in_plane(a)
     fitness = a
     a = call(middle_ring, "a3", SENT_RING, [HELD, ROWS, LEFT, RIGHT] + fine + [ONE], rate, a)
-    a = round_ring(a)
+    a = round_ring(a, "az2")
     b = call(middle_plane, "b3", SENT_PLANE, [HELD, ROWS, LEFT, RIGHT] + fine + [ONE], rate, fitness, *b)
     b = in_plane(b)
     b = call(plane_to_ring, "b4", SENT_RING, [HELD] + fine, rate, b)
-    b = round_ring(b, (3, 5, 2, 6))
+    b = round_ring(b, "bz2")
     a = call(ring_to_plane, "a4", SENT_PLANE, [HELD] + fine, rate, *a)
     a = in_plane(a)
     done = jax.ShapeDtypeStruct((RING, PLANE, REST, 128), F32)

time: 306 us -> 306 us (level)
  no operation moved by 1% of the time
where the time goes in v4:
time: 306 us; the launch traced here: 305 us
  waiting for transfers between devices  160 us (52%)
  starting transfers between devices  93.3 us (30%)
  Pallas kernels  42.5 us (14%)
  local copies, waits for them, and re-layouts  9.1 us (3%)
    ppermute x28, waiting for transfers between devices, round_ring(): moved[shift] = lax.ppermute(parts[shift], AXES, ring_pairs(shift))  159 us
    ppermute x28, starting transfers between devices, round_ring(): moved[shift] = lax.ppermute(parts[shift], AXES, ring_pairs(shift))  60.1 us
    pallas_call x10, Pallas kernels, call(): pl.pallas_call(kernel, out_shape=[far(out) for out in outs] if many else...  42.5 us
    all_to_all x4, starting transfers between devices, in_plane(): lax.all_to_all(piece, AXES, split_axis=0, concat_axis=0, tiled=True, axis...  33.2 us
    unnamed x22, local copies, waits for them, and re-layouts  9.1 us
  transfers between devices with their start and end apart: 32, of which 21 were waited for; matrix products, arithmetic and copies ran while one was open for 0% of the time, Pallas kernels for 9%

profile of v4, /device:TPU:1, one launch (start us, length us, event | category | flops | bytes accessed | tf_op | source)
XLA Modules:
  0.0 304.9 jit_solution(4724798201010995147)
XLA Ops:
  0.0 5.2 %shard_map.42 = f32[32,128,128]{2,1,0:T(8,128)} custom-call(s32[2]{0:T(128)} %rate_ref.19, s32[128,128]{1,0:T(8,128)} %bitcast.13, f32[8,1024,128]{2,1,0:T(8,128)} %bitcast.11), custom_call_target="tpu_custom_call" | custom-call | flops 268435456 | bytes 8388608 | tf_op jit(solution)/shard_map/pallas_call | solution.py:487
  5.2 8.6 %all-to-all-start.2 = ((f32[32,128,128]{2,1,0:T(8,128)}), f32[32,128,128]{2,1,0:T(8,128)S(1)}, u32[]{:S(2)}, u32[]{:S(2)}) async-start(f32[32,128,128]{2,1,0:T(8,128)} %shard_map.42), calls=%async_computation.2 | async-start | bytes 4194304 | tf_op jit(solution)/shard_map/all_to_all | solution.py:516
  13.8 5.6 %shard_map.37 = (f32[33,16,128]{2,1,0:T(8,128)}, f32[33,16,128]{2,1,0:T(8,128)}, f32[33,16,128]{2,1,0:T(8,128)}, f32[33,16,128]{2,1,0:T(8,128)}, f32[33,16,128]{...) custom-call(s32[2]{0:T(128)} %rate_ref.19, s32[128,128]{1,0:T(8,128)} %bitcast.14, ...), custom_call_target="tpu_custom_call" | custom-call | flops 268435456 | bytes 8388608 | tf_op jit(solution)/shard_map/pallas_call | solution.py:487
  21.1 3.0 collective-permute-start.1
  24.1 3.8 %collective-permute-start.2 = (f32[33,16,128]{2,1,0:T(8,128)}, f32[33,16,128]{2,1,0:T(8,128)S(1)}, u32[]{:S(2)}, u32[]{:S(2)}) collective-permute-start(f32[33,16,128]{2,1,0:T(8,128)} %get-tuple-element.40), channel_id=1, source_target_pairs={{0,192},{1,193},{2,194},{3,195},{8,200},{9,201},{10,202},{11,203},... | collective-permute-start | bytes 811016 | tf_op jit(solution)/shard_map/ppermute | solution.py:511
  28.3 4.5 %collective-permute-start.4 = (f32[33,16,128]{2,1,0:T(8,128)}, f32[33,16,128]{2,1,0:T(8,128)S(1)}, u32[]{:S(2)}, u32[]{:S(2)}) collective-permute-start(f32[33,16,128]{2,1,0:T(8,128)} %get-tuple-element.42), channel_id=1, source_target_pairs={{0,68},{1,69},{2,70},{3,71},{8,76},{9,77},{10,78},{11,79},{16,84},... | collective-permute-start | bytes 811016 | tf_op jit(solution)/shard_map/ppermute | solution.py:511
  32.8 2.4 collective-permute-start.5
  35.2 4.0 %collective-permute-done.1.refs_2_ = f32[33,16,128]{2,1,0:T(8,128)S(1)} collective-permute-done((f32[33,16,128]{2,1,0:T(8,128)}, f32[33,16,128]{2,1,0:T(8,128)S(1)}, u32[]{:S(2)}, u32[]{:S(2)}) %collective-permute-start.1) | collective-permute-done | bytes 270368 | tf_op jit(solution)/shard_map/ppermute | solution.py:511
  39.2 6.9 %collective-permute-start.6 = (f32[33,16,128]{2,1,0:T(8,128)}, f32[33,16,128]{2,1,0:T(8,128)S(1)}, u32[]{:S(2)}, u32[]{:S(2)}) collective-permute-start(f32[33,16,128]{2,1,0:T(8,128)} %get-tuple-element.44), channel_id=1, source_target_pairs={{0,196},{1,197},{2,198},{3,199},{8,204},{9,205},{10,206},{11,207},... | collective-permute-start | bytes 811016 | tf_op jit(solution)/shard_map/ppermute | solution.py:511
  46.1 15.1 %collective-permute-done.2.refs_3_ = f32[33,16,128]{2,1,0:T(8,128)S(1)} collective-permute-done((f32[33,16,128]{2,1,0:T(8,128)}, f32[33,16,128]{2,1,0:T(8,128)S(1)}, u32[]{:S(2)}, u32[]{:S(2)}) %collective-permute-start.2) | collective-permute-done | bytes 270368 | tf_op jit(solution)/shard_map/ppermute | solution.py:511
  61.2 5.1 %collective-permute-done.3.refs_4_ = f32[33,16,128]{2,1,0:T(8,128)S(1)} collective-permute-done((f32[33,16,128]{2,1,0:T(8,128)}, f32[33,16,128]{2,1,0:T(8,128)S(1)}, u32[]{:S(2)}, u32[]{:S(2)}) %collective-permute-start.3) | collective-permute-done | bytes 270368 | tf_op jit(solution)/shard_map/ppermute | solution.py:511
  66.4 7.8 %collective-permute-done.5.refs_6_ = f32[33,16,128]{2,1,0:T(8,128)S(1)} collective-permute-done((f32[33,16,128]{2,1,0:T(8,128)}, f32[33,16,128]{2,1,0:T(8,128)S(1)}, u32[]{:S(2)}, u32[]{:S(2)}) %collective-permute-start.5) | collective-permute-done | bytes 270368 | tf_op jit(solution)/shard_map/ppermute | solution.py:511
  74.2 2.4 collective-permute-done.6.refs_7_
  77.6 3.0 shard_map.38
  81.9 8.5 %all-to-all-start = ((f32[32,136,128]{2,1,0:T(8,128)}), f32[32,136,128]{2,1,0:T(8,128)S(1)}, u32[]{:S(2)}, u32[]{:S(2)}) async-start(f32[32,136,128]{2,1,0:T(8,128)} %shard_map.38), calls=%async_computation | async-start | bytes 4456448 | tf_op jit(solution)/shard_map/all_to_all | solution.py:516
  92.0 2.8 shard_map.43
  94.8 3.4 %collective-permute-start.14 = (f32[32,16,128]{2,1,0:T(8,128)}, f32[32,16,128]{2,1,0:T(8,128)S(1)}, u32[]{:S(2)}, u32[]{:S(2)}) collective-permute-start(f32[32,16,128]{2,1,0:T(8,128)} %get-tuple-element.54), channel_id=1, source_target_pairs={{0,64},{1,65},{2,66},{3,67},{8,72},{9,73},{10,74},{11,75},{16,80},... | collective-permute-start | bytes 786440 | tf_op jit(solution)/shard_map/ppermute | solution.py:511
  99.3 4.5 %collective-permute-start.17 = (f32[32,16,128]{2,1,0:T(8,128)}, f32[32,16,128]{2,1,0:T(8,128)S(1)}, u32[]{:S(2)}, u32[]{:S(2)}) collective-permute-start(f32[32,16,128]{2,1,0:T(8,128)} %get-tuple-element.57), channel_id=1, source_target_pairs={{0,4},{1,5},{2,6},{3,7},{8,12},{9,13},{10,14},{11,15},{16,20},{17,... | collective-permute-start | bytes 786440 | tf_op jit(solution)/shard_map/ppermute | solution.py:511
  105.0 2.1 collective-permute-start.19
  107.1 9.7 %collective-permute-done.15.refs_2_ = f32[32,16,128]{2,1,0:T(8,128)S(1)} collective-permute-done((f32[32,16,128]{2,1,0:T(8,128)}, f32[32,16,128]{2,1,0:T(8,128)S(1)}, u32[]{:S(2)}, u32[]{:S(2)}) %collective-permute-start.15) | collective-permute-done | bytes 262176 | tf_op jit(solution)/shard_map/ppermute | solution.py:511
  116.8 9.9 %collective-permute-done.16.refs_3_ = f32[32,16,128]{2,1,0:T(8,128)S(1)} collective-permute-done((f32[32,16,128]{2,1,0:T(8,128)}, f32[32,16,128]{2,1,0:T(8,128)S(1)}, u32[]{:S(2)}, u32[]{:S(2)}) %collective-permute-start.16) | collective-permute-done | bytes 262176 | tf_op jit(solution)/shard_map/ppermute | solution.py:511
  126.7 13.9 %collective-permute-done.17.refs_4_ = f32[32,16,128]{2,1,0:T(8,128)S(1)} collective-permute-done((f32[32,16,128]{2,1,0:T(8,128)}, f32[32,16,128]{2,1,0:T(8,128)S(1)}, u32[]{:S(2)}, u32[]{:S(2)}) %collective-permute-start.17) | collective-permute-done | bytes 262176 | tf_op jit(solution)/shard_map/ppermute | solution.py:511
  140.7 4.7 %collective-permute-done.19.refs_6_ = f32[32,16,128]{2,1,0:T(8,128)S(1)} collective-permute-done((f32[32,16,128]{2,1,0:T(8,128)}, f32[32,16,128]{2,1,0:T(8,128)S(1)}, u32[]{:S(2)}, u32[]{:S(2)}) %collective-permute-start.19) | collective-permute-done | bytes 262176 | tf_op jit(solution)/shard_map/ppermute | solution.py:511
  146.0 4.8 %collective-permute-done.20.refs_7_ = f32[32,16,128]{2,1,0:T(8,128)S(1)} collective-permute-done((f32[32,16,128]{2,1,0:T(8,128)}, f32[32,16,128]{2,1,0:T(8,128)S(1)}, u32[]{:S(2)}, u32[]{:S(2)}) %collective-permute-start.20) | collective-permute-done | bytes 262176 | tf_op jit(solution)/shard_map/ppermute | solution.py:511
  154.4 6.9 %shard_map.44 = f32[32,128,128]{2,1,0:T(8,128)} custom-call(s32[2]{0:T(128)S(1)} %copy-done.10, f32[32,136,128]{2,1,0:T(8,128)S(1)} %all-to-all-done.x_ref.fitness_ref, f32[32,16,128]{2,1,0:T(8,128)S(1)} %copy-done.4, f32[32,16,128]{2,1,0:T(8,128)S(1)} %collective-permute-done.14.refs_1_, f32[32,16,128]{2,1,0:T(8,128)S(1)} %collective-permute-done.15.refs_2_, ...), custom_call_target="tpu_custom_call" | custom-call | flops 268435456 | bytes 8388608 | tf_op jit(solution)/shard_map/pallas_call | solution.py:487
  161.4 7.7 %all-to-all-start.3 = ((f32[32,128,128]{2,1,0:T(8,128)}), f32[32,128,128]{2,1,0:T(8,128)}, u32[]{:S(2)}, u32[]{:S(2)}) async-start(f32[32,128,128]{2,1,0:T(8,128)} %shard_map.44), calls=%async_computation.3 | async-start | bytes 4194304 | tf_op jit(solution)/shard_map/all_to_all | solution.py:516
  169.1 6.4 %shard_map.39 = (f32[32,16,128]{2,1,0:T(8,128)}, f32[32,16,128]{2,1,0:T(8,128)}, f32[32,16,128]{2,1,0:T(8,128)}, f32[32,16,128]{2,1,0:T(8,128)}, f32[32,16,128]{...) custom-call(s32[2]{0:T(128)S(1)} %copy-done.10, ...), custom_call_target="tpu_custom_call" | custom-call | flops 268435456 | bytes 8388608 | tf_op jit(solution)/shard_map/pallas_call | solution.py:487
  177.3 3.3 %collective-permute-start.9 = (f32[32,16,128]{2,1,0:T(8,128)}, f32[32,16,128]{2,1,0:T(8,128)S(1)}, u32[]{:S(2)}, u32[]{:S(2)}) collective-permute-start(f32[32,16,128]{2,1,0:T(8,128)} %get-tuple-element.48), channel_id=1, source_target_pairs={{0,192},{1,193},{2,194},{3,195},{8,200},{9,201},{10,202},{11,203},... | collective-permute-start | bytes 786440 | tf_op jit(solution)/shard_map/ppermute | solution.py:511
  181.5 4.1 %collective-permute-start.11 = (f32[32,16,128]{2,1,0:T(8,128)}, f32[32,16,128]{2,1,0:T(8,128)S(1)}, u32[]{:S(2)}, u32[]{:S(2)}) collective-permute-start(f32[32,16,128]{2,1,0:T(8,128)} %get-tuple-element.50), channel_id=1, source_target_pairs={{0,68},{1,69},{2,70},{3,71},{8,76},{9,77},{10,78},{11,79},{16,84},... | collective-permute-start | bytes 786440 | tf_op jit(solution)/shard_map/ppermute | solution.py:511
  185.6 2.7 collective-permute-start.12
  188.3 9.0 %collective-permute-done.8.refs_2_ = f32[32,16,128]{2,1,0:T(8,128)S(1)} collective-permute-done((f32[32,16,128]{2,1,0:T(8,128)}, f32[32,16,128]{2,1,0:T(8,128)S(1)}, u32[]{:S(2)}, u32[]{:S(2)}) %collective-permute-start.8) | collective-permute-done | bytes 262176 | tf_op jit(solution)/shard_map/ppermute | solution.py:511
  197.3 15.0 %collective-permute-done.9.refs_3_ = f32[32,16,128]{2,1,0:T(8,128)S(1)} collective-permute-done((f32[32,16,128]{2,1,0:T(8,128)}, f32[32,16,128]{2,1,0:T(8,128)S(1)}, u32[]{:S(2)}, u32[]{:S(2)}) %collective-permute-start.9) | collective-permute-done | bytes 262176 | tf_op jit(solution)/shard_map/ppermute | solution.py:511
  212.3 10.1 %collective-permute-done.10.refs_4_ = f32[32,16,128]{2,1,0:T(8,128)S(1)} collective-permute-done((f32[32,16,128]{2,1,0:T(8,128)}, f32[32,16,128]{2,1,0:T(8,128)S(1)}, u32[]{:S(2)}, u32[]{:S(2)}) %collective-permute-start.10) | collective-permute-done | bytes 262176 | tf_op jit(solution)/shard_map/ppermute | solution.py:511
  222.4 3.7 %collective-permute-done.12.refs_6_ = f32[32,16,128]{2,1,0:T(8,128)S(1)} collective-permute-done((f32[32,16,128]{2,1,0:T(8,128)}, f32[32,16,128]{2,1,0:T(8,128)S(1)}, u32[]{:S(2)}, u32[]{:S(2)}) %collective-permute-start.12) | collective-permute-done | bytes 262176 | tf_op jit(solution)/shard_map/ppermute | solution.py:511
  226.1 2.3 collective-permute-done.13.refs_7_
  229.4 2.8 shard_map.40
  232.2 8.5 %all-to-all-start.1 = ((f32[32,128,128]{2,1,0:T(8,128)}), f32[32,128,128]{2,1,0:T(8,128)S(1)}, u32[]{:S(2)}, u32[]{:S(2)}) async-start(f32[32,128,128]{2,1,0:T(8,128)} %shard_map.40), calls=%async_computation.1 | async-start | bytes 4194304 | tf_op jit(solution)/shard_map/all_to_all | solution.py:516
  240.6 4.0 %shard_map.45 = (f32[32,16,128]{2,1,0:T(8,128)}, f32[32,16,128]{2,1,0:T(8,128)}, f32[32,16,128]{2,1,0:T(8,128)}, f32[32,16,128]{2,1,0:T(8,128)}, f32[32,16,128]{...) custom-call(s32[2]{0:T(128)S(1)} %copy-done.10, ...), custom_call_target="tpu_custom_call" | custom-call | flops 268435456 | bytes 8388608 | tf_op jit(solution)/shard_map/pallas_call | solution.py:487
  244.6 3.3 %collective-permute-start.21 = (f32[32,16,128]{2,1,0:T(8,128)}, f32[32,16,128]{2,1,0:T(8,128)S(1)}, u32[]{:S(2)}, u32[]{:S(2)}) collective-permute-start(f32[32,16,128]{2,1,0:T(8,128)} %get-tuple-element.62), channel_id=1, source_target_pairs={{0,64},{1,65},{2,66},{3,67},{8,72},{9,73},{10,74},{11,75},{16,80},... | collective-permute-start | bytes 786440 | tf_op jit(solution)/shard_map/ppermute | solution.py:511
  249.0 4.6 %collective-permute-start.24 = (f32[32,16,128]{2,1,0:T(8,128)}, f32[32,16,128]{2,1,0:T(8,128)S(1)}, u32[]{:S(2)}, u32[]{:S(2)}) collective-permute-start(f32[32,16,128]{2,1,0:T(8,128)} %get-tuple-element.65), channel_id=1, source_target_pairs={{0,4},{1,5},{2,6},{3,7},{8,12},{9,13},{10,14},{11,15},{16,20},{17,... | collective-permute-start | bytes 786440 | tf_op jit(solution)/shard_map/ppermute | solution.py:511
  254.7 2.2 collective-permute-start.26
  256.9 9.8 %collective-permute-done.22.refs_2_ = f32[32,16,128]{2,1,0:T(8,128)S(1)} collective-permute-done((f32[32,16,128]{2,1,0:T(8,128)}, f32[32,16,128]{2,1,0:T(8,128)S(1)}, u32[]{:S(2)}, u32[]{:S(2)}) %collective-permute-start.22) | collective-permute-done | bytes 262176 | tf_op jit(solution)/shard_map/ppermute | solution.py:511
  267.7 1.8 shard_map.41.other_ref
  269.5 6.7 %collective-permute-done.23.refs_3_ = f32[32,16,128]{2,1,0:T(8,128)S(1)} collective-permute-done((f32[32,16,128]{2,1,0:T(8,128)}, f32[32,16,128]{2,1,0:T(8,128)S(1)}, u32[]{:S(2)}, u32[]{:S(2)}) %collective-permute-start.23) | collective-permute-done | bytes 262176 | tf_op jit(solution)/shard_map/ppermute | solution.py:511
  276.2 14.0 %collective-permute-done.24.refs_4_ = f32[32,16,128]{2,1,0:T(8,128)S(1)} collective-permute-done((f32[32,16,128]{2,1,0:T(8,128)}, f32[32,16,128]{2,1,0:T(8,128)S(1)}, u32[]{:S(2)}, u32[]{:S(2)}) %collective-permute-start.24) | collective-permute-done | bytes 262176 | tf_op jit(solution)/shard_map/ppermute | solution.py:511
  290.2 5.0 %collective-permute-done.26.refs_6_ = f32[32,16,128]{2,1,0:T(8,128)} collective-permute-done((f32[32,16,128]{2,1,0:T(8,128)}, f32[32,16,128]{2,1,0:T(8,128)}, u32[]{:S(2)}, u32[]{:S(2)}) %collective-permute-start.26) | collective-permute-done | bytes 262176 | tf_op jit(solution)/shard_map/ppermute | solution.py:511
  295.3 5.4 %collective-permute-done.27.refs_7_ = f32[32,16,128]{2,1,0:T(8,128)} collective-permute-done((f32[32,16,128]{2,1,0:T(8,128)}, f32[32,16,128]{2,1,0:T(8,128)}, u32[]{:S(2)}, u32[]{:S(2)}) %collective-permute-start.27) | collective-permute-done | bytes 262176 | tf_op jit(solution)/shard_map/ppermute | solution.py:511
  300.7 4.1 %shard_map.46 = f32[8,1024,128]{2,1,0:T(8,128)} custom-call(s32[2]{0:T(128)S(1)} %copy-done.10, f32[8,32,16,128]{3,2,1,0:T(8,128)S(1)} %shard_map.41.other_ref, f32[32,16,128]{2,1,0:T(8,128)S(1)} %copy-done.3, f32[32,16,128]{2,1,0:T(8,128)S(1)} %collective-permute-done.21.refs_1_, f32[32,16,128]{2,1,0:T(8,128)S(1)} %collective-permute-done.22.refs_2_, ...), custom_call_target="tpu_custom_call" | custom-call | flops 268435456 | bytes 8388608 | tf_op jit(solution)/shard_map/pallas_call | solution.py:487
  (48 shorter events, 19.5 us)
Async XLA Ops:
  5.2 75.4 %all-to-all-start.2 = ((f32[32,128,128]{2,1,0:T(8,128)}), f32[32,128,128]{2,1,0:T(8,128)S(1)}, u32[]{:S(2)}, u32[]{:S(2)}) async-start(f32[32,128,128]{2,1,0:T(8,128)} %shard_map.42), calls=%async_computation.2 | async-start | bytes 4194304 | tf_op jit(solution)/shard_map/all_to_all | solution.py:516
  13.8 62.8 %copy-start.10 = (s32[2]{0:T(128)S(1)}, s32[2]{0:T(128)}, u32[]{:S(2)}) copy-start(s32[2]{0:T(128)} %rate_ref.19) | copy-start | bytes 28
  19.4 13.4 %collective-permute-start = (f32[33,16,128]{2,1,0:T(8,128)}, f32[33,16,128]{2,1,0:T(8,128)S(1)}, u32[]{:S(2)}, u32[]{:S(2)}) collective-permute-start(f32[33,16,128]{2,1,0:T(8,128)} %get-tuple-element.38), channel_id=1, source_target_pairs={{0,64},{1,65},{2,66},{3,67},{8,72},{9,73},{10,74},{11,75},{16,80},... | collective-permute-start | bytes 811016 | tf_op jit(solution)/shard_map/ppermute | solution.py:511
  21.1 18.1 %collective-permute-start.1 = (f32[33,16,128]{2,1,0:T(8,128)}, f32[33,16,128]{2,1,0:T(8,128)S(1)}, u32[]{:S(2)}, u32[]{:S(2)}) collective-permute-start(f32[33,16,128]{2,1,0:T(8,128)} %get-tuple-element.39), channel_id=1, source_target_pairs={{0,128},{1,129},{2,130},{3,131},{8,136},{9,137},{10,138},{11,139},... | collective-permute-start | bytes 811016 | tf_op jit(solution)/shard_map/ppermute | solution.py:511
  24.1 37.1 %collective-permute-start.2 = (f32[33,16,128]{2,1,0:T(8,128)}, f32[33,16,128]{2,1,0:T(8,128)S(1)}, u32[]{:S(2)}, u32[]{:S(2)}) collective-permute-start(f32[33,16,128]{2,1,0:T(8,128)} %get-tuple-element.40), channel_id=1, source_target_pairs={{0,192},{1,193},{2,194},{3,195},{8,200},{9,201},{10,202},{11,203},... | collective-permute-start | bytes 811016 | tf_op jit(solution)/shard_map/ppermute | solution.py:511
  27.9 38.5 %collective-permute-start.3 = (f32[33,16,128]{2,1,0:T(8,128)}, f32[33,16,128]{2,1,0:T(8,128)S(1)}, u32[]{:S(2)}, u32[]{:S(2)}) collective-permute-start(f32[33,16,128]{2,1,0:T(8,128)} %get-tuple-element.41), channel_id=1, source_target_pairs={{0,4},{1,5},{2,6},{3,7},{8,12},{9,13},{10,14},{11,15},{16,20},{17,... | collective-permute-start | bytes 811016 | tf_op jit(solution)/shard_map/ppermute | solution.py:511
  28.3 38.0 %collective-permute-start.4 = (f32[33,16,128]{2,1,0:T(8,128)}, f32[33,16,128]{2,1,0:T(8,128)S(1)}, u32[]{:S(2)}, u32[]{:S(2)}) collective-permute-start(f32[33,16,128]{2,1,0:T(8,128)} %get-tuple-element.42), channel_id=1, source_target_pairs={{0,68},{1,69},{2,70},{3,71},{8,76},{9,77},{10,78},{11,79},{16,84},... | collective-permute-start | bytes 811016 | tf_op jit(solution)/shard_map/ppermute | solution.py:511
  32.8 41.4 %collective-permute-start.5 = (f32[33,16,128]{2,1,0:T(8,128)}, f32[33,16,128]{2,1,0:T(8,128)S(1)}, u32[]{:S(2)}, u32[]{:S(2)}) collective-permute-start(f32[33,16,128]{2,1,0:T(8,128)} %get-tuple-element.43), channel_id=1, source_target_pairs={{0,132},{1,133},{2,134},{3,135},{8,140},{9,141},{10,142},{11,143},... | collective-permute-start | bytes 811016 | tf_op jit(solution)/shard_map/ppermute | solution.py:511
  39.2 37.4 %collective-permute-start.6 = (f32[33,16,128]{2,1,0:T(8,128)}, f32[33,16,128]{2,1,0:T(8,128)S(1)}, u32[]{:S(2)}, u32[]{:S(2)}) collective-permute-start(f32[33,16,128]{2,1,0:T(8,128)} %get-tuple-element.44), channel_id=1, source_target_pairs={{0,196},{1,197},{2,198},{3,199},{8,204},{9,205},{10,206},{11,207},... | collective-permute-start | bytes 811016 | tf_op jit(solution)/shard_map/ppermute | solution.py:511
  76.6 1.0 copy-start.2
  80.6 1.3 copy-start
  81.9 69.7 %all-to-all-start = ((f32[32,136,128]{2,1,0:T(8,128)}), f32[32,136,128]{2,1,0:T(8,128)S(1)}, u32[]{:S(2)}, u32[]{:S(2)}) async-start(f32[32,136,128]{2,1,0:T(8,128)} %shard_map.38), calls=%async_computation | async-start | bytes 4456448 | tf_op jit(solution)/shard_map/all_to_all | solution.py:516
  90.4 1.6 copy-start.1
  94.8 10.2 %collective-permute-start.14 = (f32[32,16,128]{2,1,0:T(8,128)}, f32[32,16,128]{2,1,0:T(8,128)S(1)}, u32[]{:S(2)}, u32[]{:S(2)}) collective-permute-start(f32[32,16,128]{2,1,0:T(8,128)} %get-tuple-element.54), channel_id=1, source_target_pairs={{0,64},{1,65},{2,66},{3,67},{8,72},{9,73},{10,74},{11,75},{16,80},... | collective-permute-start | bytes 786440 | tf_op jit(solution)/shard_map/ppermute | solution.py:511
  98.2 18.6 %collective-permute-start.15 = (f32[32,16,128]{2,1,0:T(8,128)}, f32[32,16,128]{2,1,0:T(8,128)S(1)}, u32[]{:S(2)}, u32[]{:S(2)}) collective-permute-start(f32[32,16,128]{2,1,0:T(8,128)} %get-tuple-element.55), channel_id=1, source_target_pairs={{0,128},{1,129},{2,130},{3,131},{8,136},{9,137},{10,138},{11,139},... | collective-permute-start | bytes 786440 | tf_op jit(solution)/shard_map/ppermute | solution.py:511
  99.0 27.7 %collective-permute-start.16 = (f32[32,16,128]{2,1,0:T(8,128)}, f32[32,16,128]{2,1,0:T(8,128)S(1)}, u32[]{:S(2)}, u32[]{:S(2)}) collective-permute-start(f32[32,16,128]{2,1,0:T(8,128)} %get-tuple-element.56), channel_id=1, source_target_pairs={{0,192},{1,193},{2,194},{3,195},{8,200},{9,201},{10,202},{11,203},... | collective-permute-start | bytes 786440 | tf_op jit(solution)/shard_map/ppermute | solution.py:511
  99.3 41.3 %collective-permute-start.17 = (f32[32,16,128]{2,1,0:T(8,128)}, f32[32,16,128]{2,1,0:T(8,128)S(1)}, u32[]{:S(2)}, u32[]{:S(2)}) collective-permute-start(f32[32,16,128]{2,1,0:T(8,128)} %get-tuple-element.57), channel_id=1, source_target_pairs={{0,4},{1,5},{2,6},{3,7},{8,12},{9,13},{10,14},{11,15},{16,20},{17,... | collective-permute-start | bytes 786440 | tf_op jit(solution)/shard_map/ppermute | solution.py:511
  103.8 36.8 %collective-permute-start.18 = (f32[32,16,128]{2,1,0:T(8,128)}, f32[32,16,128]{2,1,0:T(8,128)S(1)}, u32[]{:S(2)}, u32[]{:S(2)}) collective-permute-start(f32[32,16,128]{2,1,0:T(8,128)} %get-tuple-element.58), channel_id=1, source_target_pairs={{0,68},{1,69},{2,70},{3,71},{8,76},{9,77},{10,78},{11,79},{16,84},... | collective-permute-start | bytes 786440 | tf_op jit(solution)/shard_map/ppermute | solution.py:511
  105.0 40.4 %collective-permute-start.19 = (f32[32,16,128]{2,1,0:T(8,128)}, f32[32,16,128]{2,1,0:T(8,128)S(1)}, u32[]{:S(2)}, u32[]{:S(2)}) collective-permute-start(f32[32,16,128]{2,1,0:T(8,128)} %get-tuple-element.59), channel_id=1, source_target_pairs={{0,132},{1,133},{2,134},{3,135},{8,140},{9,141},{10,142},{11,143},... | collective-permute-start | bytes 786440 | tf_op jit(solution)/shard_map/ppermute | solution.py:511
  116.8 34.1 %collective-permute-start.20 = (f32[32,16,128]{2,1,0:T(8,128)}, f32[32,16,128]{2,1,0:T(8,128)S(1)}, u32[]{:S(2)}, u32[]{:S(2)}) collective-permute-start(f32[32,16,128]{2,1,0:T(8,128)} %get-tuple-element.60), channel_id=1, source_target_pairs={{0,196},{1,197},{2,198},{3,199},{8,204},{9,205},{10,206},{11,207},... | collective-permute-start | bytes 786440 | tf_op jit(solution)/shard_map/ppermute | solution.py:511
  145.3 0.7 copy-start.6
  150.9 0.7 copy-start.8
  151.6 1.0 copy-start.4
  152.5 0.9 copy-start.7
  153.5 0.9 copy-start.9
  161.4 70.8 %all-to-all-start.3 = ((f32[32,128,128]{2,1,0:T(8,128)}), f32[32,128,128]{2,1,0:T(8,128)}, u32[]{:S(2)}, u32[]{:S(2)}) async-start(f32[32,128,128]{2,1,0:T(8,128)} %shard_map.44), calls=%async_computation.3 | async-start | bytes 4194304 | tf_op jit(solution)/shard_map/all_to_all | solution.py:516
  175.5 10.2 %collective-permute-start.7 = (f32[32,16,128]{2,1,0:T(8,128)}, f32[32,16,128]{2,1,0:T(8,128)S(1)}, u32[]{:S(2)}, u32[]{:S(2)}) collective-permute-start(f32[32,16,128]{2,1,0:T(8,128)} %get-tuple-element.46), channel_id=1, source_target_pairs={{0,64},{1,65},{2,66},{3,67},{8,72},{9,73},{10,74},{11,75},{16,80},... | collective-permute-start | bytes 786440 | tf_op jit(solution)/shard_map/ppermute | solution.py:511
  175.8 21.5 %collective-permute-start.8 = (f32[32,16,128]{2,1,0:T(8,128)}, f32[32,16,128]{2,1,0:T(8,128)S(1)}, u32[]{:S(2)}, u32[]{:S(2)}) collective-permute-start(f32[32,16,128]{2,1,0:T(8,128)} %get-tuple-element.47), channel_id=1, source_target_pairs={{0,128},{1,129},{2,130},{3,131},{8,136},{9,137},{10,138},{11,139},... | collective-permute-start | bytes 786440 | tf_op jit(solution)/shard_map/ppermute | solution.py:511
  177.3 35.0 %collective-permute-start.9 = (f32[32,16,128]{2,1,0:T(8,128)}, f32[32,16,128]{2,1,0:T(8,128)S(1)}, u32[]{:S(2)}, u32[]{:S(2)}) collective-permute-start(f32[32,16,128]{2,1,0:T(8,128)} %get-tuple-element.48), channel_id=1, source_target_pairs={{0,192},{1,193},{2,194},{3,195},{8,200},{9,201},{10,202},{11,203},... | collective-permute-start | bytes 786440 | tf_op jit(solution)/shard_map/ppermute | solution.py:511
  180.7 41.7 %collective-permute-start.10 = (f32[32,16,128]{2,1,0:T(8,128)}, f32[32,16,128]{2,1,0:T(8,128)S(1)}, u32[]{:S(2)}, u32[]{:S(2)}) collective-permute-start(f32[32,16,128]{2,1,0:T(8,128)} %get-tuple-element.49), channel_id=1, source_target_pairs={{0,4},{1,5},{2,6},{3,7},{8,12},{9,13},{10,14},{11,15},{16,20},{17,... | collective-permute-start | bytes 786440 | tf_op jit(solution)/shard_map/ppermute | solution.py:511
  181.5 40.8 %collective-permute-start.11 = (f32[32,16,128]{2,1,0:T(8,128)}, f32[32,16,128]{2,1,0:T(8,128)S(1)}, u32[]{:S(2)}, u32[]{:S(2)}) collective-permute-start(f32[32,16,128]{2,1,0:T(8,128)} %get-tuple-element.50), channel_id=1, source_target_pairs={{0,68},{1,69},{2,70},{3,71},{8,76},{9,77},{10,78},{11,79},{16,84},... | collective-permute-start | bytes 786440 | tf_op jit(solution)/shard_map/ppermute | solution.py:511
  185.6 40.5 %collective-permute-start.12 = (f32[32,16,128]{2,1,0:T(8,128)}, f32[32,16,128]{2,1,0:T(8,128)S(1)}, u32[]{:S(2)}, u32[]{:S(2)}) collective-permute-start(f32[32,16,128]{2,1,0:T(8,128)} %get-tuple-element.51), channel_id=1, source_target_pairs={{0,132},{1,133},{2,134},{3,135},{8,140},{9,141},{10,142},{11,143},... | collective-permute-start | bytes 786440 | tf_op jit(solution)/shard_map/ppermute | solution.py:511
  197.3 31.1 %collective-permute-start.13 = (f32[32,16,128]{2,1,0:T(8,128)}, f32[32,16,128]{2,1,0:T(8,128)S(1)}, u32[]{:S(2)}, u32[]{:S(2)}) collective-permute-start(f32[32,16,128]{2,1,0:T(8,128)} %get-tuple-element.52), channel_id=1, source_target_pairs={{0,196},{1,197},{2,198},{3,199},{8,204},{9,205},{10,206},{11,207},... | collective-permute-start | bytes 786440 | tf_op jit(solution)/shard_map/ppermute | solution.py:511
  228.4 0.9 copy-start.5
  232.2 35.5 %all-to-all-start.1 = ((f32[32,128,128]{2,1,0:T(8,128)}), f32[32,128,128]{2,1,0:T(8,128)S(1)}, u32[]{:S(2)}, u32[]{:S(2)}) async-start(f32[32,128,128]{2,1,0:T(8,128)} %shard_map.40), calls=%async_computation.1 | async-start | bytes 4194304 | tf_op jit(solution)/shard_map/all_to_all | solution.py:516
  244.6 10.1 %collective-permute-start.21 = (f32[32,16,128]{2,1,0:T(8,128)}, f32[32,16,128]{2,1,0:T(8,128)S(1)}, u32[]{:S(2)}, u32[]{:S(2)}) collective-permute-start(f32[32,16,128]{2,1,0:T(8,128)} %get-tuple-element.62), channel_id=1, source_target_pairs={{0,64},{1,65},{2,66},{3,67},{8,72},{9,73},{10,74},{11,75},{16,80},... | collective-permute-start | bytes 786440 | tf_op jit(solution)/shard_map/ppermute | solution.py:511
  247.9 18.8 %collective-permute-start.22 = (f32[32,16,128]{2,1,0:T(8,128)}, f32[32,16,128]{2,1,0:T(8,128)S(1)}, u32[]{:S(2)}, u32[]{:S(2)}) collective-permute-start(f32[32,16,128]{2,1,0:T(8,128)} %get-tuple-element.63), channel_id=1, source_target_pairs={{0,128},{1,129},{2,130},{3,131},{8,136},{9,137},{10,138},{11,139},... | collective-permute-start | bytes 786440 | tf_op jit(solution)/shard_map/ppermute | solution.py:511
  248.9 27.3 %collective-permute-start.23 = (f32[32,16,128]{2,1,0:T(8,128)}, f32[32,16,128]{2,1,0:T(8,128)S(1)}, u32[]{:S(2)}, u32[]{:S(2)}) collective-permute-start(f32[32,16,128]{2,1,0:T(8,128)} %get-tuple-element.64), channel_id=1, source_target_pairs={{0,192},{1,193},{2,194},{3,195},{8,200},{9,201},{10,202},{11,203},... | collective-permute-start | bytes 786440 | tf_op jit(solution)/shard_map/ppermute | solution.py:511
  249.0 41.2 %collective-permute-start.24 = (f32[32,16,128]{2,1,0:T(8,128)}, f32[32,16,128]{2,1,0:T(8,128)S(1)}, u32[]{:S(2)}, u32[]{:S(2)}) collective-permute-start(f32[32,16,128]{2,1,0:T(8,128)} %get-tuple-element.65), channel_id=1, source_target_pairs={{0,4},{1,5},{2,6},{3,7},{8,12},{9,13},{10,14},{11,15},{16,20},{17,... | collective-permute-start | bytes 786440 | tf_op jit(solution)/shard_map/ppermute | solution.py:511
  253.7 36.6 %collective-permute-start.25 = (f32[32,16,128]{2,1,0:T(8,128)}, f32[32,16,128]{2,1,0:T(8,128)}, u32[]{:S(2)}, u32[]{:S(2)}) collective-permute-start(f32[32,16,128]{2,1,0:T(8,128)} %get-tuple-element.66), channel_id=1, source_target_pairs={{0,68},{1,69},{2,70},{3,71},{8,76},{9,77},{10,78},{11,79},{16,84},... | collective-permute-start | bytes 786440 | tf_op jit(solution)/shard_map/ppermute | solution.py:511
  254.7 40.5 %collective-permute-start.26 = (f32[32,16,128]{2,1,0:T(8,128)}, f32[32,16,128]{2,1,0:T(8,128)}, u32[]{:S(2)}, u32[]{:S(2)}) collective-permute-start(f32[32,16,128]{2,1,0:T(8,128)} %get-tuple-element.67), channel_id=1, source_target_pairs={{0,132},{1,133},{2,134},{3,135},{8,140},{9,141},{10,142},{11,143},... | collective-permute-start | bytes 786440 | tf_op jit(solution)/shard_map/ppermute | solution.py:511
  266.7 34.0 %copy-start.3 = (f32[32,16,128]{2,1,0:T(8,128)S(1)}, f32[32,16,128]{2,1,0:T(8,128)}, u32[]{:S(2)}) copy-start(f32[32,16,128]{2,1,0:T(8,128)} %get-tuple-element.61.refs_0_) | copy-start | bytes 786436
  266.7 34.0 %collective-permute-start.27 = (f32[32,16,128]{2,1,0:T(8,128)}, f32[32,16,128]{2,1,0:T(8,128)}, u32[]{:S(2)}, u32[]{:S(2)}) collective-permute-start(f32[32,16,128]{2,1,0:T(8,128)} %get-tuple-element.68), channel_id=1, source_target_pairs={{0,196},{1,197},{2,198},{3,199},{8,204},{9,205},{10,206},{11,207},... | collective-permute-start | bytes 786440 | tf_op jit(solution)/shard_map/ppermute | solution.py:511

commit v5 on v4

--- a/solution.py
+++ b/solution.py
@@ -82,21 +82,21 @@
 
 
 def left_matrix(chance):
-    high, low = crossing(256, pick(chance, [7, 8, 9, 10] + PLANE_AWAY[:4]))
+    high, low = crossing(128, pick(chance, [7, 8, 9, 10] + PLANE_AWAY[:3]))
     return jnp.concatenate([high, high, low], axis=1)
 
 
 def mix_blocks(blocks, left, right, chance):
     stacks = []
     for block in blocks:
-        high, low = halves(jnp.concatenate([block[:256], block[256:]], axis=1))
+        wide = jnp.concatenate([block[128 * at : 128 * at + 128] for at in range(4)], axis=1)
+        high, low = halves(wide)
         stacks.append(jnp.concatenate([high, low, high], axis=0))
     mixed = [jnp.dot(left, stack, preferred_element_type=F32) for stack in stacks]
     pairs = []
     for both in mixed:
-        flow = chance * (both[:, 128:] - both[:, :128])
-        tall = jnp.concatenate([both[:, :128] + flow, both[:, 128:] - flow], axis=0)
-        pairs.append(jnp.concatenate(halves(tall), axis=1))
+        quarters = mix_bits([both[:, 128 * at : 128 * at + 128] for at in range(4)], chance)
+        pairs.append(jnp.concatenate(halves(jnp.concatenate(quarters, axis=0)), axis=1))
     mixed = [jnp.dot(pair, right, preferred_element_type=F32) for pair in pairs]
     return [both[:, :128] + both[:, 128:] for both in mixed]
 
@@ -317,11 +317,11 @@
     rows_copy.wait()
 
 
-TOGETHER = 4
+TOGETHER = 8
 
 
 def apply_middle(held, rows_held, first_ring, chance, left_ref, right_ref):
-    left, right, across = left_ref[...], right_ref[...], chance[PLANE_AWAY[4]]
+    left, right, across = left_ref[...], right_ref[...], pick(chance, PLANE_AWAY[3:])
     rings = [first_ring + at for at in range(TOGETHER)]
     blocks = [held[ring].reshape(PLANE * REST, 128) for ring in rings]
     blocks = mix_blocks(blocks, left, right, across)
@@ -468,7 +468,7 @@
 ROWS = pltpu.VMEM((PLANE, RING, 128), F32)
 CLASS_ROWS = pltpu.VMEM((RING, RING, 8, 128), F32)
 MANY = pltpu.SemaphoreType.DMA((RING, RING))
-LEFT = pltpu.VMEM((256, 768), BF16)
+LEFT = pltpu.VMEM((128, 384), BF16)
 RIGHT = pltpu.VMEM((256, 256), BF16)
 EIGHT = pltpu.SemaphoreType.DMA((RING,))
 ONE = pltpu.SemaphoreType.DMA
@@ -497,7 +497,7 @@
     )(rate_index, *operands)
 
 
-LATER = {"az1": (4, 6, 2, 7, 1), "bz1": (4, 6, 2, 7, 1), "az2": (4, 6, 2, 7, 1), "bz2": (6, 2, 7, 1)}
+LATER = {"az1": (2, 6, 4, 7, 1), "bz1": (2, 6, 4, 7, 1), "az2": (2, 6, 4, 7, 1), "bz2": (2, 6, 7, 1)}
 
 
 def sooner(name):

time: 306 us -> 304 us (level)
  transfers between devices with their start and end apart: 32 -> 32, of which waited for: 21 -> 21; matrix products, arithmetic and copies ran while one was open for 0% -> 0% of each run, Pallas kernels for 9% -> 8%
where the time goes in v5:
time: 304 us; the launch traced here: 303 us
  waiting for transfers between devices  160 us (53%)
  starting transfers between devices  93.3 us (31%)
  Pallas kernels  40.7 us (13%)
  local copies, waits for them, and re-layouts  9.1 us (3%)
    ppermute x28, waiting for transfers between devices, round_ring(): moved[shift] = lax.ppermute(parts[shift], AXES, ring_pairs(shift))  159 us
    ppermute x28, starting transfers between devices, round_ring(): moved[shift] = lax.ppermute(parts[shift], AXES, ring_pairs(shift))  60.1 us
    pallas_call x10, Pallas kernels, call(): pl.pallas_call(kernel, out_shape=[far(out) for out in outs] if many else...  40.7 us
    all_to_all x4, starting transfers between devices, in_plane(): lax.all_to_all(piece, AXES, split_axis=0, concat_axis=0, tiled=True, axis...  33.2 us
    unnamed x22, local copies, waits for them, and re-layouts  9.1 us
  transfers between devices with their start and end apart: 32, of which 21 were waited for; matrix products, arithmetic and copies ran while one was open for 0% of the time, Pallas kernels for 8%

profile of v5, /device:TPU:1, one launch (start us, length us, event | category | flops | bytes accessed | tf_op | source)
XLA Modules:
  0.0 303.1 jit_solution(17824605328781979273)
XLA Ops:
  0.0 5.2 %shard_map.42 = f32[32,128,128]{2,1,0:T(8,128)} custom-call(s32[2]{0:T(128)} %rate_ref.19, s32[128,128]{1,0:T(8,128)} %bitcast.13, f32[8,1024,128]{2,1,0:T(8,128)} %bitcast.11), custom_call_target="tpu_custom_call" | custom-call | flops 268435456 | bytes 8388608 | tf_op jit(solution)/shard_map/pallas_call | solution.py:487
  5.2 8.6 %all-to-all-start.2 = ((f32[32,128,128]{2,1,0:T(8,128)}), f32[32,128,128]{2,1,0:T(8,128)S(1)}, u32[]{:S(2)}, u32[]{:S(2)}) async-start(f32[32,128,128]{2,1,0:T(8,128)} %shard_map.42), calls=%async_computation.2 | async-start | bytes 4194304 | tf_op jit(solution)/shard_map/all_to_all | solution.py:516
  13.8 5.6 %shard_map.37 = (f32[33,16,128]{2,1,0:T(8,128)}, f32[33,16,128]{2,1,0:T(8,128)}, f32[33,16,128]{2,1,0:T(8,128)}, f32[33,16,128]{2,1,0:T(8,128)}, f32[33,16,128]{...) custom-call(s32[2]{0:T(128)} %rate_ref.19, s32[128,128]{1,0:T(8,128)} %bitcast.14, ...), custom_call_target="tpu_custom_call" | custom-call | flops 268435456 | bytes 8388608 | tf_op jit(solution)/shard_map/pallas_call | solution.py:487
  21.1 3.0 collective-permute-start.1
  24.1 3.8 %collective-permute-start.2 = (f32[33,16,128]{2,1,0:T(8,128)}, f32[33,16,128]{2,1,0:T(8,128)S(1)}, u32[]{:S(2)}, u32[]{:S(2)}) collective-permute-start(f32[33,16,128]{2,1,0:T(8,128)} %get-tuple-element.40), channel_id=1, source_target_pairs={{0,192},{1,193},{2,194},{3,195},{8,200},{9,201},{10,202},{11,203},... | collective-permute-start | bytes 811016 | tf_op jit(solution)/shard_map/ppermute | solution.py:511
  28.3 4.5 %collective-permute-start.4 = (f32[33,16,128]{2,1,0:T(8,128)}, f32[33,16,128]{2,1,0:T(8,128)S(1)}, u32[]{:S(2)}, u32[]{:S(2)}) collective-permute-start(f32[33,16,128]{2,1,0:T(8,128)} %get-tuple-element.42), channel_id=1, source_target_pairs={{0,68},{1,69},{2,70},{3,71},{8,76},{9,77},{10,78},{11,79},{16,84},... | collective-permute-start | bytes 811016 | tf_op jit(solution)/shard_map/ppermute | solution.py:511
  32.8 2.4 collective-permute-start.5
  35.2 4.0 %collective-permute-done.1.refs_2_ = f32[33,16,128]{2,1,0:T(8,128)S(1)} collective-permute-done((f32[33,16,128]{2,1,0:T(8,128)}, f32[33,16,128]{2,1,0:T(8,128)S(1)}, u32[]{:S(2)}, u32[]{:S(2)}) %collective-permute-start.1) | collective-permute-done | bytes 270368 | tf_op jit(solution)/shard_map/ppermute | solution.py:511
  39.2 6.9 %collective-permute-start.6 = (f32[33,16,128]{2,1,0:T(8,128)}, f32[33,16,128]{2,1,0:T(8,128)S(1)}, u32[]{:S(2)}, u32[]{:S(2)}) collective-permute-start(f32[33,16,128]{2,1,0:T(8,128)} %get-tuple-element.44), channel_id=1, source_target_pairs={{0,196},{1,197},{2,198},{3,199},{8,204},{9,205},{10,206},{11,207},... | collective-permute-start | bytes 811016 | tf_op jit(solution)/shard_map/ppermute | solution.py:511
  46.1 15.1 %collective-permute-done.2.refs_3_ = f32[33,16,128]{2,1,0:T(8,128)S(1)} collective-permute-done((f32[33,16,128]{2,1,0:T(8,128)}, f32[33,16,128]{2,1,0:T(8,128)S(1)}, u32[]{:S(2)}, u32[]{:S(2)}) %collective-permute-start.2) | collective-permute-done | bytes 270368 | tf_op jit(solution)/shard_map/ppermute | solution.py:511
  61.2 5.1 %collective-permute-done.3.refs_4_ = f32[33,16,128]{2,1,0:T(8,128)S(1)} collective-permute-done((f32[33,16,128]{2,1,0:T(8,128)}, f32[33,16,128]{2,1,0:T(8,128)S(1)}, u32[]{:S(2)}, u32[]{:S(2)}) %collective-permute-start.3) | collective-permute-done | bytes 270368 | tf_op jit(solution)/shard_map/ppermute | solution.py:511
  66.4 7.8 %collective-permute-done.5.refs_6_ = f32[33,16,128]{2,1,0:T(8,128)S(1)} collective-permute-done((f32[33,16,128]{2,1,0:T(8,128)}, f32[33,16,128]{2,1,0:T(8,128)S(1)}, u32[]{:S(2)}, u32[]{:S(2)}) %collective-permute-start.5) | collective-permute-done | bytes 270368 | tf_op jit(solution)/shard_map/ppermute | solution.py:511
  74.2 2.4 collective-permute-done.6.refs_7_
  77.6 3.0 shard_map.38
  81.9 8.5 %all-to-all-start = ((f32[32,136,128]{2,1,0:T(8,128)}), f32[32,136,128]{2,1,0:T(8,128)S(1)}, u32[]{:S(2)}, u32[]{:S(2)}) async-start(f32[32,136,128]{2,1,0:T(8,128)} %shard_map.38), calls=%async_computation | async-start | bytes 4456448 | tf_op jit(solution)/shard_map/all_to_all | solution.py:516
  92.0 2.8 shard_map.43
  94.8 3.4 %collective-permute-start.14 = (f32[32,16,128]{2,1,0:T(8,128)}, f32[32,16,128]{2,1,0:T(8,128)S(1)}, u32[]{:S(2)}, u32[]{:S(2)}) collective-permute-start(f32[32,16,128]{2,1,0:T(8,128)} %get-tuple-element.54), channel_id=1, source_target_pairs={{0,64},{1,65},{2,66},{3,67},{8,72},{9,73},{10,74},{11,75},{16,80},... | collective-permute-start | bytes 786440 | tf_op jit(solution)/shard_map/ppermute | solution.py:511
  99.3 4.5 %collective-permute-start.17 = (f32[32,16,128]{2,1,0:T(8,128)}, f32[32,16,128]{2,1,0:T(8,128)S(1)}, u32[]{:S(2)}, u32[]{:S(2)}) collective-permute-start(f32[32,16,128]{2,1,0:T(8,128)} %get-tuple-element.57), channel_id=1, source_target_pairs={{0,4},{1,5},{2,6},{3,7},{8,12},{9,13},{10,14},{11,15},{16,20},{17,... | collective-permute-start | bytes 786440 | tf_op jit(solution)/shard_map/ppermute | solution.py:511
  105.0 2.1 collective-permute-start.19
  107.1 9.7 %collective-permute-done.15.refs_2_ = f32[32,16,128]{2,1,0:T(8,128)S(1)} collective-permute-done((f32[32,16,128]{2,1,0:T(8,128)}, f32[32,16,128]{2,1,0:T(8,128)S(1)}, u32[]{:S(2)}, u32[]{:S(2)}) %collective-permute-start.15) | collective-permute-done | bytes 262176 | tf_op jit(solution)/shard_map/ppermute | solution.py:511
  116.8 9.9 %collective-permute-done.16.refs_3_ = f32[32,16,128]{2,1,0:T(8,128)S(1)} collective-permute-done((f32[32,16,128]{2,1,0:T(8,128)}, f32[32,16,128]{2,1,0:T(8,128)S(1)}, u32[]{:S(2)}, u32[]{:S(2)}) %collective-permute-start.16) | collective-permute-done | bytes 262176 | tf_op jit(solution)/shard_map/ppermute | solution.py:511
  126.7 13.9 %collective-permute-done.17.refs_4_ = f32[32,16,128]{2,1,0:T(8,128)S(1)} collective-permute-done((f32[32,16,128]{2,1,0:T(8,128)}, f32[32,16,128]{2,1,0:T(8,128)S(1)}, u32[]{:S(2)}, u32[]{:S(2)}) %collective-permute-start.17) | collective-permute-done | bytes 262176 | tf_op jit(solution)/shard_map/ppermute | solution.py:511
  140.7 4.7 %collective-permute-done.19.refs_6_ = f32[32,16,128]{2,1,0:T(8,128)S(1)} collective-permute-done((f32[32,16,128]{2,1,0:T(8,128)}, f32[32,16,128]{2,1,0:T(8,128)S(1)}, u32[]{:S(2)}, u32[]{:S(2)}) %collective-permute-start.19) | collective-permute-done | bytes 262176 | tf_op jit(solution)/shard_map/ppermute | solution.py:511
  146.0 4.8 %collective-permute-done.20.refs_7_ = f32[32,16,128]{2,1,0:T(8,128)S(1)} collective-permute-done((f32[32,16,128]{2,1,0:T(8,128)}, f32[32,16,128]{2,1,0:T(8,128)S(1)}, u32[]{:S(2)}, u32[]{:S(2)}) %collective-permute-start.20) | collective-permute-done | bytes 262176 | tf_op jit(solution)/shard_map/ppermute | solution.py:511
  154.4 6.0 %shard_map.44 = f32[32,128,128]{2,1,0:T(8,128)} custom-call(s32[2]{0:T(128)S(1)} %copy-done.10, f32[32,136,128]{2,1,0:T(8,128)S(1)} %all-to-all-done.x_ref.fitness_ref, f32[32,16,128]{2,1,0:T(8,128)S(1)} %copy-done.4, f32[32,16,128]{2,1,0:T(8,128)S(1)} %collective-permute-done.14.refs_1_, f32[32,16,128]{2,1,0:T(8,128)S(1)} %collective-permute-done.15.refs_2_, ...), custom_call_target="tpu_custom_call" | custom-call | flops 268435456 | bytes 8388608 | tf_op jit(solution)/shard_map/pallas_call | solution.py:487
  160.5 7.7 %all-to-all-start.3 = ((f32[32,128,128]{2,1,0:T(8,128)}), f32[32,128,128]{2,1,0:T(8,128)}, u32[]{:S(2)}, u32[]{:S(2)}) async-start(f32[32,128,128]{2,1,0:T(8,128)} %shard_map.44), calls=%async_computation.3 | async-start | bytes 4194304 | tf_op jit(solution)/shard_map/all_to_all | solution.py:516
  168.2 5.5 %shard_map.39 = (f32[32,16,128]{2,1,0:T(8,128)}, f32[32,16,128]{2,1,0:T(8,128)}, f32[32,16,128]{2,1,0:T(8,128)}, f32[32,16,128]{2,1,0:T(8,128)}, f32[32,16,128]{...) custom-call(s32[2]{0:T(128)S(1)} %copy-done.10, ...), custom_call_target="tpu_custom_call" | custom-call | flops 268435456 | bytes 8388608 | tf_op jit(solution)/shard_map/pallas_call | solution.py:487
  175.5 3.3 %collective-permute-start.9 = (f32[32,16,128]{2,1,0:T(8,128)}, f32[32,16,128]{2,1,0:T(8,128)S(1)}, u32[]{:S(2)}, u32[]{:S(2)}) collective-permute-start(f32[32,16,128]{2,1,0:T(8,128)} %get-tuple-element.48), channel_id=1, source_target_pairs={{0,192},{1,193},{2,194},{3,195},{8,200},{9,201},{10,202},{11,203},... | collective-permute-start | bytes 786440 | tf_op jit(solution)/shard_map/ppermute | solution.py:511
  179.7 4.1 %collective-permute-start.11 = (f32[32,16,128]{2,1,0:T(8,128)}, f32[32,16,128]{2,1,0:T(8,128)S(1)}, u32[]{:S(2)}, u32[]{:S(2)}) collective-permute-start(f32[32,16,128]{2,1,0:T(8,128)} %get-tuple-element.50), channel_id=1, source_target_pairs={{0,68},{1,69},{2,70},{3,71},{8,76},{9,77},{10,78},{11,79},{16,84},... | collective-permute-start | bytes 786440 | tf_op jit(solution)/shard_map/ppermute | solution.py:511
  183.8 2.7 collective-permute-start.12
  186.5 9.1 %collective-permute-done.8.refs_2_ = f32[32,16,128]{2,1,0:T(8,128)S(1)} collective-permute-done((f32[32,16,128]{2,1,0:T(8,128)}, f32[32,16,128]{2,1,0:T(8,128)S(1)}, u32[]{:S(2)}, u32[]{:S(2)}) %collective-permute-start.8) | collective-permute-done | bytes 262176 | tf_op jit(solution)/shard_map/ppermute | solution.py:511
  195.6 14.9 %collective-permute-done.9.refs_3_ = f32[32,16,128]{2,1,0:T(8,128)S(1)} collective-permute-done((f32[32,16,128]{2,1,0:T(8,128)}, f32[32,16,128]{2,1,0:T(8,128)S(1)}, u32[]{:S(2)}, u32[]{:S(2)}) %collective-permute-start.9) | collective-permute-done | bytes 262176 | tf_op jit(solution)/shard_map/ppermute | solution.py:511
  210.5 10.1 %collective-permute-done.10.refs_4_ = f32[32,16,128]{2,1,0:T(8,128)S(1)} collective-permute-done((f32[32,16,128]{2,1,0:T(8,128)}, f32[32,16,128]{2,1,0:T(8,128)S(1)}, u32[]{:S(2)}, u32[]{:S(2)}) %collective-permute-start.10) | collective-permute-done | bytes 262176 | tf_op jit(solution)/shard_map/ppermute | solution.py:511
  220.6 3.7 %collective-permute-done.12.refs_6_ = f32[32,16,128]{2,1,0:T(8,128)S(1)} collective-permute-done((f32[32,16,128]{2,1,0:T(8,128)}, f32[32,16,128]{2,1,0:T(8,128)S(1)}, u32[]{:S(2)}, u32[]{:S(2)}) %collective-permute-start.12) | collective-permute-done | bytes 262176 | tf_op jit(solution)/shard_map/ppermute | solution.py:511
  224.3 2.3 collective-permute-done.13.refs_7_
  227.6 2.8 shard_map.40
  230.3 8.5 %all-to-all-start.1 = ((f32[32,128,128]{2,1,0:T(8,128)}), f32[32,128,128]{2,1,0:T(8,128)S(1)}, u32[]{:S(2)}, u32[]{:S(2)}) async-start(f32[32,128,128]{2,1,0:T(8,128)} %shard_map.40), calls=%async_computation.1 | async-start | bytes 4194304 | tf_op jit(solution)/shard_map/all_to_all | solution.py:516
  238.8 4.0 %shard_map.45 = (f32[32,16,128]{2,1,0:T(8,128)}, f32[32,16,128]{2,1,0:T(8,128)}, f32[32,16,128]{2,1,0:T(8,128)}, f32[32,16,128]{2,1,0:T(8,128)}, f32[32,16,128]{...) custom-call(s32[2]{0:T(128)S(1)} %copy-done.10, ...), custom_call_target="tpu_custom_call" | custom-call | flops 268435456 | bytes 8388608 | tf_op jit(solution)/shard_map/pallas_call | solution.py:487
  242.8 3.3 %collective-permute-start.21 = (f32[32,16,128]{2,1,0:T(8,128)}, f32[32,16,128]{2,1,0:T(8,128)S(1)}, u32[]{:S(2)}, u32[]{:S(2)}) collective-permute-start(f32[32,16,128]{2,1,0:T(8,128)} %get-tuple-element.62), channel_id=1, source_target_pairs={{0,64},{1,65},{2,66},{3,67},{8,72},{9,73},{10,74},{11,75},{16,80},... | collective-permute-start | bytes 786440 | tf_op jit(solution)/shard_map/ppermute | solution.py:511
  247.2 4.7 %collective-permute-start.24 = (f32[32,16,128]{2,1,0:T(8,128)}, f32[32,16,128]{2,1,0:T(8,128)S(1)}, u32[]{:S(2)}, u32[]{:S(2)}) collective-permute-start(f32[32,16,128]{2,1,0:T(8,128)} %get-tuple-element.65), channel_id=1, source_target_pairs={{0,4},{1,5},{2,6},{3,7},{8,12},{9,13},{10,14},{11,15},{16,20},{17,... | collective-permute-start | bytes 786440 | tf_op jit(solution)/shard_map/ppermute | solution.py:511
  252.9 2.2 collective-permute-start.26
  255.1 9.8 %collective-permute-done.22.refs_2_ = f32[32,16,128]{2,1,0:T(8,128)S(1)} collective-permute-done((f32[32,16,128]{2,1,0:T(8,128)}, f32[32,16,128]{2,1,0:T(8,128)S(1)}, u32[]{:S(2)}, u32[]{:S(2)}) %collective-permute-start.22) | collective-permute-done | bytes 262176 | tf_op jit(solution)/shard_map/ppermute | solution.py:511
  265.9 1.8 shard_map.41.other_ref
  267.7 6.7 %collective-permute-done.23.refs_3_ = f32[32,16,128]{2,1,0:T(8,128)S(1)} collective-permute-done((f32[32,16,128]{2,1,0:T(8,128)}, f32[32,16,128]{2,1,0:T(8,128)S(1)}, u32[]{:S(2)}, u32[]{:S(2)}) %collective-permute-start.23) | collective-permute-done | bytes 262176 | tf_op jit(solution)/shard_map/ppermute | solution.py:511
  274.4 14.1 %collective-permute-done.24.refs_4_ = f32[32,16,128]{2,1,0:T(8,128)S(1)} collective-permute-done((f32[32,16,128]{2,1,0:T(8,128)}, f32[32,16,128]{2,1,0:T(8,128)S(1)}, u32[]{:S(2)}, u32[]{:S(2)}) %collective-permute-start.24) | collective-permute-done | bytes 262176 | tf_op jit(solution)/shard_map/ppermute | solution.py:511
  288.5 5.0 %collective-permute-done.26.refs_6_ = f32[32,16,128]{2,1,0:T(8,128)} collective-permute-done((f32[32,16,128]{2,1,0:T(8,128)}, f32[32,16,128]{2,1,0:T(8,128)}, u32[]{:S(2)}, u32[]{:S(2)}) %collective-permute-start.26) | collective-permute-done | bytes 262176 | tf_op jit(solution)/shard_map/ppermute | solution.py:511
  293.4 5.4 %collective-permute-done.27.refs_7_ = f32[32,16,128]{2,1,0:T(8,128)} collective-permute-done((f32[32,16,128]{2,1,0:T(8,128)}, f32[32,16,128]{2,1,0:T(8,128)}, u32[]{:S(2)}, u32[]{:S(2)}) %collective-permute-start.27) | collective-permute-done | bytes 262176 | tf_op jit(solution)/shard_map/ppermute | solution.py:511
  298.9 4.1 %shard_map.46 = f32[8,1024,128]{2,1,0:T(8,128)} custom-call(s32[2]{0:T(128)S(1)} %copy-done.10, f32[8,32,16,128]{3,2,1,0:T(8,128)S(1)} %shard_map.41.other_ref, f32[32,16,128]{2,1,0:T(8,128)S(1)} %copy-done.3, f32[32,16,128]{2,1,0:T(8,128)S(1)} %collective-permute-done.21.refs_1_, f32[32,16,128]{2,1,0:T(8,128)S(1)} %collective-permute-done.22.refs_2_, ...), custom_call_target="tpu_custom_call" | custom-call | flops 268435456 | bytes 8388608 | tf_op jit(solution)/shard_map/pallas_call | solution.py:487
  (48 shorter events, 19.4 us)
Async XLA Ops:
  5.2 75.4 %all-to-all-start.2 = ((f32[32,128,128]{2,1,0:T(8,128)}), f32[32,128,128]{2,1,0:T(8,128)S(1)}, u32[]{:S(2)}, u32[]{:S(2)}) async-start(f32[32,128,128]{2,1,0:T(8,128)} %shard_map.42), calls=%async_computation.2 | async-start | bytes 4194304 | tf_op jit(solution)/shard_map/all_to_all | solution.py:516
  13.8 62.8 %copy-start.10 = (s32[2]{0:T(128)S(1)}, s32[2]{0:T(128)}, u32[]{:S(2)}) copy-start(s32[2]{0:T(128)} %rate_ref.19) | copy-start | bytes 28
  19.4 13.4 %collective-permute-start = (f32[33,16,128]{2,1,0:T(8,128)}, f32[33,16,128]{2,1,0:T(8,128)S(1)}, u32[]{:S(2)}, u32[]{:S(2)}) collective-permute-start(f32[33,16,128]{2,1,0:T(8,128)} %get-tuple-element.38), channel_id=1, source_target_pairs={{0,64},{1,65},{2,66},{3,67},{8,72},{9,73},{10,74},{11,75},{16,80},... | collective-permute-start | bytes 811016 | tf_op jit(solution)/shard_map/ppermute | solution.py:511
  21.1 18.1 %collective-permute-start.1 = (f32[33,16,128]{2,1,0:T(8,128)}, f32[33,16,128]{2,1,0:T(8,128)S(1)}, u32[]{:S(2)}, u32[]{:S(2)}) collective-permute-start(f32[33,16,128]{2,1,0:T(8,128)} %get-tuple-element.39), channel_id=1, source_target_pairs={{0,128},{1,129},{2,130},{3,131},{8,136},{9,137},{10,138},{11,139},... | collective-permute-start | bytes 811016 | tf_op jit(solution)/shard_map/ppermute | solution.py:511
  24.1 37.1 %collective-permute-start.2 = (f32[33,16,128]{2,1,0:T(8,128)}, f32[33,16,128]{2,1,0:T(8,128)S(1)}, u32[]{:S(2)}, u32[]{:S(2)}) collective-permute-start(f32[33,16,128]{2,1,0:T(8,128)} %get-tuple-element.40), channel_id=1, source_target_pairs={{0,192},{1,193},{2,194},{3,195},{8,200},{9,201},{10,202},{11,203},... | collective-permute-start | bytes 811016 | tf_op jit(solution)/shard_map/ppermute | solution.py:511
  27.9 38.5 %collective-permute-start.3 = (f32[33,16,128]{2,1,0:T(8,128)}, f32[33,16,128]{2,1,0:T(8,128)S(1)}, u32[]{:S(2)}, u32[]{:S(2)}) collective-permute-start(f32[33,16,128]{2,1,0:T(8,128)} %get-tuple-element.41), channel_id=1, source_target_pairs={{0,4},{1,5},{2,6},{3,7},{8,12},{9,13},{10,14},{11,15},{16,20},{17,... | collective-permute-start | bytes 811016 | tf_op jit(solution)/shard_map/ppermute | solution.py:511
  28.3 38.0 %collective-permute-start.4 = (f32[33,16,128]{2,1,0:T(8,128)}, f32[33,16,128]{2,1,0:T(8,128)S(1)}, u32[]{:S(2)}, u32[]{:S(2)}) collective-permute-start(f32[33,16,128]{2,1,0:T(8,128)} %get-tuple-element.42), channel_id=1, source_target_pairs={{0,68},{1,69},{2,70},{3,71},{8,76},{9,77},{10,78},{11,79},{16,84},... | collective-permute-start | bytes 811016 | tf_op jit(solution)/shard_map/ppermute | solution.py:511
  32.8 41.4 %collective-permute-start.5 = (f32[33,16,128]{2,1,0:T(8,128)}, f32[33,16,128]{2,1,0:T(8,128)S(1)}, u32[]{:S(2)}, u32[]{:S(2)}) collective-permute-start(f32[33,16,128]{2,1,0:T(8,128)} %get-tuple-element.43), channel_id=1, source_target_pairs={{0,132},{1,133},{2,134},{3,135},{8,140},{9,141},{10,142},{11,143},... | collective-permute-start | bytes 811016 | tf_op jit(solution)/shard_map/ppermute | solution.py:511
  39.2 37.4 %collective-permute-start.6 = (f32[33,16,128]{2,1,0:T(8,128)}, f32[33,16,128]{2,1,0:T(8,128)S(1)}, u32[]{:S(2)}, u32[]{:S(2)}) collective-permute-start(f32[33,16,128]{2,1,0:T(8,128)} %get-tuple-element.44), channel_id=1, source_target_pairs={{0,196},{1,197},{2,198},{3,199},{8,204},{9,205},{10,206},{11,207},... | collective-permute-start | bytes 811016 | tf_op jit(solution)/shard_map/ppermute | solution.py:511
  76.6 1.0 copy-start.2
  80.6 1.3 copy-start
  81.9 69.7 %all-to-all-start = ((f32[32,136,128]{2,1,0:T(8,128)}), f32[32,136,128]{2,1,0:T(8,128)S(1)}, u32[]{:S(2)}, u32[]{:S(2)}) async-start(f32[32,136,128]{2,1,0:T(8,128)} %shard_map.38), calls=%async_computation | async-start | bytes 4456448 | tf_op jit(solution)/shard_map/all_to_all | solution.py:516
  90.4 1.6 copy-start.1
  94.8 10.2 %collective-permute-start.14 = (f32[32,16,128]{2,1,0:T(8,128)}, f32[32,16,128]{2,1,0:T(8,128)S(1)}, u32[]{:S(2)}, u32[]{:S(2)}) collective-permute-start(f32[32,16,128]{2,1,0:T(8,128)} %get-tuple-element.54), channel_id=1, source_target_pairs={{0,64},{1,65},{2,66},{3,67},{8,72},{9,73},{10,74},{11,75},{16,80},... | collective-permute-start | bytes 786440 | tf_op jit(solution)/shard_map/ppermute | solution.py:511
  98.2 18.6 %collective-permute-start.15 = (f32[32,16,128]{2,1,0:T(8,128)}, f32[32,16,128]{2,1,0:T(8,128)S(1)}, u32[]{:S(2)}, u32[]{:S(2)}) collective-permute-start(f32[32,16,128]{2,1,0:T(8,128)} %get-tuple-element.55), channel_id=1, source_target_pairs={{0,128},{1,129},{2,130},{3,131},{8,136},{9,137},{10,138},{11,139},... | collective-permute-start | bytes 786440 | tf_op jit(solution)/shard_map/ppermute | solution.py:511
  99.0 27.7 %collective-permute-start.16 = (f32[32,16,128]{2,1,0:T(8,128)}, f32[32,16,128]{2,1,0:T(8,128)S(1)}, u32[]{:S(2)}, u32[]{:S(2)}) collective-permute-start(f32[32,16,128]{2,1,0:T(8,128)} %get-tuple-element.56), channel_id=1, source_target_pairs={{0,192},{1,193},{2,194},{3,195},{8,200},{9,201},{10,202},{11,203},... | collective-permute-start | bytes 786440 | tf_op jit(solution)/shard_map/ppermute | solution.py:511
  99.3 41.3 %collective-permute-start.17 = (f32[32,16,128]{2,1,0:T(8,128)}, f32[32,16,128]{2,1,0:T(8,128)S(1)}, u32[]{:S(2)}, u32[]{:S(2)}) collective-permute-start(f32[32,16,128]{2,1,0:T(8,128)} %get-tuple-element.57), channel_id=1, source_target_pairs={{0,4},{1,5},{2,6},{3,7},{8,12},{9,13},{10,14},{11,15},{16,20},{17,... | collective-permute-start | bytes 786440 | tf_op jit(solution)/shard_map/ppermute | solution.py:511
  103.8 36.8 %collective-permute-start.18 = (f32[32,16,128]{2,1,0:T(8,128)}, f32[32,16,128]{2,1,0:T(8,128)S(1)}, u32[]{:S(2)}, u32[]{:S(2)}) collective-permute-start(f32[32,16,128]{2,1,0:T(8,128)} %get-tuple-element.58), channel_id=1, source_target_pairs={{0,68},{1,69},{2,70},{3,71},{8,76},{9,77},{10,78},{11,79},{16,84},... | collective-permute-start | bytes 786440 | tf_op jit(solution)/shard_map/ppermute | solution.py:511
  105.0 40.4 %collective-permute-start.19 = (f32[32,16,128]{2,1,0:T(8,128)}, f32[32,16,128]{2,1,0:T(8,128)S(1)}, u32[]{:S(2)}, u32[]{:S(2)}) collective-permute-start(f32[32,16,128]{2,1,0:T(8,128)} %get-tuple-element.59), channel_id=1, source_target_pairs={{0,132},{1,133},{2,134},{3,135},{8,140},{9,141},{10,142},{11,143},... | collective-permute-start | bytes 786440 | tf_op jit(solution)/shard_map/ppermute | solution.py:511
  116.8 34.1 %collective-permute-start.20 = (f32[32,16,128]{2,1,0:T(8,128)}, f32[32,16,128]{2,1,0:T(8,128)S(1)}, u32[]{:S(2)}, u32[]{:S(2)}) collective-permute-start(f32[32,16,128]{2,1,0:T(8,128)} %get-tuple-element.60), channel_id=1, source_target_pairs={{0,196},{1,197},{2,198},{3,199},{8,204},{9,205},{10,206},{11,207},... | collective-permute-start | bytes 786440 | tf_op jit(solution)/shard_map/ppermute | solution.py:511
  145.3 0.7 copy-start.6
  150.9 0.7 copy-start.8
  151.6 1.0 copy-start.4
  152.5 0.9 copy-start.7
  153.5 0.9 copy-start.9
  160.5 69.9 %all-to-all-start.3 = ((f32[32,128,128]{2,1,0:T(8,128)}), f32[32,128,128]{2,1,0:T(8,128)}, u32[]{:S(2)}, u32[]{:S(2)}) async-start(f32[32,128,128]{2,1,0:T(8,128)} %shard_map.44), calls=%async_computation.3 | async-start | bytes 4194304 | tf_op jit(solution)/shard_map/all_to_all | solution.py:516
  173.6 10.2 %collective-permute-start.7 = (f32[32,16,128]{2,1,0:T(8,128)}, f32[32,16,128]{2,1,0:T(8,128)S(1)}, u32[]{:S(2)}, u32[]{:S(2)}) collective-permute-start(f32[32,16,128]{2,1,0:T(8,128)} %get-tuple-element.46), channel_id=1, source_target_pairs={{0,64},{1,65},{2,66},{3,67},{8,72},{9,73},{10,74},{11,75},{16,80},... | collective-permute-start | bytes 786440 | tf_op jit(solution)/shard_map/ppermute | solution.py:511
  174.0 21.6 %collective-permute-start.8 = (f32[32,16,128]{2,1,0:T(8,128)}, f32[32,16,128]{2,1,0:T(8,128)S(1)}, u32[]{:S(2)}, u32[]{:S(2)}) collective-permute-start(f32[32,16,128]{2,1,0:T(8,128)} %get-tuple-element.47), channel_id=1, source_target_pairs={{0,128},{1,129},{2,130},{3,131},{8,136},{9,137},{10,138},{11,139},... | collective-permute-start | bytes 786440 | tf_op jit(solution)/shard_map/ppermute | solution.py:511
  175.5 35.0 %collective-permute-start.9 = (f32[32,16,128]{2,1,0:T(8,128)}, f32[32,16,128]{2,1,0:T(8,128)S(1)}, u32[]{:S(2)}, u32[]{:S(2)}) collective-permute-start(f32[32,16,128]{2,1,0:T(8,128)} %get-tuple-element.48), channel_id=1, source_target_pairs={{0,192},{1,193},{2,194},{3,195},{8,200},{9,201},{10,202},{11,203},... | collective-permute-start | bytes 786440 | tf_op jit(solution)/shard_map/ppermute | solution.py:511
  178.8 41.7 %collective-permute-start.10 = (f32[32,16,128]{2,1,0:T(8,128)}, f32[32,16,128]{2,1,0:T(8,128)S(1)}, u32[]{:S(2)}, u32[]{:S(2)}) collective-permute-start(f32[32,16,128]{2,1,0:T(8,128)} %get-tuple-element.49), channel_id=1, source_target_pairs={{0,4},{1,5},{2,6},{3,7},{8,12},{9,13},{10,14},{11,15},{16,20},{17,... | collective-permute-start | bytes 786440 | tf_op jit(solution)/shard_map/ppermute | solution.py:511
  179.7 40.9 %collective-permute-start.11 = (f32[32,16,128]{2,1,0:T(8,128)}, f32[32,16,128]{2,1,0:T(8,128)S(1)}, u32[]{:S(2)}, u32[]{:S(2)}) collective-permute-start(f32[32,16,128]{2,1,0:T(8,128)} %get-tuple-element.50), channel_id=1, source_target_pairs={{0,68},{1,69},{2,70},{3,71},{8,76},{9,77},{10,78},{11,79},{16,84},... | collective-permute-start | bytes 786440 | tf_op jit(solution)/shard_map/ppermute | solution.py:511
  183.8 40.5 %collective-permute-start.12 = (f32[32,16,128]{2,1,0:T(8,128)}, f32[32,16,128]{2,1,0:T(8,128)S(1)}, u32[]{:S(2)}, u32[]{:S(2)}) collective-permute-start(f32[32,16,128]{2,1,0:T(8,128)} %get-tuple-element.51), channel_id=1, source_target_pairs={{0,132},{1,133},{2,134},{3,135},{8,140},{9,141},{10,142},{11,143},... | collective-permute-start | bytes 786440 | tf_op jit(solution)/shard_map/ppermute | solution.py:511
  195.6 31.0 %collective-permute-start.13 = (f32[32,16,128]{2,1,0:T(8,128)}, f32[32,16,128]{2,1,0:T(8,128)S(1)}, u32[]{:S(2)}, u32[]{:S(2)}) collective-permute-start(f32[32,16,128]{2,1,0:T(8,128)} %get-tuple-element.52), channel_id=1, source_target_pairs={{0,196},{1,197},{2,198},{3,199},{8,204},{9,205},{10,206},{11,207},... | collective-permute-start | bytes 786440 | tf_op jit(solution)/shard_map/ppermute | solution.py:511
  226.6 0.9 copy-start.5
  230.3 35.5 %all-to-all-start.1 = ((f32[32,128,128]{2,1,0:T(8,128)}), f32[32,128,128]{2,1,0:T(8,128)S(1)}, u32[]{:S(2)}, u32[]{:S(2)}) async-start(f32[32,128,128]{2,1,0:T(8,128)} %shard_map.40), calls=%async_computation.1 | async-start | bytes 4194304 | tf_op jit(solution)/shard_map/all_to_all | solution.py:516
  242.8 10.1 %collective-permute-start.21 = (f32[32,16,128]{2,1,0:T(8,128)}, f32[32,16,128]{2,1,0:T(8,128)S(1)}, u32[]{:S(2)}, u32[]{:S(2)}) collective-permute-start(f32[32,16,128]{2,1,0:T(8,128)} %get-tuple-element.62), channel_id=1, source_target_pairs={{0,64},{1,65},{2,66},{3,67},{8,72},{9,73},{10,74},{11,75},{16,80},... | collective-permute-start | bytes 786440 | tf_op jit(solution)/shard_map/ppermute | solution.py:511
  246.1 18.8 %collective-permute-start.22 = (f32[32,16,128]{2,1,0:T(8,128)}, f32[32,16,128]{2,1,0:T(8,128)S(1)}, u32[]{:S(2)}, u32[]{:S(2)}) collective-permute-start(f32[32,16,128]{2,1,0:T(8,128)} %get-tuple-element.63), channel_id=1, source_target_pairs={{0,128},{1,129},{2,130},{3,131},{8,136},{9,137},{10,138},{11,139},... | collective-permute-start | bytes 786440 | tf_op jit(solution)/shard_map/ppermute | solution.py:511
  247.1 27.3 %collective-permute-start.23 = (f32[32,16,128]{2,1,0:T(8,128)}, f32[32,16,128]{2,1,0:T(8,128)S(1)}, u32[]{:S(2)}, u32[]{:S(2)}) collective-permute-start(f32[32,16,128]{2,1,0:T(8,128)} %get-tuple-element.64), channel_id=1, source_target_pairs={{0,192},{1,193},{2,194},{3,195},{8,200},{9,201},{10,202},{11,203},... | collective-permute-start | bytes 786440 | tf_op jit(solution)/shard_map/ppermute | solution.py:511
  247.2 41.3 %collective-permute-start.24 = (f32[32,16,128]{2,1,0:T(8,128)}, f32[32,16,128]{2,1,0:T(8,128)S(1)}, u32[]{:S(2)}, u32[]{:S(2)}) collective-permute-start(f32[32,16,128]{2,1,0:T(8,128)} %get-tuple-element.65), channel_id=1, source_target_pairs={{0,4},{1,5},{2,6},{3,7},{8,12},{9,13},{10,14},{11,15},{16,20},{17,... | collective-permute-start | bytes 786440 | tf_op jit(solution)/shard_map/ppermute | solution.py:511
  251.8 36.6 %collective-permute-start.25 = (f32[32,16,128]{2,1,0:T(8,128)}, f32[32,16,128]{2,1,0:T(8,128)}, u32[]{:S(2)}, u32[]{:S(2)}) collective-permute-start(f32[32,16,128]{2,1,0:T(8,128)} %get-tuple-element.66), channel_id=1, source_target_pairs={{0,68},{1,69},{2,70},{3,71},{8,76},{9,77},{10,78},{11,79},{16,84},... | collective-permute-start | bytes 786440 | tf_op jit(solution)/shard_map/ppermute | solution.py:511
  252.9 40.6 %collective-permute-start.26 = (f32[32,16,128]{2,1,0:T(8,128)}, f32[32,16,128]{2,1,0:T(8,128)}, u32[]{:S(2)}, u32[]{:S(2)}) collective-permute-start(f32[32,16,128]{2,1,0:T(8,128)} %get-tuple-element.67), channel_id=1, source_target_pairs={{0,132},{1,133},{2,134},{3,135},{8,140},{9,141},{10,142},{11,143},... | collective-permute-start | bytes 786440 | tf_op jit(solution)/shard_map/ppermute | solution.py:511
  264.9 34.0 %copy-start.3 = (f32[32,16,128]{2,1,0:T(8,128)S(1)}, f32[32,16,128]{2,1,0:T(8,128)}, u32[]{:S(2)}) copy-start(f32[32,16,128]{2,1,0:T(8,128)} %get-tuple-element.61.refs_0_) | copy-start | bytes 786436
  264.9 34.0 %collective-permute-start.27 = (f32[32,16,128]{2,1,0:T(8,128)}, f32[32,16,128]{2,1,0:T(8,128)}, u32[]{:S(2)}, u32[]{:S(2)}) collective-permute-start(f32[32,16,128]{2,1,0:T(8,128)} %get-tuple-element.68), channel_id=1, source_target_pairs={{0,196},{1,197},{2,198},{3,199},{8,204},{9,205},{10,206},{11,207},... | collective-permute-start | bytes 786440 | tf_op jit(solution)/shard_map/ppermute | solution.py:511
